TPU v7x, 32 devices: a whole 2x2x4 slice. The times are simulated.
32 devices in a mesh: patch: 8 (over z, y), sample: 4 (over x, core).
Axes of the slice: x: 2, y: 2, z: 4, core: 2. Of those that a mesh axis runs over, the one named last changes fastest.
Arguments:
- features: bfloat16 [4, 4096, 512], P('sample', 'patch'), may hold values from -600 to 600
- cotangent: bfloat16 [4, 4096, 512], P('sample', 'patch'), may hold values from -6 to 6
- weight_qkv: bfloat16 [512, 1536], replicated, may hold values from -5 to 5
- weight_out: bfloat16 [512, 512], replicated, may hold values from -0.25 to 0.25
- key_tiles: int32 [32, 8], replicated, may hold values from 0 to 31, as said below
- tile_valid: int32 [32, 8], replicated, may hold values from 0 to 1, as said below
Outputs:
- grad_features: bfloat16 [4, 4096, 512], P('sample', 'patch')
- grad_qkv: float32 [512, 1536], replicated
- grad_out: float32 [512, 512], replicated
Inputs may be any that keep to these rules, and one draw needn't show every extreme that they name: `key_tiles`: row g names 8 distinct tile ids. A tile's patch is its id // 4. The first id is g itself, the next 3 are other tiles of g's patch, and the last 4 lie one each in the patches at offsets -2 to 2 other than 0 around the cycle of patches, in rising order of offset. Over the rows of one patch exactly 2 distinct tiles of each such neighbouring patch are named. `tile_valid`: column 0 is always 1.
All inputs are finite; a program needn't handle non-finite values.
Results may differ from a plain program's by a relative error of at most 0.0088.
Values may be sent and summed in bfloat16 or wider, within the bound.
No kernel may reach another device: no remote copies, remote signals or barrier semaphores. Data moves between devices by JAX's collectives and lax.ppermute only.
A program may use at most 192 MiB of HBM per device.

v0:
```python
from functools import partial
import math

import jax
import jax.numpy as jnp
from jax import lax
from jax.sharding import PartitionSpec as P

HEADS = 4
TILE = 128
NB = 8
REACH = 2
CAP = 2


epsilon = 1e-06


def from_behind(value, axis, steps):
    count = lax.axis_size(axis)
    pairs = [(source, (source + steps) % count) for source in range(count)]
    return lax.ppermute(value, axis, pairs)


def tile_backward(query_tile, pair_tiles, live_flags, grad_tile, head_count):
    row_count = query_tile.shape[0]
    model_width = query_tile.shape[1]
    head_width = model_width // head_count
    scaling = head_width ** (-0.5)
    key_heads = pair_tiles[:, :, :model_width].reshape(-1, head_count, head_width)
    value_heads = pair_tiles[:, :, model_width:].reshape(-1, head_count, head_width)
    query_heads = query_tile.reshape(row_count, head_count, head_width)
    grad_heads = grad_tile.reshape(row_count, head_count, head_width)
    scores = (
        jnp.einsum("qhd,khd->hqk", query_heads, key_heads, preferred_element_type=jnp.float32)
        * scaling
    )
    live_mask = jnp.repeat(live_flags > 0, pair_tiles.shape[1])
    scores = jnp.where(live_mask[None, None, :], scores, -jnp.inf)
    highest = jnp.max(scores, -1, keepdims=True)
    expanded = jnp.exp(scores - highest)
    attention = expanded / jnp.sum(expanded, -1, keepdims=True)
    attention_low = attention.astype(jnp.bfloat16)
    attended = jnp.einsum(
        "hqk,khd->qhd", attention_low, value_heads, preferred_element_type=jnp.float32
    )
    attended = attended.astype(jnp.bfloat16).reshape(row_count, model_width)
    dprob = jnp.einsum("qhd,khd->hqk", grad_heads, value_heads, preferred_element_type=jnp.float32)
    centre = jnp.sum(attention * dprob, -1, keepdims=True)
    dscore = (attention * (dprob - centre) * scaling).astype(jnp.bfloat16)
    dquery = jnp.einsum(
        "hqk,khd->qhd", dscore, key_heads, preferred_element_type=jnp.float32
    ).reshape(row_count, model_width)
    dkey = jnp.einsum("hqk,qhd->khd", dscore, query_heads, preferred_element_type=jnp.float32)
    dvalue = jnp.einsum(
        "hqk,qhd->khd", attention_low, grad_heads, preferred_element_type=jnp.float32
    )
    dkey = dkey.reshape(pair_tiles.shape[0], pair_tiles.shape[1], model_width)
    dvalue = dvalue.reshape(pair_tiles.shape[0], pair_tiles.shape[1], model_width)
    return (attended, dquery, jnp.concatenate([dkey, dvalue], -1))


def tile_flags(list_rows, source, tile_count):
    first_id = source * tile_count
    wanted = (
        list_rows[:, :, None] == first_id + jnp.arange(tile_count, dtype=jnp.int32)[None, None, :]
    )
    wanted_flags = jnp.any(wanted, axis=(0, 1))
    wanted_places = jnp.cumsum(wanted_flags.astype(jnp.int32)) - 1
    return (wanted_flags, wanted_places)


def on_device(features, cotangent, weight_qkv, weight_out, key_tiles, tile_valid):
    patches = lax.axis_size("patch")
    position = lax.axis_index("patch")
    rows_local = features.shape[1]
    model_width = features.shape[2]
    tile_count = rows_local // TILE
    offsets = [shift_by for shift_by in range(-REACH, REACH + 1) if shift_by != 0]
    inputs = features[0].astype(jnp.float32)
    inverse = lax.rsqrt(jnp.mean(inputs * inputs, -1, keepdims=True) + epsilon)
    normed = inputs * inverse
    normed_low = normed.astype(jnp.bfloat16)
    projected = jnp.dot(normed_low, weight_qkv, preferred_element_type=jnp.float32).astype(
        jnp.bfloat16
    )
    queries = projected[:, :model_width]
    pairs_own = projected[:, model_width:].reshape(tile_count, TILE, 2 * model_width)
    grad_rows = cotangent[0]
    grad_attended = jnp.einsum(
        "pe,de->pd", grad_rows, weight_out, preferred_element_type=jnp.float32
    ).astype(jnp.bfloat16)
    my_lists = lax.dynamic_slice_in_dim(key_tiles, position * tile_count, tile_count, 0)
    my_valid = lax.dynamic_slice_in_dim(tile_valid, position * tile_count, tile_count, 0)
    owner_patch = my_lists // tile_count
    within = my_lists % tile_count
    distance = (owner_patch - position) % patches
    distance = jnp.where(distance > patches // 2, distance - patches, distance)
    order_index = jnp.where(distance < 0, distance + REACH, distance + REACH - 1)
    senders = []
    tile_range = jnp.arange(tile_count, dtype=jnp.int32)
    arrivals = []
    place_rows = []
    for shift_by in offsets:
        target = (position - shift_by) % patches
        target_lists = lax.dynamic_slice_in_dim(key_tiles, target * tile_count, tile_count, 0)
        wanted_flags, wanted_places = tile_flags(target_lists, position, tile_count)
        picker = wanted_flags[None, :] & (
            wanted_places[None, :] == jnp.arange(CAP, dtype=jnp.int32)[:, None]
        )
        send_rows = jnp.sum(jnp.where(picker, tile_range[None, :], 0), 1)
        senders.append(send_rows)
        packed = jnp.take(pairs_own, send_rows, axis=0)
        arrived = from_behind(packed, "patch", -shift_by)
        arrivals.append(arrived)
        source = (position + shift_by) % patches
        incoming_flags, incoming_places = tile_flags(my_lists, source, tile_count)
        place_rows.append(incoming_places)
    buffer = jnp.concatenate([pairs_own] + arrivals, 0)
    place_table = jnp.concatenate(place_rows, 0)
    lookup = order_index * tile_count + within
    matched = lookup[:, :, None] == jnp.arange(place_table.shape[0], dtype=jnp.int32)[None, None, :]
    remote_place = jnp.sum(jnp.where(matched, place_table[None, None, :], 0), -1)
    slot_ids = jnp.where(distance == 0, within, tile_count + order_index * CAP + remote_place)
    group_size = math.gcd(4, tile_count)
    step_count = tile_count // group_size
    tile_pass = jax.vmap(partial(tile_backward, head_count=HEADS))
    buffer_count = buffer.shape[0]

    def advance(running, pieces):
        query_group, slot_group, live_group, grad_group = pieces
        flat_slots = slot_group.reshape(-1)
        gathered = jnp.take(buffer, flat_slots, axis=0).reshape(
            group_size, NB, TILE, 2 * model_width
        )
        attended, dquery, dpairs = tile_pass(query_group, gathered, live_group, grad_group)
        running = running.at[flat_slots].add(dpairs.reshape(group_size * NB, TILE, 2 * model_width))
        return (running, (attended, dquery))

    start_sums = jnp.zeros((buffer_count, TILE, 2 * model_width), jnp.float32)
    scanned = (
        queries.reshape(step_count, group_size, TILE, model_width),
        slot_ids.reshape(step_count, group_size, NB),
        my_valid.reshape(step_count, group_size, NB),
        grad_attended.reshape(step_count, group_size, TILE, model_width),
    )
    totals, (attended_all, dquery_all) = lax.scan(advance, start_sums, scanned)
    grads_own = totals[:tile_count]
    for offset_index, shift_by in enumerate(offsets):
        portion = totals[tile_count + offset_index * CAP : tile_count + (offset_index + 1) * CAP]
        returned = from_behind(portion.astype(jnp.bfloat16), "patch", shift_by).astype(
            portion.dtype
        )
        grads_own = grads_own.at[senders[offset_index]].add(returned)
    attended_rows = attended_all.reshape(rows_local, model_width)
    grad_projected = jnp.concatenate(
        [
            dquery_all.reshape(rows_local, model_width),
            grads_own.reshape(rows_local, 2 * model_width),
        ],
        1,
    ).astype(jnp.bfloat16)
    grad_normed = jnp.einsum(
        "pe,de->pd", grad_projected, weight_qkv, preferred_element_type=jnp.float32
    )
    grad_inputs = grad_rows.astype(jnp.float32) + inverse * (
        grad_normed - normed * jnp.mean(grad_normed * normed, -1, keepdims=True)
    )
    local_qkv = jnp.einsum(
        "pd,pe->de", normed_low, grad_projected, preferred_element_type=jnp.float32
    )
    local_out = jnp.einsum(
        "pd,pe->de", attended_rows, grad_rows, preferred_element_type=jnp.float32
    )
    summed_qkv, summed_out = lax.psum((local_qkv, local_out), ("patch", "sample"))
    factor = float(lax.axis_size("patch") * lax.axis_size("sample") * rows_local) ** (-0.5)
    return (grad_inputs.astype(jnp.bfloat16)[None], summed_qkv * factor, summed_out * factor)


def solution(mesh):
    placed = (P("sample", "patch", None), P("sample", "patch", None), P(), P(), P(), P())
    return jax.shard_map(
        on_device,
        mesh=mesh,
        in_specs=placed,
        out_specs=(P("sample", "patch", None), P(), P()),
        check_vma=False,
    )
```

profile of v0, /device:TPU:0, one launch (start us, length us, event | category | flops | bytes accessed | tf_op | source)
XLA Modules:
  0.0 483.9 jit_solution(8484835399230841525)
XLA Ops:
  14.5 1.9 broadcast_select_fusion.1
  16.4 5.1 %collective-permute-start.3 = (bf16[2,128,1024]{2,1,0:T(8,128)(2,1)}, bf16[2,128,1024]{2,1,0:T(8,128)(2,1)}, u32[]{:S(2)}, u32[]{:S(2)}) collective-permute-start(bf16[2,128,1024]{2,1,0:T(8,128)(2,1)} %broadcast_select_fusion.1), channel_id=1, source_target_pairs={{0,24},{4,28},{8,0},{12,4},{16,8},{20,12},{24,16},{28,20},{1,25},{... | collective-permute-start | bytes 1572872 | tf_op jit(solution)/shard_map/ppermute | solution.py:22
  22.9 2.0 broadcast_select_fusion.2
  28.2 2.0 broadcast_select_fusion.3
  32.2 1.9 broadcast_select_fusion.4
  36.9 2.5 convolution_convert_fusion.1
  41.3 2.0 reshape.469
  43.3 2.1 copy.88
  45.4 2.0 reshape.470
  47.3 2.0 copy.90
  50.4 6.0 %collective-permute-done = bf16[2,128,1024]{2,1,0:T(8,128)(2,1)} collective-permute-done((bf16[2,128,1024]{2,1,0:T(8,128)(2,1)}, bf16[2,128,1024]{2,1,0:T(8,128)(2,1)}, u32[]{:S(2)}, u32[]{:S(2)}) %collective-permute-start) | collective-permute-done | bytes 524320 | tf_op jit(solution)/shard_map/ppermute | solution.py:22
  63.9 7.0 %gather_fusion = bf16[32,128,1024]{2,1,0:T(8,128)(2,1)} fusion(bf16[12,128,1024]{2,1,0:T(8,128)(2,1)} %constant_dynamic-update-slice_fusion, s32[1024]{0:T(1024)S(1)} %pad_clamp_fusion), kind=kCustom, calls=%fused_computation.4 | custom fusion | bytes 16777344 | tf_op jit(solution)/shard_map/while/body/eval_jaxpr/jit(_take)/gather | solution.py:133
  70.9 7.5 %broadcast_select_fusion = bf16[4,8,128,1024]{3,2,1,0:T(8,128)(2,1)} fusion(bf16[4,8,128,1024]{3,2,1,0:T(8,128)(2,1)} %bitcast.111, pred[4,8]{1,0:T(4,128)(4,1)S(1)} %get-tuple-element.53), kind=kLoop, calls=%fused_computation.18 | loop fusion | flops 4194304 | bytes 16777248 | tf_op jit(solution)/shard_map/while/body/eval_jaxpr/jit(_take)/select_n | solution.py:133
  78.4 5.9 %fusion.74 = (bf16[4,8,128,512]{3,2,1,0:T(8,128)(2,1)}, bf16[4,8,128,512]{3,2,1,0:T(8,128)(2,1)}) fusion(bf16[4,8,128,1024]{3,2,1,0:T(8,128)(2,1)} %broadcast_select_fusion), kind=kLoop, calls=%fused_computation.171 | loop fusion | bytes 16777216 | tf_op jit(solution)/shard_map/while/body/eval_jaxpr/vmap()/slice | solution.py:31
  84.3 6.9 %reshape.576 = bf16[4,1024,4,128]{3,2,1,0:T(4,128)(2,1)} reshape(bf16[4,8,128,512]{3,2,1,0:T(8,128)(2,1)} %get-tuple-element.56) | data formatting | bytes 8388608 | tf_op jit(solution)/shard_map/while/body/eval_jaxpr/vmap()/reshape | solution.py:30
  91.2 7.5 %copy.96 = bf16[4,1024,4,128]{1,3,2,0:T(8,128)(2,1)} copy(bf16[4,1024,4,128]{3,2,1,0:T(4,128)(2,1)} %reshape.576) | data formatting | bytes 8388608 | tf_op jit(solution)/shard_map/while/body/eval_jaxpr/vmap()/reshape | solution.py:30
  98.7 6.9 %reshape.577 = bf16[4,1024,4,128]{3,2,1,0:T(4,128)(2,1)} reshape(bf16[4,8,128,512]{3,2,1,0:T(8,128)(2,1)} %get-tuple-element.55) | data formatting | bytes 8388608 | tf_op jit(solution)/shard_map/while/body/eval_jaxpr/vmap()/reshape | solution.py:31
  105.6 7.6 %copy.95 = bf16[4,1024,4,128]{1,3,2,0:T(8,128)(2,1)} copy(bf16[4,1024,4,128]{3,2,1,0:T(4,128)(2,1)} %reshape.577) | data formatting | bytes 8388608 | tf_op jit(solution)/shard_map/while/body/eval_jaxpr/vmap()/reshape | solution.py:31
  113.2 6.8 %fusion.77 = f32[4,4,128,1024]{3,2,1,0:T(8,128)} fusion(bf16[4,128,4,128]{1,3,2,0:T(8,128)(2,1)S(1)} %copy-done.3, bf16[4,1024,4,128]{1,3,2,0:T(8,128)(2,1)} %copy.95), kind=kOutput, calls=%fused_computation.174 | convolution fusion | flops 536870912 | bytes 13107200 | tf_op jit(solution)/shard_map/while/body/eval_jaxpr/vmap(qhd,khd->hqk)/dot_general | solution.py:48
  120.0 8.5 %fusion.76 = (f32[4,4,128]{2,1,0:T(4,128)S(1)}, f32[4,4,128,1024]{3,2,1,0:T(8,128)}) fusion(pred[4,1024]{1,0:T(4,128)(4,1)S(1)} %bitcast.123, bf16[4,128,4,128]{1,3,2,0:T(8,128)(2,1)S(1)} %copy-done.7, bf16[4,1024,4,128]{1,3,2,0:T(8,128)(2,1)} %copy.96), kind=kOutput, calls=%fused_computation.173 | convolution fusion | flops 545260544 | bytes 13119488 | tf_op jit(solution)/shard_map/while/body/eval_jaxpr/vmap()/sub | solution.py:41
  128.5 6.9 %fusion.30 = bf16[4,128,4,128]{1,3,2,0:T(8,128)(2,1)} fusion(bf16[4,1024,4,128]{1,3,2,0:T(8,128)(2,1)} %copy.95, f32[4,4,128,1024]{3,2,1,0:T(8,128)} %get-tuple-element.67, f32[4,4,128]{2,1,0:T(4,128)S(1)} %get-tuple-element.66), kind=kOutput, calls=%fused_computation.42 | convolution fusion | flops 541327360 | bytes 13115392 | tf_op jit(solution)/shard_map/while/body/eval_jaxpr/vmap(hqk,khd->qhd)/dot_general | solution.py:44
  135.6 4.0 convolution_bitcast_fusion
  139.6 23.7 %fusion.15 = f32[4,1024,4,128]{1,3,2,0:T(8,128)} fusion(bf16[4,128,4,128]{1,3,2,0:T(8,128)(2,1)S(1)} %copy-done.7, f32[4,4,128,1024]{3,2,1,0:T(8,128)} %fusion.77, f32[4,4,128,1024]{3,2,1,0:T(8,128)} %get-tuple-element.67, f32[4,4,128]{2,1,0:T(4,128)S(1)} %get-tuple-element.66), kind=kOutput, calls=%fused_computation.26 | convolution fusion | flops 551554048 | bytes 25698304 | tf_op jit(solution)/shard_map/while/body/eval_jaxpr/vmap(hqk,qhd->khd)/dot_general | solution.py:54
  163.3 9.9 %copy.89 = f32[4,1024,4,128]{3,2,1,0:T(4,128)} copy(f32[4,1024,4,128]{1,3,2,0:T(8,128)} %fusion.15) | data formatting | bytes 16777216 | tf_op jit(solution)/shard_map/while/body/eval_jaxpr/vmap(hqk,qhd->khd)/transpose | solution.py:54
  173.2 10.3 %concatenate.21 = f32[32,128,512]{2,1,0:T(8,128)} reshape(f32[4,1024,4,128]{3,2,1,0:T(4,128)} %copy.89) | data formatting | bytes 16777216 | tf_op jit(solution)/shard_map/while/body/eval_jaxpr/vmap()/concatenate | solution.py:60
  183.5 9.9 %copy.91 = f32[4,1024,4,128]{3,2,1,0:T(4,128)} copy(f32[4,1024,4,128]{1,3,2,0:T(8,128)} %convolution_bitcast_fusion) | data formatting | bytes 16777216 | tf_op jit(solution)/shard_map/while/body/eval_jaxpr/vmap(hqk,qhd->khd)/transpose | solution.py:55
  193.4 10.3 %concatenate.22 = f32[32,128,512]{2,1,0:T(8,128)} reshape(f32[4,1024,4,128]{3,2,1,0:T(4,128)} %copy.91) | data formatting | bytes 16777216 | tf_op jit(solution)/shard_map/while/body/eval_jaxpr/vmap()/concatenate | solution.py:60
  203.6 11.7 %pad_maximum_fusion = f32[32,128,1024]{2,1,0:T(8,128)} fusion(f32[32,128,512]{2,1,0:T(8,128)} %concatenate.22, f32[32,128,512]{2,1,0:T(8,128)} %concatenate.21), kind=kLoop, calls=%fused_computation.12 | loop fusion | flops 4194304 | bytes 33554432 | tf_op jit(solution)/shard_map/while/body/eval_jaxpr/vmap()/concatenate | solution.py:60
  215.4 3.4 broadcast_in_dim.161
  218.7 35.9 %scatter_fusion = f32[12,128,1024]{2,1,0:T(8,128)} fusion(f32[12,128,1024]{2,1,0:T(8,128)} %broadcast_in_dim.161, s32[32]{0:T(128)S(1)} %fusion.61, f32[32,128,1024]{2,1,0:T(8,128)} %pad_maximum_fusion), kind=kCustom, calls=%fused_computation.5 | custom fusion | flops 4194304 | bytes 50331776 | tf_op jit(solution)/shard_map/while/body/eval_jaxpr/scatter-add | solution.py:137
  254.6 4.9 %convert.25 = bf16[12,128,1024]{2,1,0:T(8,128)(2,1)} convert(f32[12,128,1024]{2,1,0:T(8,128)} %scatter_fusion) | non-fusion elementwise | flops 1572864 | bytes 9437184 | tf_op jit(solution)/shard_map/convert.17
  259.6 3.2 slice.56
  263.9 2.9 fusion.75
  266.8 3.4 collective-permute-start.4
  273.0 22.8 %fusion.33 = bf16[4,128,4,128]{1,3,2,0:T(8,128)(2,1)S(1)} fusion(bf16[4,1024,4,128]{1,3,2,0:T(8,128)(2,1)} %copy.96, f32[4,4,128,1024]{3,2,1,0:T(8,128)} %fusion.77, f32[4,4,128,1024]{3,2,1,0:T(8,128)} %get-tuple-element.67, f32[4,4,128]{2,1,0:T(4,128)S(1)} %get-tuple-element.66), kind=kOutput, calls=%fused_computation.43 | convolution fusion | flops 551816192 | bytes 21504000 | tf_op jit(solution)/shard_map/while/body/eval_jaxpr/vmap(hqk,khd->qhd)/dot_general | solution.py:51
  298.1 2.5 fusion.45
  300.6 2.1 convert_element_type.189
  302.7 3.4 scatter_fusion.1
  306.1 2.1 convert_element_type.190
  308.2 3.4 scatter_fusion.2
  311.6 2.1 convert_element_type.191
  313.7 3.4 scatter_fusion.3
  317.1 2.1 convert_element_type.192
  319.3 3.4 scatter_fusion.4
  325.4 2.7 fusion.42
  329.1 2.3 fusion.36
  332.7 139.3 %all-reduce.3.cloned.1.call-done = (f32[512,1536]{1,0:T(8,128)}, f32[512,512]{1,0:T(8,128)}) async-done(((f32[512,1536]{1,0:T(8,128)}, f32[512,512]{1,0:T(8,128)}), (f32[512,1536]{1,0:T(8,128)}, f32[512,512]{1,0:T(8,128)})) %all-reduce.3.cloned.1.call-update) | async-done | bytes 4194320 | tf_op jit(solution)/shard_map/psum | solution.py:175
  472.1 3.9 broadcast_multiply_fusion
  (126 shorter events, 39.4 us)
Async XLA Ops:
  7.2 3.7 copy-start
  7.2 464.9 %all-reduce.3.cloned.1.call-start = ((), (), s32[]{:S(2)}) async-start(), calls=%async_computation | async-start | bytes 8388608 | tf_op jit(solution)/shard_map/psum | solution.py:175
  11.9 1.1 copy-start.5
  13.1 23.5 %copy-start.9 = (s32[32,8]{0,1:T(8,128)S(1)}, s32[32,8]{0,1:T(8,128)}, u32[]{:S(2)}) copy-start(s32[32,8]{0,1:T(8,128)} %param.13) | copy-start | bytes 3076
  16.4 45.6 %collective-permute-start.3 = (bf16[2,128,1024]{2,1,0:T(8,128)(2,1)}, bf16[2,128,1024]{2,1,0:T(8,128)(2,1)}, u32[]{:S(2)}, u32[]{:S(2)}) collective-permute-start(bf16[2,128,1024]{2,1,0:T(8,128)(2,1)} %broadcast_select_fusion.1), channel_id=1, source_target_pairs={{0,24},{4,28},{8,0},{12,4},{16,8},{20,12},{24,16},{28,20},{1,25},{... | collective-permute-start | bytes 1572872 | tf_op jit(solution)/shard_map/ppermute | solution.py:22
  24.9 35.3 %collective-permute-start.2 = (bf16[2,128,1024]{2,1,0:T(8,128)(2,1)}, bf16[2,128,1024]{2,1,0:T(8,128)(2,1)}, u32[]{:S(2)}, u32[]{:S(2)}) collective-permute-start(bf16[2,128,1024]{2,1,0:T(8,128)(2,1)} %broadcast_select_fusion.2), channel_id=1, source_target_pairs={{0,28},{4,0},{8,4},{12,8},{16,12},{20,16},{24,20},{28,24},{1,29},{... | collective-permute-start | bytes 1572872 | tf_op jit(solution)/shard_map/ppermute | solution.py:22
  30.2 28.1 %collective-permute-start.1 = (bf16[2,128,1024]{2,1,0:T(8,128)(2,1)}, bf16[2,128,1024]{2,1,0:T(8,128)(2,1)}, u32[]{:S(2)}, u32[]{:S(2)}) collective-permute-start(bf16[2,128,1024]{2,1,0:T(8,128)(2,1)} %broadcast_select_fusion.3), channel_id=1, source_target_pairs={{0,4},{4,8},{8,12},{12,16},{16,20},{20,24},{24,28},{28,0},{1,5},{5... | collective-permute-start | bytes 1572872 | tf_op jit(solution)/shard_map/ppermute | solution.py:22
  34.2 22.3 %collective-permute-start = (bf16[2,128,1024]{2,1,0:T(8,128)(2,1)}, bf16[2,128,1024]{2,1,0:T(8,128)(2,1)}, u32[]{:S(2)}, u32[]{:S(2)}) collective-permute-start(bf16[2,128,1024]{2,1,0:T(8,128)(2,1)} %broadcast_select_fusion.4), channel_id=1, source_target_pairs={{0,8},{4,12},{8,16},{12,20},{16,24},{20,28},{24,0},{28,4},{1,9},{5... | collective-permute-start | bytes 1572872 | tf_op jit(solution)/shard_map/ppermute | solution.py:22
  105.6 7.6 %copy-start.3 = (bf16[4,128,4,128]{1,3,2,0:T(8,128)(2,1)S(1)}, bf16[4,128,4,128]{1,3,2,0:T(8,128)(2,1)}, u32[]{:S(2)}) copy-start(bf16[4,128,4,128]{1,3,2,0:T(8,128)(2,1)} %copy.90) | copy-start | bytes 1572868
  113.2 6.8 %copy-start.7 = (bf16[4,128,4,128]{1,3,2,0:T(8,128)(2,1)S(1)}, bf16[4,128,4,128]{1,3,2,0:T(8,128)(2,1)}, u32[]{:S(2)}) copy-start(bf16[4,128,4,128]{1,3,2,0:T(8,128)(2,1)} %copy.88) | copy-start | bytes 1572868
  128.5 7.0 %copy-start.10 = (f32[4,4,128,1024]{3,2,1,0:T(8,128)S(1)}, f32[4,4,128,1024]{3,2,1,0:T(8,128)}, u32[]{:S(2)}) copy-start(f32[4,4,128,1024]{3,2,1,0:T(8,128)} %get-tuple-element.67) | copy-start | bytes 25165828
  259.6 3.2 copy-start.8
  266.8 33.8 %collective-permute-start.4 = (bf16[2,128,1024]{2,1,0:T(8,128)(2,1)}, bf16[2,128,1024]{2,1,0:T(8,128)(2,1)}, u32[]{:S(2)}, u32[]{:S(2)}) collective-permute-start(bf16[2,128,1024]{2,1,0:T(8,128)(2,1)} %get-tuple-element.60), channel_id=1, source_target_pairs={{0,24},{4,28},{8,0},{12,4},{16,8},{20,12},{24,16},{28,20},{1,25},{... | collective-permute-start | bytes 1572872 | tf_op jit(solution)/shard_map/ppermute | solution.py:22
  270.2 35.9 %collective-permute-start.5 = (bf16[2,128,1024]{2,1,0:T(8,128)(2,1)}, bf16[2,128,1024]{2,1,0:T(8,128)(2,1)}, u32[]{:S(2)}, u32[]{:S(2)}) collective-permute-start(bf16[2,128,1024]{2,1,0:T(8,128)(2,1)} %get-tuple-element.59), channel_id=1, source_target_pairs={{0,28},{4,0},{8,4},{12,8},{16,12},{20,16},{24,20},{28,24},{1,29},{... | collective-permute-start | bytes 1572872 | tf_op jit(solution)/shard_map/ppermute | solution.py:22
  271.7 39.9 %collective-permute-start.6 = (bf16[2,128,1024]{2,1,0:T(8,128)(2,1)}, bf16[2,128,1024]{2,1,0:T(8,128)(2,1)}, u32[]{:S(2)}, u32[]{:S(2)}) collective-permute-start(bf16[2,128,1024]{2,1,0:T(8,128)(2,1)} %get-tuple-element.58), channel_id=1, source_target_pairs={{0,4},{4,8},{8,12},{12,16},{16,20},{20,24},{24,28},{28,0},{1,5},{5... | collective-permute-start | bytes 1572872 | tf_op jit(solution)/shard_map/ppermute | solution.py:22
  272.2 25.9 %copy-start.1 = (bf16[1,512,512]{2,1,0:T(8,128)(2,1)S(1)}, bf16[1,512,512]{2,1,0:T(8,128)(2,1)}, u32[]{:S(2)}) copy-start(bf16[1,512,512]{2,1,0:T(8,128)(2,1)} %param.9) | copy-start | bytes 1572868
  272.2 45.0 %collective-permute-start.7 = (bf16[2,128,1024]{2,1,0:T(8,128)(2,1)}, bf16[2,128,1024]{2,1,0:T(8,128)(2,1)}, u32[]{:S(2)}, u32[]{:S(2)}) collective-permute-start(bf16[2,128,1024]{2,1,0:T(8,128)(2,1)} %get-tuple-element.57), channel_id=1, source_target_pairs={{0,8},{4,12},{8,16},{12,20},{16,24},{20,28},{24,0},{28,4},{1,9},{5... | collective-permute-start | bytes 1572872 | tf_op jit(solution)/shard_map/ppermute | solution.py:22
  324.4 1.0 copy-start.2
  329.1 2.3 copy-start.4
  472.1 3.9 copy-start.6
Sparse Core Ops, SparseCore 0:
  328.2 143.8 all-reduce.2
where the time goes:
time: 487 us; the launch traced here: 484 us
  waiting for transfers between devices  145 us (30%)
  local copies, waits for them, and re-layouts  126 us (26%)
  other arithmetic  99.8 us (20%)
  matrix products  83.7 us (17%)
  starting transfers between devices  14.4 us (3%)
  between operations  14.4 us (3%)
    psum x1, waiting for transfers between devices, on_device(): lax.psum((local_qkv, local_out), ('patch', 'sample'))  139 us
    scatter-add x1, other arithmetic, advance(): running.at[flat_slots]  35.9 us
    dot_general x1, matrix products, tile_backward(): jnp.einsum('hqk,qhd->khd', dscore, query_heads, preferred_element_type=jn...  23.7 us
    dot_general x1, matrix products, tile_backward(): jnp.einsum('hqk,khd->qhd', dscore, key_heads, preferred_element_type=jnp....  22.8 us
    concatenate x2, local copies, waits for them, and re-layouts, tile_backward(): return (attended, dquery, jnp.concatenate([dkey, dvalue], -1))  20.5 us
    reshape x2, local copies, waits for them, and re-layouts, tile_backward(): pair_tiles[:, :, model_width:].reshape(-1, head_count, head_width)  14.5 us
    reshape x2, local copies, waits for them, and re-layouts, tile_backward(): pair_tiles[:, :, :model_width].reshape(-1, head_count, head_width)  14.4 us
    ppermute x8, starting transfers between devices, from_behind(): return lax.ppermute(value, axis, pairs)  14.3 us
  transfers between devices with their start and end apart: 9, of which 2 were waited for; matrix products, arithmetic and copies ran while one was open for 17% of the time, Pallas kernels for 0%

commit v1 on v0

v1 whole, which is shorter than its diff:
```python
from functools import partial

import jax
import jax.numpy as jnp
from jax import lax
from jax.experimental import pallas as pl
from jax.experimental.pallas import tpu as pltpu
from jax.sharding import PartitionSpec as P

HEADS = 4
TILE = 128
NB = 8
REACH = 2
CAP = 2
OFFSETS = [shift_by for shift_by in range(-REACH, REACH + 1) if shift_by != 0]
LOCAL = NB - len(OFFSETS)
SLOTS = CAP * len(OFFSETS)
MASKED = -1e30
AXES = ("patch", "sample")

epsilon = 1e-06

VMEM = pl.BlockSpec(memory_space=pltpu.VMEM)
SMEM = pl.BlockSpec(memory_space=pltpu.SMEM)


def nn(a, b):
    return jnp.dot(a, b, preferred_element_type=jnp.float32)


def nt(a, b):
    return lax.dot_general(a, b, (((1,), (1,)), ((), ())), preferred_element_type=jnp.float32)


def tn(a, b):
    return lax.dot_general(a, b, (((0,), (0,)), ((), ())), preferred_element_type=jnp.float32)


def normalise(rows):
    inputs = rows.astype(jnp.float32)
    inverse = lax.rsqrt(jnp.mean(inputs * inputs, -1, keepdims=True) + epsilon)
    return inputs * inverse, inverse


def named_pair(tiles_ref, first_row, column, count):
    named = [tiles_ref[first_row + row, column] for row in range(count)]
    low = high = named[0]
    for entry in named[1:]:
        low = jnp.minimum(low, entry)
        high = jnp.maximum(high, entry)
    return low, high


def sent_rows(tiles_ref, position, patches, column, shift_by, tile_count):
    target = lax.rem(position - shift_by + patches, patches)
    pair = named_pair(tiles_ref, target * tile_count, LOCAL + column, tile_count)
    return [pl.multiple_of((entry - position * tile_count) * TILE, TILE) for entry in pair]


def pack_kernel(patches, tiles_ref, place_ref, features_ref, *packed_refs):
    position = place_ref[0]
    tile_count = features_ref.shape[0] // TILE
    for column, shift_by in enumerate(OFFSETS):
        rows = sent_rows(tiles_ref, position, patches, column, shift_by, tile_count)
        for slot, first in enumerate(rows):
            packed_refs[column][slot] = features_ref[pl.ds(first, TILE), :]


def front_kernel(
    features_ref, cotangent_ref, weight_qkv_ref, weight_out_ref, normed_ref, projected_ref, grad_ref
):
    normed = normalise(features_ref[...])[0].astype(jnp.bfloat16)
    normed_ref[...] = normed
    projected_ref[...] = nn(normed, weight_qkv_ref[...]).astype(jnp.bfloat16)
    grad_ref[...] = nt(cotangent_ref[...], weight_out_ref[...]).astype(jnp.bfloat16)


def main_kernel(
    tiles_ref,
    valid_ref,
    place_ref,
    projected_ref,
    grad_ref,
    halo_a,
    halo_b,
    halo_c,
    halo_d,
    weight_ref,
    back_a,
    back_b,
    back_c,
    back_d,
    grad_own_ref,
    gp_own_ref,
    gp_halo_ref,
    normed_halo_ref,
    attended_ref,
    pair_s,
    prob_s,
    dscore_s,
    dkey_s,
    dvalue_s,
):
    halos = (halo_a, halo_b, halo_c, halo_d)
    backs = (back_a, back_b, back_c, back_d)
    position = place_ref[0]
    rows_local, width = grad_ref.shape
    tile_count = rows_local // TILE
    head_width = width // HEADS
    scaling = head_width ** (-0.5)
    first_row = position * tile_count
    for column, halo in enumerate(halos):
        for slot in range(CAP):
            normed = normalise(halo[slot])[0].astype(jnp.bfloat16)
            normed_halo_ref[pl.ds((column * CAP + slot) * TILE, TILE), :] = normed

    lane_tile = lax.broadcasted_iota(jnp.int32, (1, TILE), 1) * 0
    biases = []
    slots = []
    for tile in range(tile_count):
        row = first_row + tile
        pieces = []
        for other in range(tile_count):
            flag = jnp.int32(0)
            for column in range(LOCAL):
                flag = flag + jnp.where(
                    tiles_ref[row, column] == first_row + other, valid_ref[row, column], 0
                )
            pieces.append(jnp.where(lane_tile + flag > 0, 0.0, MASKED))
        places = []
        for column in range(len(OFFSETS)):
            high = named_pair(tiles_ref, first_row, LOCAL + column, tile_count)[1]
            place = jnp.where(tiles_ref[row, LOCAL + column] == high, 1, 0)
            places.append(column * CAP + place)
            flag = valid_ref[row, LOCAL + column]
            pieces.append(jnp.where(lane_tile + flag > 0, 0.0, MASKED))
        biases.append(jnp.concatenate(pieces, 1))
        slots.append(places)

    def one_head(head, carry):
        lanes = pl.ds(pl.multiple_of(head * head_width, head_width), head_width)
        key_lanes = pl.ds(pl.multiple_of(width + head * head_width, head_width), head_width)
        value_lanes = pl.ds(pl.multiple_of(2 * width + head * head_width, head_width), head_width)
        both = jnp.concatenate([weight_ref[:, key_lanes], weight_ref[:, value_lanes]], 1)
        pair_s[...] = nn(normed_halo_ref[...], both).astype(jnp.bfloat16)
        keys = projected_ref[:, key_lanes]
        values = projected_ref[:, value_lanes]
        queries_t = projected_ref[:, lanes].T
        grads_t = grad_ref[:, lanes].T
        dkey_s[...] = jnp.zeros_like(dkey_s)
        dvalue_s[...] = jnp.zeros_like(dvalue_s)
        for tile in range(tile_count):
            rows = pl.ds(tile * TILE, TILE)
            query = projected_ref[rows, lanes]
            grad = grad_ref[rows, lanes]
            starts = [pl.multiple_of(place * TILE, TILE) for place in slots[tile]]
            key_all = jnp.concatenate(
                [keys] + [pair_s[pl.ds(start, TILE), :head_width] for start in starts], 0
            )
            value_all = jnp.concatenate(
                [values] + [pair_s[pl.ds(start, TILE), head_width:] for start in starts], 0
            )
            scores = nt(query, key_all) * scaling + biases[tile]
            highest = jnp.max(scores, -1, keepdims=True)
            expanded = jnp.exp(scores - highest)
            attention = expanded * (1.0 / jnp.sum(expanded, -1, keepdims=True))
            low = attention.astype(jnp.bfloat16)
            attended_ref[rows, lanes] = nn(low, value_all).astype(jnp.bfloat16)
            dprob = nt(grad, value_all)
            centre = jnp.sum(attention * dprob, -1, keepdims=True)
            dscore = (attention * (dprob - centre)).astype(jnp.bfloat16)
            gp_own_ref[rows, lanes] = (nn(dscore, key_all) * scaling).astype(jnp.bfloat16)
            prob_s[rows, :] = low[:, :rows_local]
            dscore_s[rows, :] = dscore[:, :rows_local]
            dkey_t = nn(queries_t[:, tile * TILE : (tile + 1) * TILE], dscore[:, rows_local:])
            dvalue_t = nn(grads_t[:, tile * TILE : (tile + 1) * TILE], low[:, rows_local:])
            for column, place in enumerate(slots[tile]):
                part = slice(column * TILE, (column + 1) * TILE)
                dkey_s[place] += dkey_t[:, part]
                dvalue_s[place] += dvalue_t[:, part]
        dkey_own = nn(queries_t, dscore_s[...]) * scaling
        gp_own_ref[:, key_lanes] = dkey_own.T.astype(jnp.bfloat16)
        gp_own_ref[:, value_lanes] = nn(grads_t, prob_s[...]).T.astype(jnp.bfloat16)
        for place in range(SLOTS):
            rows = pl.ds(place * TILE, TILE)
            gp_halo_ref[rows, lanes] = (dkey_s[place] * scaling).T.astype(jnp.bfloat16)
            gp_halo_ref[rows, key_lanes] = dvalue_s[place].T.astype(jnp.bfloat16)
        return carry

    lax.fori_loop(0, HEADS, one_head, 0)
    for column, back in enumerate(backs):
        rows = pl.ds(column * CAP * TILE, CAP * TILE)
        part = nt(gp_halo_ref[rows, :], weight_ref[:, width:]).astype(jnp.bfloat16)
        back[...] = part.reshape(back.shape)
    grad_own_ref[...] = nt(gp_own_ref[...], weight_ref[...])


def weight_kernel(
    place_ref, normed_ref, normed_halo_ref, gp_own_ref, gp_halo_ref, attended_ref, cotangent_ref, out_ref
):
    width = normed_ref.shape[1]
    half = width // 2
    first = pl.multiple_of(place_ref[1] * half, half)
    lanes = pl.ds(first, half)
    normed = normed_ref[:, lanes]
    out_ref[:, :width] = tn(normed, gp_own_ref[:, :width]).astype(out_ref.dtype)
    pairs = tn(normed, gp_own_ref[:, width:]) + tn(normed_halo_ref[:, lanes], gp_halo_ref[...])
    out_ref[:, width : 3 * width] = pairs.astype(out_ref.dtype)
    out_ref[:, 3 * width :] = tn(attended_ref[:, lanes], cotangent_ref[...]).astype(out_ref.dtype)


def input_kernel(
    patches,
    tiles_ref,
    place_ref,
    features_ref,
    cotangent_ref,
    grad_own_ref,
    back_a,
    back_b,
    back_c,
    back_d,
    out_ref,
    total_s,
):
    position = place_ref[0]
    tile_count = features_ref.shape[0] // TILE
    total_s[...] = grad_own_ref[...]
    for column, (shift_by, back) in enumerate(zip(OFFSETS, (back_a, back_b, back_c, back_d))):
        rows = sent_rows(tiles_ref, position, patches, column, shift_by, tile_count)
        for slot, first in enumerate(rows):
            total_s[pl.ds(first, TILE), :] += back[slot].astype(jnp.float32)
    normed, inverse = normalise(features_ref[...])
    total = total_s[...]
    centred = total - normed * jnp.mean(total * normed, -1, keepdims=True)
    out_ref[...] = (cotangent_ref[...].astype(jnp.float32) + inverse * centred).astype(out_ref.dtype)


def from_behind(value, steps):
    count = lax.axis_size("patch")
    pairs = [(source, (source + steps) % count) for source in range(count)]
    return lax.ppermute(value, "patch", pairs)


def exchange(value, flip, count):
    return lax.ppermute(value, AXES, [(source, source ^ flip) for source in range(count)])


def flips_of(bits):
    return [
        sum(((step >> place) & 1) << bit for place, bit in enumerate(bits))
        for step in range(1 << len(bits))
    ]


def digit_of(index, bits):
    return sum(((index >> bit) & 1) << place for place, bit in enumerate(bits))


def reduce_phase(value, index, bits, count):
    flips = flips_of(bits)
    digit = digit_of(index, bits)
    pieces = value.reshape(len(flips), value.shape[0] // len(flips), value.shape[1])
    received = [
        exchange(lax.dynamic_index_in_dim(pieces, digit ^ step, 0, False), flips[step], count)
        for step in range(1, len(flips))
    ]
    total = lax.dynamic_index_in_dim(pieces, digit, 0, False).astype(jnp.float32)
    for piece in received:
        total = total + piece.astype(jnp.float32)
    return total


def gather_phase(value, index, bits, count):
    flips = flips_of(bits)
    digit = digit_of(index, bits)
    pieces = [value] + [exchange(value, flip, count) for flip in flips[1:]]
    stacked = jnp.zeros((len(flips),) + value.shape, value.dtype)
    for step, piece in enumerate(pieces):
        stacked = lax.dynamic_update_index_in_dim(stacked, piece, digit ^ step, 0)
    return stacked.reshape(len(flips) * value.shape[0], value.shape[1])


def on_device(features, cotangent, weight_qkv, weight_out, key_tiles, tile_valid):
    patches = lax.axis_size("patch")
    samples = lax.axis_size("sample")
    count = patches * samples
    position = lax.axis_index("patch").astype(jnp.int32)
    index = position * samples + lax.axis_index("sample").astype(jnp.int32)
    rows_local, width = features.shape[1:]
    rows = features[0]
    grad_rows = cotangent[0]
    low = jnp.bfloat16

    def shape(*dims, kind=low):
        return jax.ShapeDtypeStruct(dims, kind)

    params = pltpu.CompilerParams(vmem_limit_bytes=60 * 1024 * 1024)
    place = jnp.stack([position, index & 1])
    packed = pl.pallas_call(
        partial(pack_kernel, patches),
        out_shape=[shape(CAP, TILE, width)] * len(OFFSETS),
        in_specs=[SMEM, SMEM, VMEM],
        out_specs=[VMEM] * len(OFFSETS),
        name="pack",
    )(key_tiles, place, rows)
    halos = [from_behind(piece, -shift_by) for piece, shift_by in zip(packed, OFFSETS)]
    normed_low, projected, grad_attended = pl.pallas_call(
        front_kernel,
        out_shape=[shape(rows_local, width), shape(rows_local, 3 * width), shape(rows_local, width)],
        in_specs=[VMEM] * 4,
        out_specs=[VMEM] * 3,
        compiler_params=params,
        cost_estimate=pl.CostEstimate(
            flops=8 * rows_local * width * width, bytes_accessed=6 << 20, transcendentals=0
        ),
        name="front",
    )(rows, grad_rows, weight_qkv, weight_out)
    halo_rows = SLOTS * TILE
    head_width = width // HEADS
    outs = pl.pallas_call(
        main_kernel,
        out_shape=[shape(CAP, TILE, width)] * len(OFFSETS)
        + [
            shape(rows_local, width, kind=jnp.float32),
            shape(rows_local, 3 * width),
            shape(halo_rows, 2 * width),
            shape(halo_rows, width),
            shape(rows_local, width),
        ],
        in_specs=[SMEM] * 3 + [VMEM] * 7,
        out_specs=[VMEM] * (len(OFFSETS) + 5),
        scratch_shapes=[
            pltpu.VMEM((halo_rows, 2 * head_width), low),
            pltpu.VMEM((rows_local, rows_local), low),
            pltpu.VMEM((rows_local, rows_local), low),
            pltpu.VMEM((SLOTS, head_width, TILE), jnp.float32),
            pltpu.VMEM((SLOTS, head_width, TILE), jnp.float32),
        ],
        compiler_params=params,
        name="attend",
    )(key_tiles, tile_valid, place, projected, grad_attended, *halos, weight_qkv)
    backs, (grad_own, gp_own, gp_halo, normed_halo, attended) = outs[:4], outs[4:]
    returned = [from_behind(piece, shift_by) for piece, shift_by in zip(backs, OFFSETS)]

    def weights(side, kind):
        return pl.pallas_call(
            weight_kernel,
            out_shape=shape(width // 2, 4 * width, kind=kind),
            in_specs=[SMEM] + [VMEM] * 6,
            out_specs=VMEM,
            compiler_params=params,
            cost_estimate=pl.CostEstimate(
                flops=5 * rows_local * width * width, bytes_accessed=8 << 20, transcendentals=0
            ),
            name="weights",
        )(
            jnp.stack([position, side]),
            normed_low,
            normed_halo,
            gp_own,
            gp_halo,
            attended,
            grad_rows,
        )

    side = index & 1
    sent = weights(1 - side, low)
    arrived = exchange(sent, 1, count)
    kept = weights(side, jnp.float32)
    total = kept + arrived.astype(jnp.float32)
    bit_count = count.bit_length() - 1
    phases = [list(range(bit, min(bit + 2, bit_count))) for bit in range(1, bit_count, 2)]
    for bits in phases:
        total = reduce_phase(total.astype(low), index, bits, count)
    factor = float(count * rows_local) ** (-0.5)
    gathered = (total * factor).astype(low)
    for bits in phases[::-1] + [[0]]:
        gathered = gather_phase(gathered, index, bits, count)
    grad_qkv = gathered[:, : 3 * width].astype(jnp.float32)
    grad_out = gathered[:, 3 * width :].astype(jnp.float32)
    grad_features = pl.pallas_call(
        partial(input_kernel, patches),
        out_shape=shape(rows_local, width),
        in_specs=[SMEM, SMEM] + [VMEM] * 7,
        out_specs=VMEM,
        scratch_shapes=[pltpu.VMEM((rows_local, width), jnp.float32)],
        compiler_params=params,
        cost_estimate=pl.CostEstimate(
            flops=20 * rows_local * width, bytes_accessed=4 << 20, transcendentals=0
        ),
        name="inputs",
    )(key_tiles, place, rows, grad_rows, grad_own, *returned)
    return (grad_features[None], grad_qkv, grad_out)


def solution(mesh):
    placed = (P("sample", "patch", None), P("sample", "patch", None), P(), P(), P(), P())
    return jax.shard_map(
        on_device,
        mesh=mesh,
        in_specs=placed,
        out_specs=(P("sample", "patch", None), P(), P()),
        check_vma=False,
    )
```

time: 487 us -> 141 us (0.29)
  local copies, waits for them, and re-layouts: 126 us -> 4.94 us
  other arithmetic: 99.8 us -> 6.39 us
  waiting for transfers between devices: 145 us -> 54.3 us
  matrix products: 83.7 us -> 0 us
  Pallas kernels: 0 us -> 45.9 us
  starting transfers between devices: 14.4 us -> 28.4 us
  between operations: 14.4 us -> 0.83 us
    psum x1 -> x0, waiting for transfers between devices: 139 us -> none  [on_device(): lax.psum((local_qkv, local_out), ('patch', 'sample'))]
    dot_general x10 -> x0, matrix products: 75.2 us -> none  [the longest x1 23.7 us: tile_backward(): jnp.einsum('hqk,qhd->khd', dscore, query_heads, preferred_element_type=jn...]
    scatter-add x5 -> x0, other arithmetic: 49.5 us -> none  [the longest x1 35.9 us: advance(): running.at[flat_slots]]
    ppermute x8 -> x22, waiting for transfers between devices: 6.06 us -> 54.3 us  [the longest x14 29.4 us: exchange(): lax.ppermute(value, AXES, [(source, source ^ flip) for source in range(co...]
    pallas_call x0 -> x6, Pallas kernels: none -> 45.9 us  [the longest x1 25.8 us: on_device(): pl.pallas_call(main_kernel, out_shape=[shape(CAP, TILE, width)] * len(OFF...]
    reshape x9 -> x0, local copies, waits for them, and re-layouts: 37.1 us -> none  [the longest x2 14.5 us: tile_backward(): pair_tiles[:, :, model_width:].reshape(-1, head_count, head_width)]
    concatenate x3 -> x0, local copies, waits for them, and re-layouts: 22.4 us -> none  [the longest x2 20.5 us: tile_backward(): return (attended, dquery, jnp.concatenate([dkey, dvalue], -1))]
    transpose x3 -> x0, local copies, waits for them, and re-layouts: 20.9 us -> none  [the longest x1 9.91 us: tile_backward(): jnp.einsum('hqk,qhd->khd', dscore, query_heads, preferred_element_type=jn...]
  transfers between devices with their start and end apart: 9 -> 22, of which waited for: 2 -> 14; matrix products, arithmetic and copies ran while one was open for 17% -> 2% of each run, Pallas kernels for 0% -> 9%
where the time goes in v1:
time: 141 us
  waiting for transfers between devices  54.3 us (39%)
  Pallas kernels  45.9 us (33%)
  starting transfers between devices  28.4 us (20%)
  other arithmetic  6.39 us (5%)
  local copies, waits for them, and re-layouts  4.94 us (4%)
    ppermute x14, waiting for transfers between devices, exchange(): lax.ppermute(value, AXES, [(source, source ^ flip) for source in range(co...  29.4 us
    pallas_call x1, Pallas kernels, on_device(): pl.pallas_call(main_kernel, out_shape=[shape(CAP, TILE, width)] * len(OFF...  25.8 us
    ppermute x8, waiting for transfers between devices, from_behind(): return lax.ppermute(value, 'patch', pairs)  24.9 us
    ppermute x14, starting transfers between devices, exchange(): lax.ppermute(value, AXES, [(source, source ^ flip) for source in range(co...  16.1 us
    ppermute x8, starting transfers between devices, from_behind(): return lax.ppermute(value, 'patch', pairs)  12.4 us
    pallas_call x2, Pallas kernels, weights(): pl.pallas_call(weight_kernel, out_shape=shape(width // 2, 4 * width, kind...  10.5 us
    pallas_call x1, Pallas kernels, on_device(): pl.pallas_call(front_kernel, out_shape=[shape(rows_local, width), shape(r...  4.22 us
    unnamed x20, local copies, waits for them, and re-layouts  4.12 us
  transfers between devices with their start and end apart: 22, of which 14 were waited for; matrix products, arithmetic and copies ran while one was open for 2% of the time, Pallas kernels for 9%

profile of v1, /device:TPU:0, one launch (start us, length us, event | category | flops | bytes accessed | tf_op | source)
XLA Modules:
  0.0 140.8 jit_solution(10632374822284110232)
XLA Ops:
  0.6 1.4 copy.12.tiles_ref
  2.0 0.6 pad_add_fusion.place_ref
  2.6 2.1 %pack.1 = (bf16[2,128,512]{2,1,0:T(8,128)(2,1)}, bf16[2,128,512]{2,1,0:T(8,128)(2,1)}, bf16[2,128,512]{2,1,0:T(8,128)(2,1)}, bf16[2,128,512]{2,1,0:T(8,128)(2,1)}) custom-call(s32[32,8]{1,0:T(8,128)} %copy.12.tiles_ref, s32[2]{0:T(128)} %pad_add_fusion.place_ref, bf16[512,512]{1,0:T(8,128)(2,1)} %bitcast.62), custom_call_target="tpu_custom_call" | custom-call | tf_op jit(solution)/shard_map/pack/pallas_call | solution.py:300
  4.7 3.1 %collective-permute-start = (bf16[2,128,512]{2,1,0:T(8,128)(2,1)}, bf16[2,128,512]{2,1,0:T(8,128)(2,1)S(1)}, u32[]{:S(2)}, u32[]{:S(2)}) collective-permute-start(bf16[2,128,512]{2,1,0:T(8,128)(2,1)} %get-tuple-element.21), channel_id=1, source_target_pairs={{0,8},{4,12},{8,16},{12,20},{16,24},{20,28},{24,0},{28,4},{1,9},{5... | collective-permute-start | bytes 786440 | tf_op jit(solution)/shard_map/ppermute | solution.py:242
  7.8 1.5 %collective-permute-start.1 = (bf16[2,128,512]{2,1,0:T(8,128)(2,1)}, bf16[2,128,512]{2,1,0:T(8,128)(2,1)S(1)}, u32[]{:S(2)}, u32[]{:S(2)}) collective-permute-start(bf16[2,128,512]{2,1,0:T(8,128)(2,1)} %get-tuple-element.22), channel_id=1, source_target_pairs={{0,4},{4,8},{8,12},{12,16},{16,20},{20,24},{24,28},{28,0},{1,5},{5... | collective-permute-start | bytes 786440 | tf_op jit(solution)/shard_map/ppermute | solution.py:242
  9.3 3.2 %collective-permute-start.2 = (bf16[2,128,512]{2,1,0:T(8,128)(2,1)}, bf16[2,128,512]{2,1,0:T(8,128)(2,1)S(1)}, u32[]{:S(2)}, u32[]{:S(2)}) collective-permute-start(bf16[2,128,512]{2,1,0:T(8,128)(2,1)} %get-tuple-element.23), channel_id=1, source_target_pairs={{0,28},{4,0},{8,4},{12,8},{16,12},{20,16},{24,20},{28,24},{1,29},{... | collective-permute-start | bytes 786440 | tf_op jit(solution)/shard_map/ppermute | solution.py:242
  12.5 0.3 collective-permute-start.3
  12.8 1.4 copy.11.valid_ref
  14.2 4.2 %front.1 = (bf16[512,512]{1,0:T(8,128)(2,1)}, bf16[512,1536]{1,0:T(8,128)(2,1)}, bf16[512,512]{1,0:T(8,128)(2,1)}) custom-call(bf16[512,512]{1,0:T(8,128)(2,1)} %bitcast.63, bf16[512,512]{1,0:T(8,128)(2,1)} %bitcast.54, bf16[512,1536]{1,0:T(8,128)(2,1)} %weight_ref.1, bf16[512,512]{1,0:T(8,128)(2,1)} %weight_out_ref.1), custom_call_target="tpu_custom_call" | custom-call | flops 1073741824 | bytes 6291456 | tf_op jit(solution)/shard_map/front/pallas_call | solution.py:308
  18.4 0.6 pad_add_fusion.1.place_ref
  18.9 5.1 %collective-permute-done.1.halo_b = bf16[2,128,512]{2,1,0:T(8,128)(2,1)S(1)} collective-permute-done((bf16[2,128,512]{2,1,0:T(8,128)(2,1)}, bf16[2,128,512]{2,1,0:T(8,128)(2,1)S(1)}, u32[]{:S(2)}, u32[]{:S(2)}) %collective-permute-start.1) | collective-permute-done | bytes 262176 | tf_op jit(solution)/shard_map/ppermute | solution.py:242
  24.0 3.5 %collective-permute-done.3.halo_d = bf16[2,128,512]{2,1,0:T(8,128)(2,1)S(1)} collective-permute-done((bf16[2,128,512]{2,1,0:T(8,128)(2,1)}, bf16[2,128,512]{2,1,0:T(8,128)(2,1)S(1)}, u32[]{:S(2)}, u32[]{:S(2)}) %collective-permute-start.3) | collective-permute-done | bytes 262176 | tf_op jit(solution)/shard_map/ppermute | solution.py:242
  27.6 0.7 copy-done.3
  28.3 25.8 %attend.1 = (bf16[2,128,512]{2,1,0:T(8,128)(2,1)}, bf16[2,128,512]{2,1,0:T(8,128)(2,1)}, bf16[2,128,512]{2,1,0:T(8,128)(2,1)}, bf16[2,128,512]{2,1,0:T(8,128)(2,...) custom-call(s32[32,8]{1,0:T(8,128)} %copy.12.tiles_ref, ...), custom_call_target="tpu_custom_call" | custom-call | tf_op jit(solution)/shard_map/attend/pallas_call | solution.py:321
  54.1 5.1 %weights.3 = bf16[256,2048]{1,0:T(8,128)(2,1)} custom-call(s32[2]{0:T(128)} %pad_add_fusion.1.place_ref, bf16[512,512]{1,0:T(8,128)(2,1)} %get-tuple-element.30.normed_ref, bf16[1024,512]{1,0:T(8,128)(2,1)} %get-tuple-element.31.normed_halo_ref, bf16[512,1536]{1,0:T(8,128)(2,1)} %get-tuple-element.32.gp_own_ref, ...), custom_call_target="tpu_custom_call" | custom-call | flops 671088640 | bytes 8388608 | tf_op jit(solution)/shard_map/weights/pallas_call | solution.py:347
  59.2 5.4 %weights.2 = f32[256,2048]{1,0:T(8,128)} custom-call(s32[2]{0:T(128)} %pad_add_fusion.place_ref, bf16[512,512]{1,0:T(8,128)(2,1)} %get-tuple-element.30.normed_ref, bf16[1024,512]{1,0:T(8,128)(2,1)} %get-tuple-element.31.normed_halo_ref, bf16[512,1536]{1,0:T(8,128)(2,1)} %get-tuple-element.32.gp_own_ref, bf16[1024,1024]{1,0:T(8,128)(2,1)} %get-tuple-element.33.gp_halo_ref, ...), custom_call_target="tpu_custom_call" | custom-call | flops 671088640 | bytes 8388608 | tf_op jit(solution)/shard_map/weights/pallas_call | solution.py:347
  64.6 1.9 %add_convert_fusion = bf16[256,2048]{1,0:T(8,128)(2,1)S(1)} fusion(f32[256,2048]{1,0:T(8,128)} %weights.2, bf16[256,2048]{1,0:T(8,128)(2,1)S(1)} %collective-permute-done.8), kind=kLoop, calls=%fused_computation | loop fusion | flops 1572864 | bytes 4194304 | tf_op jit(solution)/shard_map/convert_element_type | solution.py:375
  66.6 1.6 %collective-permute-start.10 = (bf16[64,2048]{1,0:T(8,128)(2,1)S(1)}, bf16[64,2048]{1,0:T(8,128)(2,1)S(1)}, u32[]{:S(2)}, u32[]{:S(2)}) collective-permute-start(bf16[64,2048]{1,0:T(8,128)(2,1)S(1)} %get-tuple-element.39), channel_id=1, source_target_pairs={{0,4},{1,5},{2,6},{3,7},{4,0},{5,1},{6,2},{7,3},{8,12},{9,13},{10,... | collective-permute-start | bytes 786440 | tf_op jit(solution)/shard_map/ppermute | solution.py:246
  68.1 1.4 %collective-permute-start.11 = (bf16[64,2048]{1,0:T(8,128)(2,1)S(1)}, bf16[64,2048]{1,0:T(8,128)(2,1)S(1)}, u32[]{:S(2)}, u32[]{:S(2)}) collective-permute-start(bf16[64,2048]{1,0:T(8,128)(2,1)S(1)} %get-tuple-element.38), channel_id=1, source_target_pairs={{0,6},{1,7},{2,4},{3,5},{4,2},{5,3},{6,0},{7,1},{8,14},{9,15},{10,... | collective-permute-start | bytes 786440 | tf_op jit(solution)/shard_map/ppermute | solution.py:246
  69.6 0.5 collective-permute-start.9
  70.1 10.9 %collective-permute-done.10 = bf16[64,2048]{1,0:T(8,128)(2,1)S(1)} collective-permute-done((bf16[64,2048]{1,0:T(8,128)(2,1)S(1)}, bf16[64,2048]{1,0:T(8,128)(2,1)S(1)}, u32[]{:S(2)}, u32[]{:S(2)}) %collective-permute-start.10) | collective-permute-done | bytes 262176 | tf_op jit(solution)/shard_map/ppermute | solution.py:246
  81.0 1.2 collective-permute-done.9
  82.4 0.7 collective-permute-start.12
  83.1 2.9 %collective-permute-start.13 = (bf16[16,2048]{1,0:T(8,128)(2,1)S(1)}, bf16[16,2048]{1,0:T(8,128)(2,1)S(1)}, u32[]{:S(2)}, u32[]{:S(2)}) collective-permute-start(bf16[16,2048]{1,0:T(8,128)(2,1)S(1)} %get-tuple-element.42), channel_id=1, source_target_pairs={{0,16},{1,17},{2,18},{3,19},{4,20},{5,21},{6,22},{7,23},{8,24},{9,... | collective-permute-start | bytes 196616 | tf_op jit(solution)/shard_map/ppermute | solution.py:246
  85.9 0.9 collective-permute-start.14
  86.8 0.5 collective-permute-done.12
  87.3 2.8 %collective-permute-done.13 = bf16[16,2048]{1,0:T(8,128)(2,1)S(1)} collective-permute-done((bf16[16,2048]{1,0:T(8,128)(2,1)S(1)}, bf16[16,2048]{1,0:T(8,128)(2,1)S(1)}, u32[]{:S(2)}, u32[]{:S(2)}) %collective-permute-start.13) | collective-permute-done | bytes 65568 | tf_op jit(solution)/shard_map/ppermute | solution.py:246
  90.1 1.9 %collective-permute-done.14 = bf16[16,2048]{1,0:T(8,128)(2,1)S(1)} collective-permute-done((bf16[16,2048]{1,0:T(8,128)(2,1)S(1)}, bf16[16,2048]{1,0:T(8,128)(2,1)S(1)}, u32[]{:S(2)}, u32[]{:S(2)}) %collective-permute-start.14) | collective-permute-done | bytes 65568 | tf_op jit(solution)/shard_map/ppermute | solution.py:246
  92.2 1.9 %collective-permute-start.16 = (bf16[16,2048]{1,0:T(8,128)(2,1)S(1)}, bf16[16,2048]{1,0:T(8,128)(2,1)S(1)}, u32[]{:S(2)}, u32[]{:S(2)}) collective-permute-start(bf16[16,2048]{1,0:T(8,128)(2,1)S(1)} %get-tuple-element.36), channel_id=1, source_target_pairs={{0,16},{1,17},{2,18},{3,19},{4,20},{5,21},{6,22},{7,23},{8,24},{9,... | collective-permute-start | bytes 196616 | tf_op jit(solution)/shard_map/ppermute | solution.py:246
  94.1 2.5 %collective-permute-start.17 = (bf16[16,2048]{1,0:T(8,128)(2,1)S(1)}, bf16[16,2048]{1,0:T(8,128)(2,1)S(1)}, u32[]{:S(2)}, u32[]{:S(2)}) collective-permute-start(bf16[16,2048]{1,0:T(8,128)(2,1)S(1)} %get-tuple-element.36), channel_id=1, source_target_pairs={{0,24},{1,25},{2,26},{3,27},{4,28},{5,29},{6,30},{7,31},{8,16},{9,... | collective-permute-start | bytes 196616 | tf_op jit(solution)/shard_map/ppermute | solution.py:246
  96.5 1.3 collective-permute-done.15
  97.9 2.3 %collective-permute-done.17 = bf16[16,2048]{1,0:T(8,128)(2,1)S(1)} collective-permute-done((bf16[16,2048]{1,0:T(8,128)(2,1)S(1)}, bf16[16,2048]{1,0:T(8,128)(2,1)S(1)}, u32[]{:S(2)}, u32[]{:S(2)}) %collective-permute-start.17) | collective-permute-done | bytes 65568 | tf_op jit(solution)/shard_map/ppermute | solution.py:246
  100.2 1.6 %collective-permute-start.18 = (bf16[64,2048]{1,0:T(8,128)(2,1)S(1)}, bf16[64,2048]{1,0:T(8,128)(2,1)S(1)}, u32[]{:S(2)}, u32[]{:S(2)}) collective-permute-start(bf16[64,2048]{1,0:T(8,128)(2,1)S(1)} %bitcast.67), channel_id=1, source_target_pairs={{0,2},{1,3},{2,0},{3,1},{4,6},{5,7},{6,4},{7,5},{8,10},{9,11},{10,... | collective-permute-start | bytes 786440 | tf_op jit(solution)/shard_map/ppermute | solution.py:246
  101.8 1.1 collective-permute-start.19
  102.9 0.9 collective-permute-start.20
  103.9 4.6 %collective-permute-done.18 = bf16[64,2048]{1,0:T(8,128)(2,1)S(1)} collective-permute-done((bf16[64,2048]{1,0:T(8,128)(2,1)S(1)}, bf16[64,2048]{1,0:T(8,128)(2,1)S(1)}, u32[]{:S(2)}, u32[]{:S(2)}) %collective-permute-start.18) | collective-permute-done | bytes 262176 | tf_op jit(solution)/shard_map/ppermute | solution.py:246
  108.5 4.0 %collective-permute-done.19 = bf16[64,2048]{1,0:T(8,128)(2,1)S(1)} collective-permute-done((bf16[64,2048]{1,0:T(8,128)(2,1)S(1)}, bf16[64,2048]{1,0:T(8,128)(2,1)S(1)}, u32[]{:S(2)}, u32[]{:S(2)}) %collective-permute-start.19) | collective-permute-done | bytes 262176 | tf_op jit(solution)/shard_map/ppermute | solution.py:246
  112.6 1.9 %collective-permute-start.4 = (bf16[2,128,512]{2,1,0:T(8,128)(2,1)}, bf16[2,128,512]{2,1,0:T(8,128)(2,1)S(1)}, u32[]{:S(2)}, u32[]{:S(2)}) collective-permute-start(bf16[2,128,512]{2,1,0:T(8,128)(2,1)} %get-tuple-element.26), channel_id=1, source_target_pairs={{0,24},{4,28},{8,0},{12,4},{16,8},{20,12},{24,16},{28,20},{1,25},{... | collective-permute-start | bytes 786440 | tf_op jit(solution)/shard_map/ppermute | solution.py:242
  114.5 0.6 collective-permute-start.5
  115.2 1.4 collective-permute-start.6
  116.6 0.4 collective-permute-start.7
  116.9 5.1 %collective-permute-done.4.back_a = bf16[2,128,512]{2,1,0:T(8,128)(2,1)S(1)} collective-permute-done((bf16[2,128,512]{2,1,0:T(8,128)(2,1)}, bf16[2,128,512]{2,1,0:T(8,128)(2,1)S(1)}, u32[]{:S(2)}, u32[]{:S(2)}) %collective-permute-start.4) | collective-permute-done | bytes 262176 | tf_op jit(solution)/shard_map/ppermute | solution.py:242
  122.1 6.7 %collective-permute-done.5.back_b = bf16[2,128,512]{2,1,0:T(8,128)(2,1)S(1)} collective-permute-done((bf16[2,128,512]{2,1,0:T(8,128)(2,1)}, bf16[2,128,512]{2,1,0:T(8,128)(2,1)S(1)}, u32[]{:S(2)}, u32[]{:S(2)}) %collective-permute-start.5) | collective-permute-done | bytes 262176 | tf_op jit(solution)/shard_map/ppermute | solution.py:242
  128.7 4.5 %collective-permute-done.7.back_d = bf16[2,128,512]{2,1,0:T(8,128)(2,1)S(1)} collective-permute-done((bf16[2,128,512]{2,1,0:T(8,128)(2,1)S(1)}, bf16[2,128,512]{2,1,0:T(8,128)(2,1)S(1)}, u32[]{:S(2)}, u32[]{:S(2)}) %collective-permute-start.7) | collective-permute-done | bytes 262176 | tf_op jit(solution)/shard_map/ppermute | solution.py:242
  133.2 0.7 copy-done.7
  133.9 3.3 %inputs.1 = bf16[512,512]{1,0:T(8,128)(2,1)} custom-call(s32[32,8]{1,0:T(8,128)} %copy.12.tiles_ref, s32[2]{0:T(128)} %pad_add_fusion.place_ref, bf16[512,512]{1,0:T(8,128)(2,1)} %bitcast.64, bf16[512,512]{1,0:T(8,128)(2,1)} %bitcast.57, f32[512,512]{1,0:T(8,128)} %get-tuple-element.25.grad_own_ref, bf16[2,128,512]{2,1,0:T(8,128)(2,1)} %copy-done.4, ...), custom_call_target="tpu_custom_call" | custom-call | flops 5242880 | bytes 4194304 | tf_op jit(solution)/shard_map/inputs/pallas_call | solution.py:382
  137.7 2.1 %slice_convert_fusion = f32[512,1536]{1,0:T(8,128)} fusion(bf16[512,2048]{1,0:T(8,128)(2,1)S(1)} %bitcast.52), kind=kLoop, calls=%fused_computation.1 | loop fusion | flops 786432 | bytes 4718592 | tf_op jit(solution)/shard_map/convert_element_type | solution.py:380
  139.7 1.1 slice_convert_fusion.1
  (43 shorter events, 1.2 us)
Async XLA Ops:
  4.7 14.2 %collective-permute-start = (bf16[2,128,512]{2,1,0:T(8,128)(2,1)}, bf16[2,128,512]{2,1,0:T(8,128)(2,1)S(1)}, u32[]{:S(2)}, u32[]{:S(2)}) collective-permute-start(bf16[2,128,512]{2,1,0:T(8,128)(2,1)} %get-tuple-element.21), channel_id=1, source_target_pairs={{0,8},{4,12},{8,16},{12,20},{16,24},{20,28},{24,0},{28,4},{1,9},{5... | collective-permute-start | bytes 786440 | tf_op jit(solution)/shard_map/ppermute | solution.py:242
  7.8 16.2 %collective-permute-start.1 = (bf16[2,128,512]{2,1,0:T(8,128)(2,1)}, bf16[2,128,512]{2,1,0:T(8,128)(2,1)S(1)}, u32[]{:S(2)}, u32[]{:S(2)}) collective-permute-start(bf16[2,128,512]{2,1,0:T(8,128)(2,1)} %get-tuple-element.22), channel_id=1, source_target_pairs={{0,4},{4,8},{8,12},{12,16},{16,20},{20,24},{24,28},{28,0},{1,5},{5... | collective-permute-start | bytes 786440 | tf_op jit(solution)/shard_map/ppermute | solution.py:242
  9.3 14.7 %collective-permute-start.2 = (bf16[2,128,512]{2,1,0:T(8,128)(2,1)}, bf16[2,128,512]{2,1,0:T(8,128)(2,1)S(1)}, u32[]{:S(2)}, u32[]{:S(2)}) collective-permute-start(bf16[2,128,512]{2,1,0:T(8,128)(2,1)} %get-tuple-element.23), channel_id=1, source_target_pairs={{0,28},{4,0},{8,4},{12,8},{16,12},{20,16},{24,20},{28,24},{1,29},{... | collective-permute-start | bytes 786440 | tf_op jit(solution)/shard_map/ppermute | solution.py:242
  12.5 15.0 %collective-permute-start.3 = (bf16[2,128,512]{2,1,0:T(8,128)(2,1)}, bf16[2,128,512]{2,1,0:T(8,128)(2,1)S(1)}, u32[]{:S(2)}, u32[]{:S(2)}) collective-permute-start(bf16[2,128,512]{2,1,0:T(8,128)(2,1)} %get-tuple-element.24), channel_id=1, source_target_pairs={{0,24},{4,28},{8,0},{12,4},{16,8},{20,12},{24,16},{28,20},{1,25},{... | collective-permute-start | bytes 786440 | tf_op jit(solution)/shard_map/ppermute | solution.py:242
  18.9 8.6 %copy-start = (bf16[2,128,512]{2,1,0:T(8,128)(2,1)}, bf16[2,128,512]{2,1,0:T(8,128)(2,1)S(1)}, u32[]{:S(2)}) copy-start(bf16[2,128,512]{2,1,0:T(8,128)(2,1)S(1)} %collective-permute-done.halo_a) | copy-start | bytes 786436
  24.0 3.6 %copy-start.1 = (bf16[2,128,512]{2,1,0:T(8,128)(2,1)}, bf16[2,128,512]{2,1,0:T(8,128)(2,1)S(1)}, u32[]{:S(2)}) copy-start(bf16[2,128,512]{2,1,0:T(8,128)(2,1)S(1)} %collective-permute-done.1.halo_b) | copy-start | bytes 786436
  24.0 3.6 %copy-start.2 = (bf16[2,128,512]{2,1,0:T(8,128)(2,1)}, bf16[2,128,512]{2,1,0:T(8,128)(2,1)S(1)}, u32[]{:S(2)}) copy-start(bf16[2,128,512]{2,1,0:T(8,128)(2,1)S(1)} %collective-permute-done.2.halo_c) | copy-start | bytes 786436
  27.6 0.7 copy-start.3
  59.2 5.4 %collective-permute-start.8 = (bf16[256,2048]{1,0:T(8,128)(2,1)}, bf16[256,2048]{1,0:T(8,128)(2,1)S(1)}, u32[]{:S(2)}, u32[]{:S(2)}) collective-permute-start(bf16[256,2048]{1,0:T(8,128)(2,1)} %weights.3), channel_id=1, source_target_pairs={{0,1},{1,0},{2,3},{3,2},{4,5},{5,4},{6,7},{7,6},{8,9},{9,8},{10,11... | collective-permute-start | bytes 3145736 | tf_op jit(solution)/shard_map/ppermute | solution.py:246
  66.6 14.4 %collective-permute-start.10 = (bf16[64,2048]{1,0:T(8,128)(2,1)S(1)}, bf16[64,2048]{1,0:T(8,128)(2,1)S(1)}, u32[]{:S(2)}, u32[]{:S(2)}) collective-permute-start(bf16[64,2048]{1,0:T(8,128)(2,1)S(1)} %get-tuple-element.39), channel_id=1, source_target_pairs={{0,4},{1,5},{2,6},{3,7},{4,0},{5,1},{6,2},{7,3},{8,12},{9,13},{10,... | collective-permute-start | bytes 786440 | tf_op jit(solution)/shard_map/ppermute | solution.py:246
  68.1 12.9 %collective-permute-start.11 = (bf16[64,2048]{1,0:T(8,128)(2,1)S(1)}, bf16[64,2048]{1,0:T(8,128)(2,1)S(1)}, u32[]{:S(2)}, u32[]{:S(2)}) collective-permute-start(bf16[64,2048]{1,0:T(8,128)(2,1)S(1)} %get-tuple-element.38), channel_id=1, source_target_pairs={{0,6},{1,7},{2,4},{3,5},{4,2},{5,3},{6,0},{7,1},{8,14},{9,15},{10,... | collective-permute-start | bytes 786440 | tf_op jit(solution)/shard_map/ppermute | solution.py:246
  69.6 12.6 %collective-permute-start.9 = (bf16[64,2048]{1,0:T(8,128)(2,1)S(1)}, bf16[64,2048]{1,0:T(8,128)(2,1)S(1)}, u32[]{:S(2)}, u32[]{:S(2)}) collective-permute-start(bf16[64,2048]{1,0:T(8,128)(2,1)S(1)} %get-tuple-element.37), channel_id=1, source_target_pairs={{0,2},{1,3},{2,0},{3,1},{4,6},{5,7},{6,4},{7,5},{8,10},{9,11},{10,... | collective-permute-start | bytes 786440 | tf_op jit(solution)/shard_map/ppermute | solution.py:246
  82.4 4.9 %collective-permute-start.12 = (bf16[16,2048]{1,0:T(8,128)(2,1)S(1)}, bf16[16,2048]{1,0:T(8,128)(2,1)S(1)}, u32[]{:S(2)}, u32[]{:S(2)}) collective-permute-start(bf16[16,2048]{1,0:T(8,128)(2,1)S(1)} %get-tuple-element.40), channel_id=1, source_target_pairs={{0,8},{1,9},{2,10},{3,11},{4,12},{5,13},{6,14},{7,15},{8,0},{9,1},... | collective-permute-start | bytes 196616 | tf_op jit(solution)/shard_map/ppermute | solution.py:246
  83.1 7.1 %collective-permute-start.13 = (bf16[16,2048]{1,0:T(8,128)(2,1)S(1)}, bf16[16,2048]{1,0:T(8,128)(2,1)S(1)}, u32[]{:S(2)}, u32[]{:S(2)}) collective-permute-start(bf16[16,2048]{1,0:T(8,128)(2,1)S(1)} %get-tuple-element.42), channel_id=1, source_target_pairs={{0,16},{1,17},{2,18},{3,19},{4,20},{5,21},{6,22},{7,23},{8,24},{9,... | collective-permute-start | bytes 196616 | tf_op jit(solution)/shard_map/ppermute | solution.py:246
  85.9 6.1 %collective-permute-start.14 = (bf16[16,2048]{1,0:T(8,128)(2,1)S(1)}, bf16[16,2048]{1,0:T(8,128)(2,1)S(1)}, u32[]{:S(2)}, u32[]{:S(2)}) collective-permute-start(bf16[16,2048]{1,0:T(8,128)(2,1)S(1)} %get-tuple-element.41), channel_id=1, source_target_pairs={{0,24},{1,25},{2,26},{3,27},{4,28},{5,29},{6,30},{7,31},{8,16},{9,... | collective-permute-start | bytes 196616 | tf_op jit(solution)/shard_map/ppermute | solution.py:246
  86.8 29.7 %copy-start.8 = (bf16[2,128,512]{2,1,0:T(8,128)(2,1)S(1)}, bf16[2,128,512]{2,1,0:T(8,128)(2,1)}, u32[]{:S(2)}) copy-start(bf16[2,128,512]{2,1,0:T(8,128)(2,1)} %get-tuple-element.29) | copy-start | bytes 786436
  92.1 5.7 %collective-permute-start.15 = (bf16[16,2048]{1,0:T(8,128)(2,1)S(1)}, bf16[16,2048]{1,0:T(8,128)(2,1)S(1)}, u32[]{:S(2)}, u32[]{:S(2)}) collective-permute-start(bf16[16,2048]{1,0:T(8,128)(2,1)S(1)} %get-tuple-element.36), channel_id=1, source_target_pairs={{0,8},{1,9},{2,10},{3,11},{4,12},{5,13},{6,14},{7,15},{8,0},{9,1},... | collective-permute-start | bytes 196616 | tf_op jit(solution)/shard_map/ppermute | solution.py:246
  92.2 5.7 %collective-permute-start.16 = (bf16[16,2048]{1,0:T(8,128)(2,1)S(1)}, bf16[16,2048]{1,0:T(8,128)(2,1)S(1)}, u32[]{:S(2)}, u32[]{:S(2)}) collective-permute-start(bf16[16,2048]{1,0:T(8,128)(2,1)S(1)} %get-tuple-element.36), channel_id=1, source_target_pairs={{0,16},{1,17},{2,18},{3,19},{4,20},{5,21},{6,22},{7,23},{8,24},{9,... | collective-permute-start | bytes 196616 | tf_op jit(solution)/shard_map/ppermute | solution.py:246
  94.1 6.1 %collective-permute-start.17 = (bf16[16,2048]{1,0:T(8,128)(2,1)S(1)}, bf16[16,2048]{1,0:T(8,128)(2,1)S(1)}, u32[]{:S(2)}, u32[]{:S(2)}) collective-permute-start(bf16[16,2048]{1,0:T(8,128)(2,1)S(1)} %get-tuple-element.36), channel_id=1, source_target_pairs={{0,24},{1,25},{2,26},{3,27},{4,28},{5,29},{6,30},{7,31},{8,16},{9,... | collective-permute-start | bytes 196616 | tf_op jit(solution)/shard_map/ppermute | solution.py:246
  100.2 8.3 %collective-permute-start.18 = (bf16[64,2048]{1,0:T(8,128)(2,1)S(1)}, bf16[64,2048]{1,0:T(8,128)(2,1)S(1)}, u32[]{:S(2)}, u32[]{:S(2)}) collective-permute-start(bf16[64,2048]{1,0:T(8,128)(2,1)S(1)} %bitcast.67), channel_id=1, source_target_pairs={{0,2},{1,3},{2,0},{3,1},{4,6},{5,7},{6,4},{7,5},{8,10},{9,11},{10,... | collective-permute-start | bytes 786440 | tf_op jit(solution)/shard_map/ppermute | solution.py:246
  101.8 10.7 %collective-permute-start.19 = (bf16[64,2048]{1,0:T(8,128)(2,1)S(1)}, bf16[64,2048]{1,0:T(8,128)(2,1)S(1)}, u32[]{:S(2)}, u32[]{:S(2)}) collective-permute-start(bf16[64,2048]{1,0:T(8,128)(2,1)S(1)} %bitcast.68), channel_id=1, source_target_pairs={{0,4},{1,5},{2,6},{3,7},{4,0},{5,1},{6,2},{7,3},{8,12},{9,13},{10,... | collective-permute-start | bytes 786440 | tf_op jit(solution)/shard_map/ppermute | solution.py:246
  102.9 9.6 %collective-permute-start.20 = (bf16[64,2048]{1,0:T(8,128)(2,1)S(1)}, bf16[64,2048]{1,0:T(8,128)(2,1)S(1)}, u32[]{:S(2)}, u32[]{:S(2)}) collective-permute-start(bf16[64,2048]{1,0:T(8,128)(2,1)S(1)} %bitcast.69), channel_id=1, source_target_pairs={{0,6},{1,7},{2,4},{3,5},{4,2},{5,3},{6,0},{7,1},{8,14},{9,15},{10,... | collective-permute-start | bytes 786440 | tf_op jit(solution)/shard_map/ppermute | solution.py:246
  112.6 25.0 %collective-permute-start.21 = (bf16[256,2048]{1,0:T(8,128)(2,1)S(1)}, bf16[256,2048]{1,0:T(8,128)(2,1)S(1)}, u32[]{:S(2)}, u32[]{:S(2)}) collective-permute-start(bf16[256,2048]{1,0:T(8,128)(2,1)S(1)} %bitcast.58), channel_id=1, source_target_pairs={{0,1},{1,0},{2,3},{3,2},{4,5},{5,4},{6,7},{7,6},{8,9},{9,8},{10,11... | collective-permute-start | bytes 3145736 | tf_op jit(solution)/shard_map/ppermute | solution.py:246
  112.6 9.4 %collective-permute-start.4 = (bf16[2,128,512]{2,1,0:T(8,128)(2,1)}, bf16[2,128,512]{2,1,0:T(8,128)(2,1)S(1)}, u32[]{:S(2)}, u32[]{:S(2)}) collective-permute-start(bf16[2,128,512]{2,1,0:T(8,128)(2,1)} %get-tuple-element.26), channel_id=1, source_target_pairs={{0,24},{4,28},{8,0},{12,4},{16,8},{20,12},{24,16},{28,20},{1,25},{... | collective-permute-start | bytes 786440 | tf_op jit(solution)/shard_map/ppermute | solution.py:242
  114.5 14.2 %collective-permute-start.5 = (bf16[2,128,512]{2,1,0:T(8,128)(2,1)}, bf16[2,128,512]{2,1,0:T(8,128)(2,1)S(1)}, u32[]{:S(2)}, u32[]{:S(2)}) collective-permute-start(bf16[2,128,512]{2,1,0:T(8,128)(2,1)} %get-tuple-element.27), channel_id=1, source_target_pairs={{0,28},{4,0},{8,4},{12,8},{16,12},{20,16},{24,20},{28,24},{1,29},{... | collective-permute-start | bytes 786440 | tf_op jit(solution)/shard_map/ppermute | solution.py:242
  115.2 13.6 %collective-permute-start.6 = (bf16[2,128,512]{2,1,0:T(8,128)(2,1)}, bf16[2,128,512]{2,1,0:T(8,128)(2,1)S(1)}, u32[]{:S(2)}, u32[]{:S(2)}) collective-permute-start(bf16[2,128,512]{2,1,0:T(8,128)(2,1)} %get-tuple-element.28), channel_id=1, source_target_pairs={{0,4},{4,8},{8,12},{12,16},{16,20},{20,24},{24,28},{28,0},{1,5},{5... | collective-permute-start | bytes 786440 | tf_op jit(solution)/shard_map/ppermute | solution.py:242
  116.6 16.7 %collective-permute-start.7 = (bf16[2,128,512]{2,1,0:T(8,128)(2,1)S(1)}, bf16[2,128,512]{2,1,0:T(8,128)(2,1)S(1)}, u32[]{:S(2)}, u32[]{:S(2)}) collective-permute-start(bf16[2,128,512]{2,1,0:T(8,128)(2,1)S(1)} %copy-done.8), channel_id=1, source_target_pairs={{0,8},{4,12},{8,16},{12,20},{16,24},{20,28},{24,0},{28,4},{1,9},{5... | collective-permute-start | bytes 786440 | tf_op jit(solution)/shard_map/ppermute | solution.py:242
  122.1 11.1 %copy-start.4 = (bf16[2,128,512]{2,1,0:T(8,128)(2,1)}, bf16[2,128,512]{2,1,0:T(8,128)(2,1)S(1)}, u32[]{:S(2)}) copy-start(bf16[2,128,512]{2,1,0:T(8,128)(2,1)S(1)} %collective-permute-done.4.back_a) | copy-start | bytes 786436
  128.7 4.5 %copy-start.5 = (bf16[2,128,512]{2,1,0:T(8,128)(2,1)}, bf16[2,128,512]{2,1,0:T(8,128)(2,1)S(1)}, u32[]{:S(2)}) copy-start(bf16[2,128,512]{2,1,0:T(8,128)(2,1)S(1)} %collective-permute-done.5.back_b) | copy-start | bytes 786436
  128.7 4.5 %copy-start.6 = (bf16[2,128,512]{2,1,0:T(8,128)(2,1)}, bf16[2,128,512]{2,1,0:T(8,128)(2,1)S(1)}, u32[]{:S(2)}) copy-start(bf16[2,128,512]{2,1,0:T(8,128)(2,1)S(1)} %collective-permute-done.6.back_c) | copy-start | bytes 786436
  133.2 0.7 copy-start.7

commit v2 on v1

v2 whole, which is shorter than its diff:
```python
from functools import partial

import jax
import jax.numpy as jnp
from jax import lax
from jax.experimental import pallas as pl
from jax.experimental.pallas import tpu as pltpu
from jax.sharding import PartitionSpec as P


HEADS = 4
TILE = 128
NB = 8
REACH = 2
CAP = 2
OFFSETS = [shift_by for shift_by in range(-REACH, REACH + 1) if shift_by != 0]
LOCAL = NB - len(OFFSETS)
SLOTS = CAP * len(OFFSETS)
MASKED = -1e30
CHUNK = 16
AXES = ("patch", "sample")

epsilon = 1e-06

VMEM = pl.BlockSpec(memory_space=pltpu.VMEM)
SMEM = pl.BlockSpec(memory_space=pltpu.SMEM)
ANY = pl.BlockSpec(memory_space=pl.ANY)


def nn(a, b):
    return jnp.dot(a, b, preferred_element_type=jnp.float32)


def nt(a, b):
    return lax.dot_general(a, b, (((1,), (1,)), ((), ())), preferred_element_type=jnp.float32)


def normalise(rows):
    inputs = rows.astype(jnp.float32)
    inverse = lax.rsqrt(jnp.mean(inputs * inputs, -1, keepdims=True) + epsilon)
    return inputs * inverse, inverse


def named_pair(tiles_ref, first_row, column, count):
    named = [tiles_ref[first_row + row, column] for row in range(count)]
    low = high = named[0]
    for entry in named[1:]:
        low = jnp.minimum(low, entry)
        high = jnp.maximum(high, entry)
    return low, high


def sent_rows(tiles_ref, position, patches, column, shift_by, tile_count):
    target = lax.rem(position - shift_by + patches, patches)
    pair = named_pair(tiles_ref, target * tile_count, LOCAL + column, tile_count)
    return [pl.multiple_of((entry - position * tile_count) * TILE, TILE) for entry in pair]


def pack_kernel(patches, tiles_ref, place_ref, features_ref, *packed_refs):
    position = place_ref[0]
    tile_count = features_ref.shape[0] // TILE
    for column, shift_by in enumerate(OFFSETS):
        rows = sent_rows(tiles_ref, position, patches, column, shift_by, tile_count)
        for slot, first in enumerate(rows):
            packed_refs[column][slot] = features_ref[pl.ds(first, TILE), :]


def front_kernel(
    features_ref,
    cotangent_ref,
    weight_qkv_ref,
    weight_out_ref,
    normed_ref,
    normed_t_ref,
    cotangent_t_ref,
    projected_ref,
    grad_ref,
):
    normed = normalise(features_ref[...])[0].astype(jnp.bfloat16)
    normed_ref[...] = normed
    normed_t_ref[...] = normed.T
    cotangent_t_ref[...] = cotangent_ref[...].T
    projected_ref[...] = nn(normed, weight_qkv_ref[...]).astype(jnp.bfloat16)
    grad_ref[...] = nt(cotangent_ref[...], weight_out_ref[...]).astype(jnp.bfloat16)


def main_kernel(
    tiles_ref,
    valid_ref,
    place_ref,
    projected_ref,
    grad_ref,
    normed_ref,
    normed_t_ref,
    cotangent_t_ref,
    halo_a,
    halo_b,
    halo_c,
    halo_d,
    weight_ref,
    back_a,
    back_b,
    back_c,
    back_d,
    dquery_ref,
    dpair_ref,
    sent_ref,
    kept_ref,
    normed_s,
    pair_s,
    score_s,
    dprob_s,
    low_s,
    dscore_s,
    dkey_s,
    dvalue_s,
    dpair_s,
    attended_s,
):
    halos = (halo_a, halo_b, halo_c, halo_d)
    backs = (back_a, back_b, back_c, back_d)
    position = place_ref[0]
    rows_local, width = grad_ref.shape
    tile_count = rows_local // TILE
    head_width = width // HEADS
    scaling = head_width ** (-0.5)
    first_row = position * tile_count
    normed_s[:rows_local, :] = normed_ref[...]
    for column, halo in enumerate(halos):
        for slot in range(CAP):
            normed = normalise(halo[slot])[0].astype(jnp.bfloat16)
            first = rows_local + (column * CAP + slot) * TILE
            normed_s[first : first + TILE, :] = normed

    lane_tile = lax.broadcasted_iota(jnp.int32, (1, TILE), 1) * 0
    biases = []
    slots = []
    for tile in range(tile_count):
        row = first_row + tile
        pieces = []
        for other in range(tile_count):
            flag = jnp.int32(0)
            for column in range(LOCAL):
                flag = flag + jnp.where(
                    tiles_ref[row, column] == first_row + other, valid_ref[row, column], 0
                )
            pieces.append(jnp.where(lane_tile + flag > 0, 0.0, MASKED))
        places = []
        for column in range(len(OFFSETS)):
            high = named_pair(tiles_ref, first_row, LOCAL + column, tile_count)[1]
            place = jnp.where(tiles_ref[row, LOCAL + column] == high, 1, 0)
            places.append(column * CAP + place)
            flag = valid_ref[row, LOCAL + column]
            pieces.append(jnp.where(lane_tile + flag > 0, 0.0, MASKED))
        biases.append(jnp.concatenate(pieces, 1))
        slots.append(places)

    def one_head(head, carry):
        lanes = pl.ds(pl.multiple_of(head * head_width, head_width), head_width)
        key_lanes = pl.ds(pl.multiple_of(width + head * head_width, head_width), head_width)
        value_lanes = pl.ds(pl.multiple_of(2 * width + head * head_width, head_width), head_width)
        both = jnp.concatenate([weight_ref[:, key_lanes], weight_ref[:, value_lanes]], 1)
        pair_s[...] = nn(normed_s[rows_local:, :], both).astype(jnp.bfloat16)
        keys = projected_ref[:, key_lanes]
        values = projected_ref[:, value_lanes]
        score_s[:, :rows_local] = nt(projected_ref[:, lanes], keys)
        dprob_s[:, :rows_local] = nt(grad_ref[:, lanes], values)
        queries_t = projected_ref[:, lanes].T
        grads_t = grad_ref[:, lanes].T
        dkey_s[...] = jnp.zeros_like(dkey_s)
        dvalue_s[...] = jnp.zeros_like(dvalue_s)

        def rows_of(tile):
            return slice(tile * TILE, (tile + 1) * TILE)

        def halo_of(tile, part):
            starts = [pl.multiple_of(place * TILE, TILE) for place in slots[tile]]
            return jnp.concatenate([pair_s[pl.ds(start, TILE), part] for start in starts], 0)

        key_part, value_part = slice(0, head_width), slice(head_width, 2 * head_width)

        def products(tile):
            rows = rows_of(tile)
            score_s[rows, rows_local:] = nt(projected_ref[rows, lanes], halo_of(tile, key_part))
            dprob_s[rows, rows_local:] = nt(grad_ref[rows, lanes], halo_of(tile, value_part))

        def softmax(tile):
            chunks = [
                slice(first, first + CHUNK) for first in range(tile * TILE, (tile + 1) * TILE, CHUNK)
            ]
            highest = [
                jnp.max(score_s[chunk, :] * scaling + biases[tile], -1, keepdims=True)
                for chunk in chunks
            ]
            stats = []
            for chunk, high in zip(chunks, highest):
                expanded = jnp.exp(score_s[chunk, :] * scaling + (biases[tile] - high))
                score_s[chunk, :] = expanded
                over = 1.0 / jnp.sum(expanded, -1, keepdims=True)
                centre = jnp.sum(expanded * dprob_s[chunk, :], -1, keepdims=True) * over
                stats.append((over, centre))
            for chunk, (over, centre) in zip(chunks, stats):
                attention = score_s[chunk, :] * over
                low_s[chunk, :] = attention.astype(jnp.bfloat16)
                dscore = attention * (dprob_s[chunk, :] - centre)
                dscore_s[chunk, :] = dscore.astype(jnp.bfloat16)

        def finish(tile):
            rows = rows_of(tile)
            attended = nn(low_s[rows, :], jnp.concatenate([values, halo_of(tile, value_part)], 0))
            attended_s[rows, lanes] = attended.astype(jnp.bfloat16)
            key_all = jnp.concatenate([keys, halo_of(tile, key_part)], 0)
            dquery = nn(dscore_s[rows, :], key_all) * scaling
            dquery_ref[rows, lanes] = dquery.astype(jnp.bfloat16)
            dkey_t = nn(queries_t[:, rows], dscore_s[rows, rows_local:])
            dvalue_t = nn(grads_t[:, rows], low_s[rows, rows_local:])
            for column, place in enumerate(slots[tile]):
                part = slice(column * TILE, (column + 1) * TILE)
                dkey_s[place] += dkey_t[:, part]
                dvalue_s[place] += dvalue_t[:, part]

        products(0)
        for tile in range(tile_count):
            if tile + 1 < tile_count:
                products(tile + 1)
            if tile > 0:
                finish(tile - 1)
            softmax(tile)
        finish(tile_count - 1)
        low = jnp.bfloat16
        key_rows = lanes
        value_rows = key_lanes
        dpair_s[key_rows, :rows_local] = (nn(queries_t, dscore_s[:, :rows_local]) * scaling).astype(low)
        dpair_s[value_rows, :rows_local] = nn(grads_t, low_s[:, :rows_local]).astype(low)
        for place in range(SLOTS):
            part = slice(rows_local + place * TILE, rows_local + (place + 1) * TILE)
            dpair_s[key_rows, part] = (dkey_s[place] * scaling).astype(low)
            dpair_s[value_rows, part] = dvalue_s[place].astype(low)
        return carry

    lax.fori_loop(0, HEADS, one_head, 0)
    blocks = width // TILE
    side = place_ref[1]
    for out_ref, half in ((sent_ref, 1 - side), (kept_ref, side)):
        first = pl.multiple_of(half * width, width)
        pairs = nn(dpair_s[pl.ds(first, width), :], normed_s[...])
        store_blocks(out_ref, 0, pairs, blocks)

        @pl.when(half == 0)
        def _():
            store_blocks(out_ref, TILE, nn(normed_t_ref[...], dquery_ref[...]), blocks)

        @pl.when(half != 0)
        def _():
            store_blocks(out_ref, TILE, nn(cotangent_t_ref[...], attended_s[...]), blocks, True)

    for column, back in enumerate(backs):
        first = rows_local + column * CAP * TILE
        part = nn(weight_ref[:, width:], dpair_s[:, first : first + CAP * TILE])
        back[...] = part.astype(jnp.bfloat16).T.reshape(back.shape)
    dpair_ref[...] = dpair_s[:, :rows_local]


def store_blocks(out_ref, first, value, blocks, across=False):
    for row in range(blocks):
        for column in range(blocks):
            block = value[row * TILE : (row + 1) * TILE, column * TILE : (column + 1) * TILE]
            place = column * blocks + row if across else row * blocks + column
            start = place * 2 * TILE + first
            out_ref[start : start + TILE, :] = block.astype(out_ref.dtype)


def output_kernel(flip, place_ref, gathered_ref, *refs):
    qkv_ref, out_ref, pair_s, other_s, sems = refs[-5:]
    width = out_ref.shape[0]
    blocks = width // TILE
    half = place_ref[1] ^ flip
    first = pl.multiple_of((half + 1) * width, width)

    def spot(index):
        return slice(index * TILE, (index + 1) * TILE)

    def strips(row):
        start = pl.multiple_of(first + row * TILE, TILE)
        pair = pltpu.make_async_copy(
            pair_s.at[row], qkv_ref.at[:, pl.ds(start, TILE)], sems.at[row]
        )
        own, sem = other_s.at[row], sems.at[blocks + row]
        left = pltpu.make_async_copy(own, qkv_ref.at[spot(row), :width], sem)
        right = pltpu.make_async_copy(own, out_ref.at[spot(row), :], sem)
        return pair, left, right

    for row in range(blocks):
        pair, left, right = strips(row)
        for column in range(blocks):
            chunk = 2 * (row * blocks + column)
            pair_s[row, spot(column), :] = gathered_ref[spot(chunk), :].astype(jnp.float32)
            other_s[row, :, spot(column)] = gathered_ref[spot(chunk + 1), :].astype(jnp.float32)
        pair.start()
        pl.when(half == 0)(left.start)
        pl.when(half != 0)(right.start)
    for row in range(blocks):
        pair, left, right = strips(row)
        pair.wait()
        pl.when(half == 0)(left.wait)
        pl.when(half != 0)(right.wait)


def input_kernel(
    patches,
    tiles_ref,
    place_ref,
    features_ref,
    cotangent_ref,
    dquery_ref,
    dpair_ref,
    weight_ref,
    back_a,
    back_b,
    back_c,
    back_d,
    out_ref,
    total_s,
):
    position = place_ref[0]
    width = features_ref.shape[1]
    tile_count = features_ref.shape[0] // TILE
    pairs = nn(weight_ref[:, width:], dpair_ref[...])
    total_s[...] = nt(dquery_ref[...], weight_ref[:, :width]) + pairs.T
    for column, (shift_by, back) in enumerate(zip(OFFSETS, (back_a, back_b, back_c, back_d))):
        rows = sent_rows(tiles_ref, position, patches, column, shift_by, tile_count)
        for slot, first in enumerate(rows):
            total_s[pl.ds(first, TILE), :] += back[slot].astype(jnp.float32)
    normed, inverse = normalise(features_ref[...])
    total = total_s[...]
    centred = total - normed * jnp.mean(total * normed, -1, keepdims=True)
    out_ref[...] = (cotangent_ref[...].astype(jnp.float32) + inverse * centred).astype(out_ref.dtype)


def from_behind(value, steps):
    count = lax.axis_size("patch")
    pairs = [(source, (source + steps) % count) for source in range(count)]
    return lax.ppermute(value, "patch", pairs)


def exchange(value, flip, count):
    return lax.ppermute(value, AXES, [(source, source ^ flip) for source in range(count)])


def flips_of(bits):
    return [
        sum(((step >> place) & 1) << bit for place, bit in enumerate(bits))
        for step in range(1 << len(bits))
    ]


def digit_of(index, bits):
    return sum(((index >> bit) & 1) << place for place, bit in enumerate(bits))


def reduce_phase(value, index, bits, count):
    flips = flips_of(bits)
    digit = digit_of(index, bits)
    pieces = value.reshape(len(flips), value.shape[0] // len(flips), value.shape[1])
    received = [
        exchange(lax.dynamic_index_in_dim(pieces, digit ^ step, 0, False), flips[step], count)
        for step in range(1, len(flips))
    ]
    total = lax.dynamic_index_in_dim(pieces, digit, 0, False).astype(jnp.float32)
    for piece in received:
        total = total + piece.astype(jnp.float32)
    return total


def gather_phase(value, index, bits, count):
    flips = flips_of(bits)
    digit = digit_of(index, bits)
    pieces = [value]
    for flip in flips[1:]:
        pieces.append(exchange(value, flip, count))
    stacked = jnp.zeros((len(flips),) + value.shape, value.dtype)
    for step, piece in enumerate(pieces):
        stacked = lax.dynamic_update_index_in_dim(stacked, piece, digit ^ step, 0)
    return stacked.reshape(len(flips) * value.shape[0], value.shape[1])


def first_chunk(index, phases, chunks):
    spread, start = chunks, 0
    for bits in [[0]] + phases:
        spread = spread >> len(bits)
        start = start + digit_of(index, bits) * spread
    return start


def turned(value, first, chunks):
    pairs = value.reshape(-1, 2, TILE, TILE)
    flipped = jnp.swapaxes(pairs, 2, 3)
    chunk = first + jnp.arange(pairs.shape[0], dtype=jnp.int32)
    second = jnp.where((chunk < chunks // 2)[:, None, None], pairs[:, 1], flipped[:, 1])
    return jnp.stack([flipped[:, 0], second], 1).reshape(value.shape)


def on_device(features, cotangent, weight_qkv, weight_out, key_tiles, tile_valid):
    patches = lax.axis_size("patch")
    samples = lax.axis_size("sample")
    count = patches * samples
    position = lax.axis_index("patch").astype(jnp.int32)
    index = position * samples + lax.axis_index("sample").astype(jnp.int32)
    rows_local, width = features.shape[1:]
    rows = features[0]
    grad_rows = cotangent[0]
    low = jnp.bfloat16

    def shape(*dims, kind=low):
        return jax.ShapeDtypeStruct(dims, kind)

    def params(mebibytes):
        return pltpu.CompilerParams(vmem_limit_bytes=mebibytes << 20)

    place = jnp.stack([position, index & 1])
    packed = pl.pallas_call(
        partial(pack_kernel, patches),
        out_shape=[shape(CAP, TILE, width)] * len(OFFSETS),
        in_specs=[SMEM, SMEM, VMEM],
        out_specs=[VMEM] * len(OFFSETS),
        compiler_params=params(60),
        name="pack",
    )(key_tiles, place, rows)
    halos = [from_behind(piece, -shift_by) for piece, shift_by in zip(packed, OFFSETS)]
    square = shape(rows_local, width)
    normed_low, normed_t, cotangent_t, projected, grad_attended = pl.pallas_call(
        front_kernel,
        out_shape=[
            square,
            shape(width, rows_local),
            shape(width, rows_local),
            shape(rows_local, 3 * width),
            square,
        ],
        in_specs=[VMEM] * 4,
        out_specs=[VMEM] * 5,
        compiler_params=params(60),
        cost_estimate=pl.CostEstimate(
            flops=8 * rows_local * width * width, bytes_accessed=6 << 20, transcendentals=0
        ),
        name="front",
    )(rows, grad_rows, weight_qkv, weight_out)
    halo_rows = SLOTS * TILE
    all_rows = rows_local + halo_rows
    keys_seen = rows_local + len(OFFSETS) * TILE
    head_width = width // HEADS
    side = index & 1
    block_rows = 4 * width * width // TILE
    outs = pl.pallas_call(
        main_kernel,
        out_shape=[shape(CAP, TILE, width)] * len(OFFSETS)
        + [
            square,
            shape(2 * width, rows_local),
            shape(block_rows // 2, TILE),
            shape(block_rows // 2, TILE),
        ],
        in_specs=[SMEM] * 3 + [VMEM] * 10,
        out_specs=[VMEM] * (len(OFFSETS) + 4),
        scratch_shapes=[
            pltpu.VMEM((all_rows, width), low),
            pltpu.VMEM((halo_rows, 2 * head_width), low),
            pltpu.VMEM((rows_local, keys_seen), jnp.float32),
            pltpu.VMEM((rows_local, keys_seen), jnp.float32),
            pltpu.VMEM((rows_local, keys_seen), low),
            pltpu.VMEM((rows_local, keys_seen), low),
            pltpu.VMEM((SLOTS, head_width, TILE), jnp.float32),
            pltpu.VMEM((SLOTS, head_width, TILE), jnp.float32),
            pltpu.VMEM((2 * width, all_rows), low),
            pltpu.VMEM((rows_local, width), low),
        ],
        compiler_params=params(60),
        name="attend",
    )(
        key_tiles,
        tile_valid,
        place,
        projected,
        grad_attended,
        normed_low,
        normed_t,
        cotangent_t,
        *halos,
        weight_qkv,
    )
    backs, (dquery, dpair, sent, kept) = outs[:4], outs[4:]
    far = [column for column, shift_by in enumerate(OFFSETS) if abs(shift_by) == REACH]
    near = [column for column in range(len(OFFSETS)) if column not in far]
    backs = list(backs)
    returned = {}
    for column in far:
        returned[column] = from_behind(backs[column], OFFSETS[column])
    arrived = exchange(sent, 1, count)
    total = kept.astype(jnp.float32) + arrived.astype(jnp.float32)
    bit_count = count.bit_length() - 1
    phases = [list(range(bit, min(bit + 2, bit_count))) for bit in range(1, bit_count, 2)]
    for turn, bits in enumerate(phases):
        total = reduce_phase(total.astype(low), index, bits, count)
        if turn == 0:
            total, waiting = lax.optimization_barrier((total, [backs[column] for column in near]))
            for column, piece in zip(near, waiting):
                returned[column] = from_behind(piece, OFFSETS[column])
    factor = float(count * rows_local) ** (-0.5)
    total = total * factor
    chunks = block_rows // (2 * TILE)
    whole_chunks = total.shape[0] % (2 * TILE) == 0
    if whole_chunks:
        total = turned(total, first_chunk(index, phases, chunks), chunks)
    gathered = total.astype(low)
    grad_features = None
    for turn, bits in enumerate(phases[::-1]):
        if turn == 1:
            gathered, held = lax.optimization_barrier(
                (gathered, [returned[column] for column in range(len(OFFSETS))])
            )
            grad_features = pl.pallas_call(
                partial(input_kernel, patches),
                out_shape=square,
                in_specs=[SMEM, SMEM] + [VMEM] * 9,
                out_specs=VMEM,
                scratch_shapes=[pltpu.VMEM((rows_local, width), jnp.float32)],
                compiler_params=params(60),
                cost_estimate=pl.CostEstimate(
                    flops=6 * rows_local * width * width, bytes_accessed=6 << 20, transcendentals=0
                ),
                name="inputs",
            )(key_tiles, place, rows, grad_rows, dquery, dpair, weight_qkv, *held)
        gathered = gather_phase(gathered, index, bits, count)
    other = exchange(gathered, 1, count)
    if not whole_chunks:
        gathered = turned(gathered, side * (chunks // 2), chunks)
        other = turned(other, (1 - side) * (chunks // 2), chunks)

    def outputs(flip, half, *started):
        return pl.pallas_call(
            partial(output_kernel, flip),
            out_shape=[
                shape(width, 3 * width, kind=jnp.float32),
                shape(width, width, kind=jnp.float32),
            ],
            in_specs=[SMEM, VMEM] + [ANY] * len(started),
            out_specs=[ANY] * 2,
            scratch_shapes=[
                pltpu.VMEM((width // TILE, width, TILE), jnp.float32),
                pltpu.VMEM((width // TILE, TILE, width), jnp.float32),
                pltpu.SemaphoreType.DMA((2 * width // TILE,)),
            ],
            input_output_aliases={2: 0, 3: 1} if started else {},
            compiler_params=params(10),
            cost_estimate=pl.CostEstimate(flops=0, bytes_accessed=4 << 20, transcendentals=0),
            name="outputs",
        )(place, half, *started)

    started = outputs(0, gathered)
    grad_qkv, grad_out = outputs(1, other, *started)
    return (grad_features[None], grad_qkv, grad_out)


def solution(mesh):
    placed = (P("sample", "patch", None), P("sample", "patch", None), P(), P(), P(), P())
    return jax.shard_map(
        on_device,
        mesh=mesh,
        in_specs=placed,
        out_specs=(P("sample", "patch", None), P(), P()),
        check_vma=False,
    )
```

time: 141 us -> 131 us (0.929)
  Pallas kernels: 45.9 us -> 38.9 us
  other arithmetic: 6.39 us -> 2.26 us
    ppermute x14, waiting for transfers between devices: 29.4 us -> 46.6 us  [exchange(): lax.ppermute(value, AXES, [(source, source ^ flip) for source in range(co...]
    ppermute x8, waiting for transfers between devices: 24.9 us -> 8.83 us  [from_behind(): return lax.ppermute(value, 'patch', pairs)]
    pallas_call x4, Pallas kernels: 18 us -> 13.2 us  [the longest x1 4.75 us: on_device(): pl.pallas_call(partial(input_kernel, patches), out_shape=square, in_specs...]
    convert_element_type x2 -> x1, other arithmetic: 3.14 us -> 0.01 us  [on_device(): gathered = total.astype(low)]
    ppermute x8, starting transfers between devices: 12.4 us -> 14.8 us  [from_behind(): return lax.ppermute(value, 'patch', pairs)]
    pallas_call x1, Pallas kernels: 25.8 us -> 23.6 us  [on_device(): pl.pallas_call(main_kernel, out_shape=[shape(CAP, TILE, width)] * len(OFF...]
    ppermute x14, starting transfers between devices: 16.1 us -> 14.6 us  [exchange(): lax.ppermute(value, AXES, [(source, source ^ flip) for source in range(co...]
    unnamed x20 -> x26, local copies, waits for them, and re-layouts: 4.12 us -> 3.46 us
  transfers between devices with their start and end apart: 22 -> 22, of which waited for: 14 -> 11; matrix products, arithmetic and copies ran while one was open for 2% -> 1% of each run, Pallas kernels for 9% -> 9%
where the time goes in v2:
time: 131 us
  waiting for transfers between devices  55.4 us (42%)
  Pallas kernels  38.9 us (30%)
  starting transfers between devices  29.4 us (22%)
  local copies, waits for them, and re-layouts  4.05 us (3%)
  other arithmetic  2.26 us (2%)
    ppermute x14, waiting for transfers between devices, exchange(): lax.ppermute(value, AXES, [(source, source ^ flip) for source in range(co...  46.6 us
    pallas_call x1, Pallas kernels, on_device(): pl.pallas_call(main_kernel, out_shape=[shape(CAP, TILE, width)] * len(OFF...  23.6 us
    ppermute x8, starting transfers between devices, from_behind(): return lax.ppermute(value, 'patch', pairs)  14.8 us
    ppermute x14, starting transfers between devices, exchange(): lax.ppermute(value, AXES, [(source, source ^ flip) for source in range(co...  14.6 us
    ppermute x8, waiting for transfers between devices, from_behind(): return lax.ppermute(value, 'patch', pairs)  8.83 us
    pallas_call x1, Pallas kernels, on_device(): pl.pallas_call(partial(input_kernel, patches), out_shape=square, in_specs...  4.75 us
    pallas_call x1, Pallas kernels, on_device(): pl.pallas_call(front_kernel, out_shape=[square, shape(width, rows_local),...  4.57 us
    pallas_call x2, Pallas kernels, outputs(): pl.pallas_call(partial(output_kernel, flip), out_shape=[shape(width, 3 *...  3.87 us
  transfers between devices with their start and end apart: 22, of which 11 were waited for; matrix products, arithmetic and copies ran while one was open for 1% of the time, Pallas kernels for 9%

profile of v2, /device:TPU:0, one launch (start us, length us, event | category | flops | bytes accessed | tf_op | source)
XLA Modules:
  0.0 131.2 jit_solution(6102768732430873461)
XLA Ops:
  0.6 1.4 %copy.15.tiles_ref = s32[32,8]{1,0:T(8,128)} copy(s32[32,8]{0,1:T(8,128)} %param.10) | data formatting | bytes 2048 | tf_op args[4]
  2.0 0.6 pad_add_fusion.place_ref
  2.5 2.1 %pack.1 = (bf16[2,128,512]{2,1,0:T(8,128)(2,1)}, bf16[2,128,512]{2,1,0:T(8,128)(2,1)}, bf16[2,128,512]{2,1,0:T(8,128)(2,1)}, bf16[2,128,512]{2,1,0:T(8,128)(2,1)}) custom-call(s32[32,8]{1,0:T(8,128)} %copy.15.tiles_ref, s32[2]{0:T(128)} %pad_add_fusion.place_ref, bf16[512,512]{1,0:T(8,128)(2,1)} %bitcast.49), custom_call_target="tpu_custom_call" | custom-call | tf_op jit(solution)/shard_map/pack/pallas_call | solution.py:421
  4.6 3.1 %collective-permute-start = (bf16[2,128,512]{2,1,0:T(8,128)(2,1)}, bf16[2,128,512]{2,1,0:T(8,128)(2,1)S(1)}, u32[]{:S(2)}, u32[]{:S(2)}) collective-permute-start(bf16[2,128,512]{2,1,0:T(8,128)(2,1)} %get-tuple-element.37), channel_id=1, source_target_pairs={{0,8},{4,12},{8,16},{12,20},{16,24},{20,28},{24,0},{28,4},{1,9},{5... | collective-permute-start | bytes 786440 | tf_op jit(solution)/shard_map/ppermute | solution.py:343
  7.7 1.5 %collective-permute-start.1 = (bf16[2,128,512]{2,1,0:T(8,128)(2,1)}, bf16[2,128,512]{2,1,0:T(8,128)(2,1)S(1)}, u32[]{:S(2)}, u32[]{:S(2)}) collective-permute-start(bf16[2,128,512]{2,1,0:T(8,128)(2,1)} %get-tuple-element.38), channel_id=1, source_target_pairs={{0,4},{4,8},{8,12},{12,16},{16,20},{20,24},{24,28},{28,0},{1,5},{5... | collective-permute-start | bytes 786440 | tf_op jit(solution)/shard_map/ppermute | solution.py:343
  9.2 3.2 %collective-permute-start.2 = (bf16[2,128,512]{2,1,0:T(8,128)(2,1)}, bf16[2,128,512]{2,1,0:T(8,128)(2,1)S(1)}, u32[]{:S(2)}, u32[]{:S(2)}) collective-permute-start(bf16[2,128,512]{2,1,0:T(8,128)(2,1)} %get-tuple-element.39), channel_id=1, source_target_pairs={{0,28},{4,0},{8,4},{12,8},{16,12},{20,16},{24,20},{28,24},{1,29},{... | collective-permute-start | bytes 786440 | tf_op jit(solution)/shard_map/ppermute | solution.py:343
  12.4 0.3 collective-permute-start.3
  12.7 1.4 %copy.13.valid_ref = s32[32,8]{1,0:T(8,128)} copy(s32[32,8]{0,1:T(8,128)} %param.11) | data formatting | bytes 2048 | tf_op args[5]
  14.1 4.6 %front.1 = (bf16[512,512]{1,0:T(8,128)(2,1)}, bf16[512,512]{1,0:T(8,128)(2,1)}, bf16[512,512]{1,0:T(8,128)(2,1)}, bf16[512,1536]{1,0:T(8,128)(2,1)}, bf16[512,512]{1,0:T(8,128)(2,1)}) custom-call(bf16[512,512]{1,0:T(8,128)(2,1)} %bitcast.50, bf16[512,512]{1,0:T(8,128)(2,1)} %bitcast.58, bf16[512,1536]{1,0:T(8,128)(2,1)} %weight_ref.3, ...), custom_call_target="tpu_custom_call" | custom-call | flops 1073741824 | bytes 6291456 | tf_op jit(solution)/shard_map/front/pallas_call | solution.py:431
  18.6 0.0 collective-permute-done.halo_a
  18.7 5.3 %collective-permute-done.1.halo_b = bf16[2,128,512]{2,1,0:T(8,128)(2,1)S(1)} collective-permute-done((bf16[2,128,512]{2,1,0:T(8,128)(2,1)}, bf16[2,128,512]{2,1,0:T(8,128)(2,1)S(1)}, u32[]{:S(2)}, u32[]{:S(2)}) %collective-permute-start.1) | collective-permute-done | bytes 262176 | tf_op jit(solution)/shard_map/ppermute | solution.py:343
  23.9 3.5 %collective-permute-done.3.halo_d = bf16[2,128,512]{2,1,0:T(8,128)(2,1)S(1)} collective-permute-done((bf16[2,128,512]{2,1,0:T(8,128)(2,1)}, bf16[2,128,512]{2,1,0:T(8,128)(2,1)S(1)}, u32[]{:S(2)}, u32[]{:S(2)}) %collective-permute-start.3) | collective-permute-done | bytes 262176 | tf_op jit(solution)/shard_map/ppermute | solution.py:343
  27.5 0.7 copy-done.8
  28.2 23.6 %attend.1 = (bf16[2,128,512]{2,1,0:T(8,128)(2,1)}, bf16[2,128,512]{2,1,0:T(8,128)(2,1)}, bf16[2,128,512]{2,1,0:T(8,128)(2,1)}, bf16[2,128,512]{2,1,0:T(8,128)(2,...) custom-call(s32[32,8]{1,0:T(8,128)} %copy.15.tiles_ref, ...), custom_call_target="tpu_custom_call" | custom-call | tf_op jit(solution)/shard_map/attend/pallas_call | solution.py:454
  51.8 0.1 collective-permute-start.4
  51.9 2.8 %collective-permute-done.4 = bf16[4096,128]{1,0:T(8,128)(2,1)S(1)} collective-permute-done((bf16[4096,128]{1,0:T(8,128)(2,1)}, bf16[4096,128]{1,0:T(8,128)(2,1)S(1)}, u32[]{:S(2)}, u32[]{:S(2)}) %collective-permute-start.4) | collective-permute-done | bytes 1048608 | tf_op jit(solution)/shard_map/ppermute | solution.py:347
  54.7 1.5 %add_convert_fusion = bf16[4096,128]{1,0:T(8,128)(2,1)S(1)} fusion(bf16[4096,128]{1,0:T(8,128)(2,1)S(1)} %collective-permute-done.4, bf16[4096,128]{1,0:T(8,128)(2,1)} %get-tuple-element.43), kind=kLoop, calls=%fused_computation | loop fusion | flops 2097152 | bytes 3145728 | tf_op jit(solution)/shard_map/convert_element_type | solution.py:503
  56.3 0.1 dynamic-slice_bitcast_fusion.2
  56.3 2.5 %collective-permute-start.7 = (bf16[1024,128]{1,0:T(8,128)(2,1)S(1)}, bf16[1024,128]{1,0:T(8,128)(2,1)S(1)}, u32[]{:S(2)}, u32[]{:S(2)}) collective-permute-start(bf16[1024,128]{1,0:T(8,128)(2,1)S(1)} %get-tuple-element.62), channel_id=1, source_target_pairs={{0,6},{1,7},{2,4},{3,5},{4,2},{5,3},{6,0},{7,1},{8,14},{9,15},{10,... | collective-permute-start | bytes 786440 | tf_op jit(solution)/shard_map/ppermute | solution.py:347
  58.8 0.5 collective-permute-start.6
  59.3 0.5 collective-permute-start.5
  59.9 6.6 %collective-permute-done.7 = bf16[1024,128]{1,0:T(8,128)(2,1)S(1)} collective-permute-done((bf16[1024,128]{1,0:T(8,128)(2,1)S(1)}, bf16[1024,128]{1,0:T(8,128)(2,1)S(1)}, u32[]{:S(2)}, u32[]{:S(2)}) %collective-permute-start.7) | collective-permute-done | bytes 262176 | tf_op jit(solution)/shard_map/ppermute | solution.py:347
  66.5 4.7 %collective-permute-done.6 = bf16[1024,128]{1,0:T(8,128)(2,1)S(1)} collective-permute-done((bf16[1024,128]{1,0:T(8,128)(2,1)S(1)}, bf16[1024,128]{1,0:T(8,128)(2,1)S(1)}, u32[]{:S(2)}, u32[]{:S(2)}) %collective-permute-start.6) | collective-permute-done | bytes 262176 | tf_op jit(solution)/shard_map/ppermute | solution.py:347
  71.3 0.1 collective-permute-done.5
  71.3 0.1 fusion.1
  71.5 2.9 %collective-permute-start.10 = (bf16[256,128]{1,0:T(8,128)(2,1)S(1)}, bf16[256,128]{1,0:T(8,128)(2,1)S(1)}, u32[]{:S(2)}, u32[]{:S(2)}) collective-permute-start(bf16[256,128]{1,0:T(8,128)(2,1)S(1)} %get-tuple-element.65), channel_id=1, source_target_pairs={{0,24},{1,25},{2,26},{3,27},{4,28},{5,29},{6,30},{7,31},{8,16},{9,... | collective-permute-start | bytes 196616 | tf_op jit(solution)/shard_map/ppermute | solution.py:347
  74.4 1.5 %collective-permute-start.8 = (bf16[256,128]{1,0:T(8,128)(2,1)S(1)}, bf16[256,128]{1,0:T(8,128)(2,1)S(1)}, u32[]{:S(2)}, u32[]{:S(2)}) collective-permute-start(bf16[256,128]{1,0:T(8,128)(2,1)S(1)} %get-tuple-element.64), channel_id=1, source_target_pairs={{0,8},{1,9},{2,10},{3,11},{4,12},{5,13},{6,14},{7,15},{8,0},{9,1},... | collective-permute-start | bytes 196616 | tf_op jit(solution)/shard_map/ppermute | solution.py:347
  76.0 2.9 %collective-permute-start.14 = (bf16[2,128,512]{2,1,0:T(8,128)(2,1)}, bf16[2,128,512]{2,1,0:T(8,128)(2,1)S(1)}, u32[]{:S(2)}, u32[]{:S(2)}) collective-permute-start(bf16[2,128,512]{2,1,0:T(8,128)(2,1)} %get-tuple-element.48), channel_id=1, source_target_pairs={{0,24},{4,28},{8,0},{12,4},{16,8},{20,12},{24,16},{28,20},{1,25},{... | collective-permute-start | bytes 786440 | tf_op jit(solution)/shard_map/ppermute | solution.py:343
  78.9 3.9 %collective-permute-start.15 = (bf16[2,128,512]{2,1,0:T(8,128)(2,1)S(1)}, bf16[2,128,512]{2,1,0:T(8,128)(2,1)S(1)}, u32[]{:S(2)}, u32[]{:S(2)}) collective-permute-start(bf16[2,128,512]{2,1,0:T(8,128)(2,1)S(1)} %copy-done.10), channel_id=1, source_target_pairs={{0,28},{4,0},{8,4},{12,8},{16,12},{20,16},{24,20},{28,24},{1,29},{... | collective-permute-start | bytes 786440 | tf_op jit(solution)/shard_map/ppermute | solution.py:343
  82.7 0.0 collective-permute-start.16
  82.8 0.1 copy.14
  82.9 0.1 collective-permute-start.11
  83.1 15.4 %collective-permute-done.11 = bf16[256,128]{1,0:T(8,128)(2,1)S(1)} collective-permute-done((bf16[256,128]{1,0:T(8,128)(2,1)S(1)}, bf16[256,128]{1,0:T(8,128)(2,1)S(1)}, u32[]{:S(2)}, u32[]{:S(2)}) %collective-permute-start.11) | collective-permute-done | bytes 65568 | tf_op jit(solution)/shard_map/ppermute | solution.py:347
  98.5 0.6 collective-permute-start.12
  99.2 5.2 %collective-permute-done.12 = bf16[256,128]{1,0:T(8,128)(2,1)S(1)} collective-permute-done((bf16[256,128]{1,0:T(8,128)(2,1)S(1)}, bf16[256,128]{1,0:T(8,128)(2,1)S(1)}, u32[]{:S(2)}, u32[]{:S(2)}) %collective-permute-start.12) | collective-permute-done | bytes 65568 | tf_op jit(solution)/shard_map/ppermute | solution.py:347
  104.4 2.2 %collective-permute-start.13 = (bf16[256,128]{1,0:T(8,128)(2,1)S(1)}, bf16[256,128]{1,0:T(8,128)(2,1)S(1)}, u32[]{:S(2)}, u32[]{:S(2)}) collective-permute-start(bf16[256,128]{1,0:T(8,128)(2,1)S(1)} %bitcast.66), channel_id=1, source_target_pairs={{0,24},{1,25},{2,26},{3,27},{4,28},{5,29},{6,30},{7,31},{8,16},{9,... | collective-permute-start | bytes 196616 | tf_op jit(solution)/shard_map/ppermute | solution.py:347
  106.6 3.9 %collective-permute-done.13 = bf16[256,128]{1,0:T(8,128)(2,1)S(1)} collective-permute-done((bf16[256,128]{1,0:T(8,128)(2,1)S(1)}, bf16[256,128]{1,0:T(8,128)(2,1)S(1)}, u32[]{:S(2)}, u32[]{:S(2)}) %collective-permute-start.13) | collective-permute-done | bytes 65568 | tf_op jit(solution)/shard_map/ppermute | solution.py:347
  110.5 0.0 copy-start.1
  110.6 0.8 collective-permute-start.18
  111.4 1.0 collective-permute-start.19
  112.4 1.7 %collective-permute-start.20 = (bf16[1024,128]{1,0:T(8,128)(2,1)S(1)}, bf16[1024,128]{1,0:T(8,128)(2,1)S(1)}, u32[]{:S(2)}, u32[]{:S(2)}) collective-permute-start(bf16[1024,128]{1,0:T(8,128)(2,1)S(1)} %bitcast.56), channel_id=1, source_target_pairs={{0,6},{1,7},{2,4},{3,5},{4,2},{5,3},{6,0},{7,1},{8,14},{9,15},{10,... | collective-permute-start | bytes 786440 | tf_op jit(solution)/shard_map/ppermute | solution.py:347
  114.1 0.1 broadcast_in_dim.48
  114.3 4.3 %collective-permute-done.18 = bf16[1024,128]{1,0:T(8,128)(2,1)S(1)} collective-permute-done((bf16[1024,128]{1,0:T(8,128)(2,1)S(1)}, bf16[1024,128]{1,0:T(8,128)(2,1)S(1)}, u32[]{:S(2)}, u32[]{:S(2)}) %collective-permute-start.18) | collective-permute-done | bytes 262176 | tf_op jit(solution)/shard_map/ppermute | solution.py:347
  118.7 3.5 %collective-permute-done.19 = bf16[1024,128]{1,0:T(8,128)(2,1)S(1)} collective-permute-done((bf16[1024,128]{1,0:T(8,128)(2,1)S(1)}, bf16[1024,128]{1,0:T(8,128)(2,1)S(1)}, u32[]{:S(2)}, u32[]{:S(2)}) %collective-permute-start.19) | collective-permute-done | bytes 262176 | tf_op jit(solution)/shard_map/ppermute | solution.py:347
  122.2 0.1 collective-permute-start.21
  122.4 4.8 %inputs.1 = bf16[512,512]{1,0:T(8,128)(2,1)} custom-call(s32[32,8]{1,0:T(8,128)} %copy.15.tiles_ref, s32[2]{0:T(128)} %pad_add_fusion.place_ref, bf16[512,512]{1,0:T(8,128)(2,1)} %bitcast.51, bf16[512,512]{1,0:T(8,128)(2,1)} %bitcast.59, bf16[512,512]{1,0:T(8,128)(2,1)} %get-tuple-element.41.dquery_ref, bf16[1024,512]{1,0:T(8,128)(2,1)} %get-tuple-element.42.dpair_ref, ...), custom_call_target="tpu_custom_call" | custom-call | flops 805306368 | bytes 6291456 | tf_op jit(solution)/shard_map/inputs/pallas_call | solution.py:521
  127.1 1.9 %outputs.2 = (f32[512,1536]{1,0:T(8,128)}, f32[512,512]{1,0:T(8,128)}) custom-call(s32[2]{0:T(128)S(1)} %copy-done, bf16[4096,128]{1,0:T(8,128)(2,1)S(1)} %bitcast.46), custom_call_target="tpu_custom_call" | custom-call | bytes 4194304 | tf_op jit(solution)/shard_map/outputs/pallas_call | solution.py:540
  129.1 1.9 %outputs.3 = (f32[512,1536]{1,0:T(8,128)}, f32[512,512]{1,0:T(8,128)}) custom-call(s32[2]{0:T(128)S(1)} %copy-done, bf16[4096,128]{1,0:T(8,128)(2,1)S(1)} %collective-permute-done.21.gathered_ref, f32[512,1536]{1,0:T(8,128)} %get-tuple-element.57.refs_0_, f32[512,512]{1,0:T(8,128)} %get-tuple-element.58.refs_1_), custom_call_target="tpu_custom_call", output_to_operand_aliasing={{0}: (2, {}), {1}: (3, {})} | custom-call | bytes 4194304 | tf_op jit(solution)/shard_map/outputs/pallas_call | solution.py:540
  (47 shorter events, 0.4 us)
Async XLA Ops:
  4.6 14.0 %collective-permute-start = (bf16[2,128,512]{2,1,0:T(8,128)(2,1)}, bf16[2,128,512]{2,1,0:T(8,128)(2,1)S(1)}, u32[]{:S(2)}, u32[]{:S(2)}) collective-permute-start(bf16[2,128,512]{2,1,0:T(8,128)(2,1)} %get-tuple-element.37), channel_id=1, source_target_pairs={{0,8},{4,12},{8,16},{12,20},{16,24},{20,28},{24,0},{28,4},{1,9},{5... | collective-permute-start | bytes 786440 | tf_op jit(solution)/shard_map/ppermute | solution.py:343
  7.7 16.2 %collective-permute-start.1 = (bf16[2,128,512]{2,1,0:T(8,128)(2,1)}, bf16[2,128,512]{2,1,0:T(8,128)(2,1)S(1)}, u32[]{:S(2)}, u32[]{:S(2)}) collective-permute-start(bf16[2,128,512]{2,1,0:T(8,128)(2,1)} %get-tuple-element.38), channel_id=1, source_target_pairs={{0,4},{4,8},{8,12},{12,16},{16,20},{20,24},{24,28},{28,0},{1,5},{5... | collective-permute-start | bytes 786440 | tf_op jit(solution)/shard_map/ppermute | solution.py:343
  9.2 14.7 %collective-permute-start.2 = (bf16[2,128,512]{2,1,0:T(8,128)(2,1)}, bf16[2,128,512]{2,1,0:T(8,128)(2,1)S(1)}, u32[]{:S(2)}, u32[]{:S(2)}) collective-permute-start(bf16[2,128,512]{2,1,0:T(8,128)(2,1)} %get-tuple-element.39), channel_id=1, source_target_pairs={{0,28},{4,0},{8,4},{12,8},{16,12},{20,16},{24,20},{28,24},{1,29},{... | collective-permute-start | bytes 786440 | tf_op jit(solution)/shard_map/ppermute | solution.py:343
  12.4 15.0 %collective-permute-start.3 = (bf16[2,128,512]{2,1,0:T(8,128)(2,1)}, bf16[2,128,512]{2,1,0:T(8,128)(2,1)S(1)}, u32[]{:S(2)}, u32[]{:S(2)}) collective-permute-start(bf16[2,128,512]{2,1,0:T(8,128)(2,1)} %get-tuple-element.40), channel_id=1, source_target_pairs={{0,24},{4,28},{8,0},{12,4},{16,8},{20,12},{24,16},{28,20},{1,25},{... | collective-permute-start | bytes 786440 | tf_op jit(solution)/shard_map/ppermute | solution.py:343
  18.7 8.8 %copy-start.5 = (bf16[2,128,512]{2,1,0:T(8,128)(2,1)}, bf16[2,128,512]{2,1,0:T(8,128)(2,1)S(1)}, u32[]{:S(2)}) copy-start(bf16[2,128,512]{2,1,0:T(8,128)(2,1)S(1)} %collective-permute-done.halo_a) | copy-start | bytes 786436
  23.9 3.6 %copy-start.6 = (bf16[2,128,512]{2,1,0:T(8,128)(2,1)}, bf16[2,128,512]{2,1,0:T(8,128)(2,1)S(1)}, u32[]{:S(2)}) copy-start(bf16[2,128,512]{2,1,0:T(8,128)(2,1)S(1)} %collective-permute-done.1.halo_b) | copy-start | bytes 786436
  23.9 3.6 %copy-start.7 = (bf16[2,128,512]{2,1,0:T(8,128)(2,1)}, bf16[2,128,512]{2,1,0:T(8,128)(2,1)S(1)}, u32[]{:S(2)}) copy-start(bf16[2,128,512]{2,1,0:T(8,128)(2,1)S(1)} %collective-permute-done.2.halo_c) | copy-start | bytes 786436
  27.5 0.7 copy-start.8
  51.8 2.9 %collective-permute-start.4 = (bf16[4096,128]{1,0:T(8,128)(2,1)}, bf16[4096,128]{1,0:T(8,128)(2,1)S(1)}, u32[]{:S(2)}, u32[]{:S(2)}) collective-permute-start(bf16[4096,128]{1,0:T(8,128)(2,1)} %get-tuple-element.44), channel_id=1, source_target_pairs={{0,1},{1,0},{2,3},{3,2},{4,5},{5,4},{6,7},{7,6},{8,9},{9,8},{10,11... | collective-permute-start | bytes 3145736 | tf_op jit(solution)/shard_map/ppermute | solution.py:347
  56.2 22.6 %copy-start.11 = (bf16[2,128,512]{2,1,0:T(8,128)(2,1)S(1)}, bf16[2,128,512]{2,1,0:T(8,128)(2,1)}, u32[]{:S(2)}) copy-start(bf16[2,128,512]{2,1,0:T(8,128)(2,1)} %get-tuple-element.51) | copy-start | bytes 786436
  56.2 22.6 %copy-start.10 = (bf16[2,128,512]{2,1,0:T(8,128)(2,1)S(1)}, bf16[2,128,512]{2,1,0:T(8,128)(2,1)}, u32[]{:S(2)}) copy-start(bf16[2,128,512]{2,1,0:T(8,128)(2,1)} %get-tuple-element.49) | copy-start | bytes 786436
  56.3 26.5 %copy-start.9 = (bf16[2,128,512]{2,1,0:T(8,128)(2,1)S(1)}, bf16[2,128,512]{2,1,0:T(8,128)(2,1)}, u32[]{:S(2)}) copy-start(bf16[2,128,512]{2,1,0:T(8,128)(2,1)} %get-tuple-element.50) | copy-start | bytes 786436
  56.3 10.2 %collective-permute-start.7 = (bf16[1024,128]{1,0:T(8,128)(2,1)S(1)}, bf16[1024,128]{1,0:T(8,128)(2,1)S(1)}, u32[]{:S(2)}, u32[]{:S(2)}) collective-permute-start(bf16[1024,128]{1,0:T(8,128)(2,1)S(1)} %get-tuple-element.62), channel_id=1, source_target_pairs={{0,6},{1,7},{2,4},{3,5},{4,2},{5,3},{6,0},{7,1},{8,14},{9,15},{10,... | collective-permute-start | bytes 786440 | tf_op jit(solution)/shard_map/ppermute | solution.py:347
  58.8 12.4 %collective-permute-start.6 = (bf16[1024,128]{1,0:T(8,128)(2,1)S(1)}, bf16[1024,128]{1,0:T(8,128)(2,1)S(1)}, u32[]{:S(2)}, u32[]{:S(2)}) collective-permute-start(bf16[1024,128]{1,0:T(8,128)(2,1)S(1)} %get-tuple-element.63), channel_id=1, source_target_pairs={{0,4},{1,5},{2,6},{3,7},{4,0},{5,1},{6,2},{7,3},{8,12},{9,13},{10,... | collective-permute-start | bytes 786440 | tf_op jit(solution)/shard_map/ppermute | solution.py:347
  59.3 12.0 %collective-permute-start.5 = (bf16[1024,128]{1,0:T(8,128)(2,1)S(1)}, bf16[1024,128]{1,0:T(8,128)(2,1)S(1)}, u32[]{:S(2)}, u32[]{:S(2)}) collective-permute-start(bf16[1024,128]{1,0:T(8,128)(2,1)S(1)} %get-tuple-element.61), channel_id=1, source_target_pairs={{0,2},{1,3},{2,0},{3,1},{4,6},{5,7},{6,4},{7,5},{8,10},{9,11},{10,... | collective-permute-start | bytes 786440 | tf_op jit(solution)/shard_map/ppermute | solution.py:347
  71.5 7.3 %collective-permute-start.10 = (bf16[256,128]{1,0:T(8,128)(2,1)S(1)}, bf16[256,128]{1,0:T(8,128)(2,1)S(1)}, u32[]{:S(2)}, u32[]{:S(2)}) collective-permute-start(bf16[256,128]{1,0:T(8,128)(2,1)S(1)} %get-tuple-element.65), channel_id=1, source_target_pairs={{0,24},{1,25},{2,26},{3,27},{4,28},{5,29},{6,30},{7,31},{8,16},{9,... | collective-permute-start | bytes 196616 | tf_op jit(solution)/shard_map/ppermute | solution.py:347
  74.4 8.3 %collective-permute-start.9 = (bf16[256,128]{1,0:T(8,128)(2,1)S(1)}, bf16[256,128]{1,0:T(8,128)(2,1)S(1)}, u32[]{:S(2)}, u32[]{:S(2)}) collective-permute-start(bf16[256,128]{1,0:T(8,128)(2,1)S(1)} %get-tuple-element.66), channel_id=1, source_target_pairs={{0,16},{1,17},{2,18},{3,19},{4,20},{5,21},{6,22},{7,23},{8,24},{9,... | collective-permute-start | bytes 196616 | tf_op jit(solution)/shard_map/ppermute | solution.py:347
  74.4 8.3 %collective-permute-start.8 = (bf16[256,128]{1,0:T(8,128)(2,1)S(1)}, bf16[256,128]{1,0:T(8,128)(2,1)S(1)}, u32[]{:S(2)}, u32[]{:S(2)}) collective-permute-start(bf16[256,128]{1,0:T(8,128)(2,1)S(1)} %get-tuple-element.64), channel_id=1, source_target_pairs={{0,8},{1,9},{2,10},{3,11},{4,12},{5,13},{6,14},{7,15},{8,0},{9,1},... | collective-permute-start | bytes 196616 | tf_op jit(solution)/shard_map/ppermute | solution.py:347
  76.0 34.5 %collective-permute-start.14 = (bf16[2,128,512]{2,1,0:T(8,128)(2,1)}, bf16[2,128,512]{2,1,0:T(8,128)(2,1)S(1)}, u32[]{:S(2)}, u32[]{:S(2)}) collective-permute-start(bf16[2,128,512]{2,1,0:T(8,128)(2,1)} %get-tuple-element.48), channel_id=1, source_target_pairs={{0,24},{4,28},{8,0},{12,4},{16,8},{20,12},{24,16},{28,20},{1,25},{... | collective-permute-start | bytes 786440 | tf_op jit(solution)/shard_map/ppermute | solution.py:343
  78.8 31.7 %collective-permute-start.17 = (bf16[2,128,512]{2,1,0:T(8,128)(2,1)S(1)}, bf16[2,128,512]{2,1,0:T(8,128)(2,1)S(1)}, u32[]{:S(2)}, u32[]{:S(2)}) collective-permute-start(bf16[2,128,512]{2,1,0:T(8,128)(2,1)S(1)} %copy-done.11), channel_id=1, source_target_pairs={{0,8},{4,12},{8,16},{12,20},{16,24},{20,28},{24,0},{28,4},{1,9},{5... | collective-permute-start | bytes 786440 | tf_op jit(solution)/shard_map/ppermute | solution.py:343
  78.9 31.7 %collective-permute-start.15 = (bf16[2,128,512]{2,1,0:T(8,128)(2,1)S(1)}, bf16[2,128,512]{2,1,0:T(8,128)(2,1)S(1)}, u32[]{:S(2)}, u32[]{:S(2)}) collective-permute-start(bf16[2,128,512]{2,1,0:T(8,128)(2,1)S(1)} %copy-done.10), channel_id=1, source_target_pairs={{0,28},{4,0},{8,4},{12,8},{16,12},{20,16},{24,20},{28,24},{1,29},{... | collective-permute-start | bytes 786440 | tf_op jit(solution)/shard_map/ppermute | solution.py:343
  82.7 27.8 %collective-permute-start.16 = (bf16[2,128,512]{2,1,0:T(8,128)(2,1)S(1)}, bf16[2,128,512]{2,1,0:T(8,128)(2,1)S(1)}, u32[]{:S(2)}, u32[]{:S(2)}) collective-permute-start(bf16[2,128,512]{2,1,0:T(8,128)(2,1)S(1)} %copy-done.9), channel_id=1, source_target_pairs={{0,4},{4,8},{8,12},{12,16},{16,20},{20,24},{24,28},{28,0},{1,5},{5... | collective-permute-start | bytes 786440 | tf_op jit(solution)/shard_map/ppermute | solution.py:343
  82.9 15.6 %collective-permute-start.11 = (bf16[256,128]{1,0:T(8,128)(2,1)S(1)}, bf16[256,128]{1,0:T(8,128)(2,1)S(1)}, u32[]{:S(2)}, u32[]{:S(2)}) collective-permute-start(bf16[256,128]{1,0:T(8,128)(2,1)S(1)} %bitcast.63), channel_id=1, source_target_pairs={{0,8},{1,9},{2,10},{3,11},{4,12},{5,13},{6,14},{7,15},{8,0},{9,1},... | collective-permute-start | bytes 196616 | tf_op jit(solution)/shard_map/ppermute | solution.py:347
  98.5 5.9 %collective-permute-start.12 = (bf16[256,128]{1,0:T(8,128)(2,1)S(1)}, bf16[256,128]{1,0:T(8,128)(2,1)S(1)}, u32[]{:S(2)}, u32[]{:S(2)}) collective-permute-start(bf16[256,128]{1,0:T(8,128)(2,1)S(1)} %bitcast.65), channel_id=1, source_target_pairs={{0,16},{1,17},{2,18},{3,19},{4,20},{5,21},{6,22},{7,23},{8,24},{9,... | collective-permute-start | bytes 196616 | tf_op jit(solution)/shard_map/ppermute | solution.py:347
  104.4 6.1 %collective-permute-start.13 = (bf16[256,128]{1,0:T(8,128)(2,1)S(1)}, bf16[256,128]{1,0:T(8,128)(2,1)S(1)}, u32[]{:S(2)}, u32[]{:S(2)}) collective-permute-start(bf16[256,128]{1,0:T(8,128)(2,1)S(1)} %bitcast.66), channel_id=1, source_target_pairs={{0,24},{1,25},{2,26},{3,27},{4,28},{5,29},{6,30},{7,31},{8,16},{9,... | collective-permute-start | bytes 196616 | tf_op jit(solution)/shard_map/ppermute | solution.py:347
  110.5 11.8 %copy-start.1 = (bf16[2,128,512]{2,1,0:T(8,128)(2,1)}, bf16[2,128,512]{2,1,0:T(8,128)(2,1)S(1)}, u32[]{:S(2)}) copy-start(bf16[2,128,512]{2,1,0:T(8,128)(2,1)S(1)} %collective-permute-done.14.back_a) | copy-start | bytes 786436
  110.5 11.8 %copy-start.2 = (bf16[2,128,512]{2,1,0:T(8,128)(2,1)}, bf16[2,128,512]{2,1,0:T(8,128)(2,1)S(1)}, u32[]{:S(2)}) copy-start(bf16[2,128,512]{2,1,0:T(8,128)(2,1)S(1)} %collective-permute-done.17.back_d) | copy-start | bytes 786436
  110.5 11.8 %copy-start.3 = (bf16[2,128,512]{2,1,0:T(8,128)(2,1)}, bf16[2,128,512]{2,1,0:T(8,128)(2,1)S(1)}, u32[]{:S(2)}) copy-start(bf16[2,128,512]{2,1,0:T(8,128)(2,1)S(1)} %collective-permute-done.15.back_b) | copy-start | bytes 786436
  110.6 11.8 %copy-start.4 = (bf16[2,128,512]{2,1,0:T(8,128)(2,1)}, bf16[2,128,512]{2,1,0:T(8,128)(2,1)S(1)}, u32[]{:S(2)}) copy-start(bf16[2,128,512]{2,1,0:T(8,128)(2,1)S(1)} %collective-permute-done.16.back_c) | copy-start | bytes 786436
  110.6 8.1 %collective-permute-start.18 = (bf16[1024,128]{1,0:T(8,128)(2,1)S(1)}, bf16[1024,128]{1,0:T(8,128)(2,1)S(1)}, u32[]{:S(2)}, u32[]{:S(2)}) collective-permute-start(bf16[1024,128]{1,0:T(8,128)(2,1)S(1)} %bitcast.54), channel_id=1, source_target_pairs={{0,2},{1,3},{2,0},{3,1},{4,6},{5,7},{6,4},{7,5},{8,10},{9,11},{10,... | collective-permute-start | bytes 786440 | tf_op jit(solution)/shard_map/ppermute | solution.py:347
  111.4 10.8 %collective-permute-start.19 = (bf16[1024,128]{1,0:T(8,128)(2,1)S(1)}, bf16[1024,128]{1,0:T(8,128)(2,1)S(1)}, u32[]{:S(2)}, u32[]{:S(2)}) collective-permute-start(bf16[1024,128]{1,0:T(8,128)(2,1)S(1)} %bitcast.55), channel_id=1, source_target_pairs={{0,4},{1,5},{2,6},{3,7},{4,0},{5,1},{6,2},{7,3},{8,12},{9,13},{10,... | collective-permute-start | bytes 786440 | tf_op jit(solution)/shard_map/ppermute | solution.py:347
  112.4 9.8 %collective-permute-start.20 = (bf16[1024,128]{1,0:T(8,128)(2,1)S(1)}, bf16[1024,128]{1,0:T(8,128)(2,1)S(1)}, u32[]{:S(2)}, u32[]{:S(2)}) collective-permute-start(bf16[1024,128]{1,0:T(8,128)(2,1)S(1)} %bitcast.56), channel_id=1, source_target_pairs={{0,6},{1,7},{2,4},{3,5},{4,2},{5,3},{6,0},{7,1},{8,14},{9,15},{10,... | collective-permute-start | bytes 786440 | tf_op jit(solution)/shard_map/ppermute | solution.py:347
  122.2 6.8 %collective-permute-start.21 = (bf16[4096,128]{1,0:T(8,128)(2,1)S(1)}, bf16[4096,128]{1,0:T(8,128)(2,1)S(1)}, u32[]{:S(2)}, u32[]{:S(2)}) collective-permute-start(bf16[4096,128]{1,0:T(8,128)(2,1)S(1)} %bitcast.45), channel_id=1, source_target_pairs={{0,1},{1,0},{2,3},{3,2},{4,5},{5,4},{6,7},{7,6},{8,9},{9,8},{10,11... | collective-permute-start | bytes 3145736 | tf_op jit(solution)/shard_map/ppermute | solution.py:347
  122.4 4.8 %copy-start = (s32[2]{0:T(128)S(1)}, s32[2]{0:T(128)}, u32[]{:S(2)}) copy-start(s32[2]{0:T(128)} %pad_add_fusion.place_ref) | copy-start | bytes 28

commit v3 on v2

--- a/solution.py
+++ b/solution.py
@@ -1,4 +1,5 @@
 from functools import partial
+import math
 
 import jax
 import jax.numpy as jnp
@@ -18,6 +19,7 @@
 SLOTS = CAP * len(OFFSETS)
 MASKED = -1e30
 CHUNK = 16
+OPEN_AT = 3
 AXES = ("patch", "sample")
 
 epsilon = 1e-06
@@ -116,6 +118,7 @@
     dvalue_s,
     dpair_s,
     attended_s,
+    turned_s,
 ):
     halos = (halo_a, halo_b, halo_c, halo_d)
     backs = (back_a, back_b, back_c, back_d)
@@ -124,6 +127,7 @@
     tile_count = rows_local // TILE
     head_width = width // HEADS
     scaling = head_width ** (-0.5)
+    scaling_2 = scaling * math.log2(math.e)
     first_row = position * tile_count
     normed_s[:rows_local, :] = normed_ref[...]
     for column, halo in enumerate(halos):
@@ -155,90 +159,106 @@
         biases.append(jnp.concatenate(pieces, 1))
         slots.append(places)
 
-    def one_head(head, carry):
-        lanes = pl.ds(pl.multiple_of(head * head_width, head_width), head_width)
-        key_lanes = pl.ds(pl.multiple_of(width + head * head_width, head_width), head_width)
-        value_lanes = pl.ds(pl.multiple_of(2 * width + head * head_width, head_width), head_width)
-        both = jnp.concatenate([weight_ref[:, key_lanes], weight_ref[:, value_lanes]], 1)
-        pair_s[...] = nn(normed_s[rows_local:, :], both).astype(jnp.bfloat16)
-        keys = projected_ref[:, key_lanes]
-        values = projected_ref[:, value_lanes]
-        score_s[:, :rows_local] = nt(projected_ref[:, lanes], keys)
-        dprob_s[:, :rows_local] = nt(grad_ref[:, lanes], values)
-        queries_t = projected_ref[:, lanes].T
-        grads_t = grad_ref[:, lanes].T
-        dkey_s[...] = jnp.zeros_like(dkey_s)
-        dvalue_s[...] = jnp.zeros_like(dvalue_s)
-
-        def rows_of(tile):
-            return slice(tile * TILE, (tile + 1) * TILE)
-
-        def halo_of(tile, part):
-            starts = [pl.multiple_of(place * TILE, TILE) for place in slots[tile]]
-            return jnp.concatenate([pair_s[pl.ds(start, TILE), part] for start in starts], 0)
-
-        key_part, value_part = slice(0, head_width), slice(head_width, 2 * head_width)
-
-        def products(tile):
+    low = jnp.bfloat16
+    key_part, value_part = slice(0, head_width), slice(head_width, 2 * head_width)
+
+    def lanes_of(part, head):
+        return pl.ds(part * width + head * head_width, head_width)
+
+    def rows_of(tile):
+        return slice(tile * TILE, (tile + 1) * TILE)
+
+    def halo_of(head, tile, part):
+        starts = [pl.multiple_of(place * TILE, TILE) for place in slots[tile]]
+        return jnp.concatenate([pair_s[head % 2, pl.ds(start, TILE), part] for start in starts], 0)
+
+    def project(head):
+        both = jnp.concatenate(
+            [weight_ref[:, lanes_of(1, head)], weight_ref[:, lanes_of(2, head)]], 1
+        )
+        pair_s[head % 2] = nn(normed_s[rows_local:, :], both).astype(low)
+
+    def open_head(head):
+        turn = head % 2
+        lanes = lanes_of(0, head)
+        local = nt(projected_ref[:, lanes], projected_ref[:, lanes_of(1, head)])
+        for tile in range(tile_count):
             rows = rows_of(tile)
-            score_s[rows, rows_local:] = nt(projected_ref[rows, lanes], halo_of(tile, key_part))
-            dprob_s[rows, rows_local:] = nt(grad_ref[rows, lanes], halo_of(tile, value_part))
-
-        def softmax(tile):
-            chunks = [
-                slice(first, first + CHUNK) for first in range(tile * TILE, (tile + 1) * TILE, CHUNK)
-            ]
-            highest = [
-                jnp.max(score_s[chunk, :] * scaling + biases[tile], -1, keepdims=True)
-                for chunk in chunks
-            ]
-            stats = []
-            for chunk, high in zip(chunks, highest):
-                expanded = jnp.exp(score_s[chunk, :] * scaling + (biases[tile] - high))
-                score_s[chunk, :] = expanded
-                over = 1.0 / jnp.sum(expanded, -1, keepdims=True)
-                centre = jnp.sum(expanded * dprob_s[chunk, :], -1, keepdims=True) * over
-                stats.append((over, centre))
-            for chunk, (over, centre) in zip(chunks, stats):
-                attention = score_s[chunk, :] * over
-                low_s[chunk, :] = attention.astype(jnp.bfloat16)
-                dscore = attention * (dprob_s[chunk, :] - centre)
-                dscore_s[chunk, :] = dscore.astype(jnp.bfloat16)
-
-        def finish(tile):
-            rows = rows_of(tile)
-            attended = nn(low_s[rows, :], jnp.concatenate([values, halo_of(tile, value_part)], 0))
-            attended_s[rows, lanes] = attended.astype(jnp.bfloat16)
-            key_all = jnp.concatenate([keys, halo_of(tile, key_part)], 0)
-            dquery = nn(dscore_s[rows, :], key_all) * scaling
-            dquery_ref[rows, lanes] = dquery.astype(jnp.bfloat16)
-            dkey_t = nn(queries_t[:, rows], dscore_s[rows, rows_local:])
-            dvalue_t = nn(grads_t[:, rows], low_s[rows, rows_local:])
-            for column, place in enumerate(slots[tile]):
-                part = slice(column * TILE, (column + 1) * TILE)
-                dkey_s[place] += dkey_t[:, part]
-                dvalue_s[place] += dvalue_t[:, part]
-
-        products(0)
-        for tile in range(tile_count):
-            if tile + 1 < tile_count:
-                products(tile + 1)
-            if tile > 0:
-                finish(tile - 1)
-            softmax(tile)
-        finish(tile_count - 1)
-        low = jnp.bfloat16
-        key_rows = lanes
-        value_rows = key_lanes
-        dpair_s[key_rows, :rows_local] = (nn(queries_t, dscore_s[:, :rows_local]) * scaling).astype(low)
-        dpair_s[value_rows, :rows_local] = nn(grads_t, low_s[:, :rows_local]).astype(low)
+            score_s[turn, rows, :rows_local] = local[rows, :] + biases[tile][:, :rows_local]
+        dprob_s[turn, :, :rows_local] = nt(grad_ref[:, lanes], projected_ref[:, lanes_of(2, head)])
+        turned_s[turn, 0] = projected_ref[:, lanes].T
+        turned_s[turn, 1] = grad_ref[:, lanes].T
+        dkey_s[turn] = jnp.zeros(dkey_s.shape[1:], jnp.float32)
+        dvalue_s[turn] = jnp.zeros(dvalue_s.shape[1:], jnp.float32)
+
+    def products(head, tile):
+        turn, rows, lanes = head % 2, rows_of(tile), lanes_of(0, head)
+        seen = nt(projected_ref[rows, lanes], halo_of(head, tile, key_part))
+        score_s[turn, rows, rows_local:] = seen + biases[tile][:, rows_local:]
+        dprob_s[turn, rows, rows_local:] = nt(grad_ref[rows, lanes], halo_of(head, tile, value_part))
+
+    def softmax(head, tile):
+        turn = head % 2
+        chunks = [
+            slice(first, first + CHUNK) for first in range(tile * TILE, (tile + 1) * TILE, CHUNK)
+        ]
+        highest = [jnp.max(score_s[turn, chunk, :], -1, keepdims=True) for chunk in chunks]
+        stats = []
+        for chunk, high in zip(chunks, highest):
+            expanded = jnp.exp2(score_s[turn, chunk, :] * scaling_2 - high * scaling_2)
+            score_s[turn, chunk, :] = expanded
+            over = 1.0 / jnp.sum(expanded, -1, keepdims=True)
+            centre = jnp.sum(expanded * dprob_s[turn, chunk, :], -1, keepdims=True) * over
+            stats.append((over, centre))
+        for chunk, (over, centre) in zip(chunks, stats):
+            attention = score_s[turn, chunk, :] * over
+            low_s[turn, chunk, :] = attention.astype(low)
+            dscore_s[turn, chunk, :] = (attention * (dprob_s[turn, chunk, :] - centre)).astype(low)
+
+    def finish(head, tile):
+        turn, rows, lanes = head % 2, rows_of(tile), lanes_of(0, head)
+        values = projected_ref[:, lanes_of(2, head)]
+        value_all = jnp.concatenate([values, halo_of(head, tile, value_part)], 0)
+        attended_s[rows, lanes] = nn(low_s[turn, rows, :], value_all).astype(low)
+        keys = projected_ref[:, lanes_of(1, head)]
+        key_all = jnp.concatenate([keys, halo_of(head, tile, key_part)], 0)
+        dquery_ref[rows, lanes] = (nn(dscore_s[turn, rows, :], key_all) * scaling).astype(low)
+        dkey_t = nn(turned_s[turn, 0, :, rows], dscore_s[turn, rows, rows_local:])
+        dvalue_t = nn(turned_s[turn, 1, :, rows], low_s[turn, rows, rows_local:])
+        for column, place in enumerate(slots[tile]):
+            part = slice(column * TILE, (column + 1) * TILE)
+            dkey_s[turn, place] += dkey_t[:, part]
+            dvalue_s[turn, place] += dvalue_t[:, part]
+
+    def close_head(head):
+        turn = head % 2
+        key_rows, value_rows = lanes_of(0, head), lanes_of(1, head)
+        dkey = nn(turned_s[turn, 0], dscore_s[turn, :, :rows_local]) * scaling
+        dpair_s[key_rows, :rows_local] = dkey.astype(low)
+        dpair_s[value_rows, :rows_local] = nn(turned_s[turn, 1], low_s[turn, :, :rows_local]).astype(low)
         for place in range(SLOTS):
             part = slice(rows_local + place * TILE, rows_local + (place + 1) * TILE)
-            dpair_s[key_rows, part] = (dkey_s[place] * scaling).astype(low)
-            dpair_s[value_rows, part] = dvalue_s[place].astype(low)
-        return carry
-
-    lax.fori_loop(0, HEADS, one_head, 0)
+            dpair_s[key_rows, part] = (dkey_s[turn, place] * scaling).astype(low)
+            dpair_s[value_rows, part] = dvalue_s[turn, place].astype(low)
+
+    steps = [(head, tile) for head in range(HEADS) for tile in range(tile_count)]
+    project(0)
+    open_head(0)
+    products(*steps[0])
+    for place, (head, tile) in enumerate(steps):
+        if tile == 1 and head + 1 < HEADS:
+            project(head + 1)
+        if tile == OPEN_AT and head + 1 < HEADS:
+            open_head(head + 1)
+        if place + 1 < len(steps):
+            products(*steps[place + 1])
+        if place > 0:
+            finish(*steps[place - 1])
+            if tile == 0:
+                close_head(head - 1)
+        softmax(head, tile)
+    finish(*steps[-1])
+    close_head(HEADS - 1)
     blocks = width // TILE
     side = place_ref[1]
     for out_ref, half in ((sent_ref, 1 - side), (kept_ref, side)):
@@ -259,6 +279,27 @@
         part = nn(weight_ref[:, width:], dpair_s[:, first : first + CAP * TILE])
         back[...] = part.astype(jnp.bfloat16).T.reshape(back.shape)
     dpair_ref[...] = dpair_s[:, :rows_local]
+
+
+def main_scratch(rows_local, width):
+    halo_rows = SLOTS * TILE
+    all_rows = rows_local + halo_rows
+    keys_seen = rows_local + len(OFFSETS) * TILE
+    head_width = width // HEADS
+    low = jnp.bfloat16
+    return [
+        pltpu.VMEM((all_rows, width), low),
+        pltpu.VMEM((2, halo_rows, 2 * head_width), low),
+        pltpu.VMEM((2, rows_local, keys_seen), jnp.float32),
+        pltpu.VMEM((2, rows_local, keys_seen), jnp.float32),
+        pltpu.VMEM((2, rows_local, keys_seen), low),
+        pltpu.VMEM((2, rows_local, keys_seen), low),
+        pltpu.VMEM((2, SLOTS, head_width, TILE), jnp.float32),
+        pltpu.VMEM((2, SLOTS, head_width, TILE), jnp.float32),
+        pltpu.VMEM((2 * width, all_rows), low),
+        pltpu.VMEM((rows_local, width), low),
+        pltpu.VMEM((2, 2, head_width, rows_local), low),
+    ]
 
 
 def store_blocks(out_ref, first, value, blocks, across=False):
@@ -362,10 +403,10 @@
     flips = flips_of(bits)
     digit = digit_of(index, bits)
     pieces = value.reshape(len(flips), value.shape[0] // len(flips), value.shape[1])
-    received = [
-        exchange(lax.dynamic_index_in_dim(pieces, digit ^ step, 0, False), flips[step], count)
-        for step in range(1, len(flips))
-    ]
+    received = []
+    for step in range(1, len(flips)):
+        piece = lax.dynamic_index_in_dim(pieces, digit ^ step, 0, False)
+        received.append(exchange(piece, flips[step], count))
     total = lax.dynamic_index_in_dim(pieces, digit, 0, False).astype(jnp.float32)
     for piece in received:
         total = total + piece.astype(jnp.float32)
@@ -445,10 +486,6 @@
         ),
         name="front",
     )(rows, grad_rows, weight_qkv, weight_out)
-    halo_rows = SLOTS * TILE
-    all_rows = rows_local + halo_rows
-    keys_seen = rows_local + len(OFFSETS) * TILE
-    head_width = width // HEADS
     side = index & 1
     block_rows = 4 * width * width // TILE
     outs = pl.pallas_call(
@@ -462,18 +499,7 @@
         ],
         in_specs=[SMEM] * 3 + [VMEM] * 10,
         out_specs=[VMEM] * (len(OFFSETS) + 4),
-        scratch_shapes=[
-            pltpu.VMEM((all_rows, width), low),
-            pltpu.VMEM((halo_rows, 2 * head_width), low),
-            pltpu.VMEM((rows_local, keys_seen), jnp.float32),
-            pltpu.VMEM((rows_local, keys_seen), jnp.float32),
-            pltpu.VMEM((rows_local, keys_seen), low),
-            pltpu.VMEM((rows_local, keys_seen), low),
-            pltpu.VMEM((SLOTS, head_width, TILE), jnp.float32),
-            pltpu.VMEM((SLOTS, head_width, TILE), jnp.float32),
-            pltpu.VMEM((2 * width, all_rows), low),
-            pltpu.VMEM((rows_local, width), low),
-        ],
+        scratch_shapes=main_scratch(rows_local, width),
         compiler_params=params(60),
         name="attend",
     )(

time: 131 us -> 128 us (0.977)
  Pallas kernels: 38.9 us -> 35.9 us
    pallas_call x1, Pallas kernels: 23.6 us -> 20.6 us  [on_device(): pl.pallas_call(main_kernel, out_shape=[shape(CAP, TILE, width)] * len(OFF...]
where the time goes in v3:
time: 128 us
  waiting for transfers between devices  55.5 us (43%)
  Pallas kernels  35.9 us (28%)
  starting transfers between devices  29.4 us (23%)
  local copies, waits for them, and re-layouts  4.05 us (3%)
  other arithmetic  2.26 us (2%)
    ppermute x14, waiting for transfers between devices, exchange(): lax.ppermute(value, AXES, [(source, source ^ flip) for source in range(co...  46.6 us
    pallas_call x1, Pallas kernels, on_device(): pl.pallas_call(main_kernel, out_shape=[shape(CAP, TILE, width)] * len(OFF...  20.6 us
    ppermute x8, starting transfers between devices, from_behind(): return lax.ppermute(value, 'patch', pairs)  14.8 us
    ppermute x14, starting transfers between devices, exchange(): lax.ppermute(value, AXES, [(source, source ^ flip) for source in range(co...  14.6 us
    ppermute x8, waiting for transfers between devices, from_behind(): return lax.ppermute(value, 'patch', pairs)  8.83 us
    pallas_call x1, Pallas kernels, on_device(): pl.pallas_call(partial(input_kernel, patches), out_shape=square, in_specs...  4.75 us
    pallas_call x1, Pallas kernels, on_device(): pl.pallas_call(front_kernel, out_shape=[square, shape(width, rows_local),...  4.57 us
    pallas_call x2, Pallas kernels, outputs(): pl.pallas_call(partial(output_kernel, flip), out_shape=[shape(width, 3 *...  3.87 us
  transfers between devices with their start and end apart: 22, of which 11 were waited for; matrix products, arithmetic and copies ran while one was open for 1% of the time, Pallas kernels for 9%

profile of v3, /device:TPU:0, one launch (start us, length us, event | category | flops | bytes accessed | tf_op | source)
XLA Modules:
  0.0 128.2 jit_solution(2002802997446122600)
XLA Ops:
  0.6 1.4 %copy.15.tiles_ref = s32[32,8]{1,0:T(8,128)} copy(s32[32,8]{0,1:T(8,128)} %param.10) | data formatting | bytes 2048 | tf_op args[4]
  2.0 0.6 pad_add_fusion.place_ref
  2.5 2.1 %pack.1 = (bf16[2,128,512]{2,1,0:T(8,128)(2,1)}, bf16[2,128,512]{2,1,0:T(8,128)(2,1)}, bf16[2,128,512]{2,1,0:T(8,128)(2,1)}, bf16[2,128,512]{2,1,0:T(8,128)(2,1)}) custom-call(s32[32,8]{1,0:T(8,128)} %copy.15.tiles_ref, s32[2]{0:T(128)} %pad_add_fusion.place_ref, bf16[512,512]{1,0:T(8,128)(2,1)} %bitcast.49), custom_call_target="tpu_custom_call" | custom-call | tf_op jit(solution)/shard_map/pack/pallas_call | solution.py:462
  4.6 3.1 %collective-permute-start = (bf16[2,128,512]{2,1,0:T(8,128)(2,1)}, bf16[2,128,512]{2,1,0:T(8,128)(2,1)S(1)}, u32[]{:S(2)}, u32[]{:S(2)}) collective-permute-start(bf16[2,128,512]{2,1,0:T(8,128)(2,1)} %get-tuple-element.37), channel_id=1, source_target_pairs={{0,8},{4,12},{8,16},{12,20},{16,24},{20,28},{24,0},{28,4},{1,9},{5... | collective-permute-start | bytes 786440 | tf_op jit(solution)/shard_map/ppermute | solution.py:384
  7.7 1.5 %collective-permute-start.1 = (bf16[2,128,512]{2,1,0:T(8,128)(2,1)}, bf16[2,128,512]{2,1,0:T(8,128)(2,1)S(1)}, u32[]{:S(2)}, u32[]{:S(2)}) collective-permute-start(bf16[2,128,512]{2,1,0:T(8,128)(2,1)} %get-tuple-element.38), channel_id=1, source_target_pairs={{0,4},{4,8},{8,12},{12,16},{16,20},{20,24},{24,28},{28,0},{1,5},{5... | collective-permute-start | bytes 786440 | tf_op jit(solution)/shard_map/ppermute | solution.py:384
  9.2 3.2 %collective-permute-start.2 = (bf16[2,128,512]{2,1,0:T(8,128)(2,1)}, bf16[2,128,512]{2,1,0:T(8,128)(2,1)S(1)}, u32[]{:S(2)}, u32[]{:S(2)}) collective-permute-start(bf16[2,128,512]{2,1,0:T(8,128)(2,1)} %get-tuple-element.39), channel_id=1, source_target_pairs={{0,28},{4,0},{8,4},{12,8},{16,12},{20,16},{24,20},{28,24},{1,29},{... | collective-permute-start | bytes 786440 | tf_op jit(solution)/shard_map/ppermute | solution.py:384
  12.4 0.3 collective-permute-start.3
  12.7 1.4 %copy.13.valid_ref = s32[32,8]{1,0:T(8,128)} copy(s32[32,8]{0,1:T(8,128)} %param.11) | data formatting | bytes 2048 | tf_op args[5]
  14.1 4.6 %front.1 = (bf16[512,512]{1,0:T(8,128)(2,1)}, bf16[512,512]{1,0:T(8,128)(2,1)}, bf16[512,512]{1,0:T(8,128)(2,1)}, bf16[512,1536]{1,0:T(8,128)(2,1)}, bf16[512,512]{1,0:T(8,128)(2,1)}) custom-call(bf16[512,512]{1,0:T(8,128)(2,1)} %bitcast.50, bf16[512,512]{1,0:T(8,128)(2,1)} %bitcast.58, bf16[512,1536]{1,0:T(8,128)(2,1)} %weight_ref.3, ...), custom_call_target="tpu_custom_call" | custom-call | flops 1073741824 | bytes 6291456 | tf_op jit(solution)/shard_map/front/pallas_call | solution.py:472
  18.6 0.0 collective-permute-done.halo_a
  18.7 5.3 %collective-permute-done.1.halo_b = bf16[2,128,512]{2,1,0:T(8,128)(2,1)S(1)} collective-permute-done((bf16[2,128,512]{2,1,0:T(8,128)(2,1)}, bf16[2,128,512]{2,1,0:T(8,128)(2,1)S(1)}, u32[]{:S(2)}, u32[]{:S(2)}) %collective-permute-start.1) | collective-permute-done | bytes 262176 | tf_op jit(solution)/shard_map/ppermute | solution.py:384
  23.9 3.5 %collective-permute-done.3.halo_d = bf16[2,128,512]{2,1,0:T(8,128)(2,1)S(1)} collective-permute-done((bf16[2,128,512]{2,1,0:T(8,128)(2,1)}, bf16[2,128,512]{2,1,0:T(8,128)(2,1)S(1)}, u32[]{:S(2)}, u32[]{:S(2)}) %collective-permute-start.3) | collective-permute-done | bytes 262176 | tf_op jit(solution)/shard_map/ppermute | solution.py:384
  27.5 0.7 copy-done.8
  28.2 20.6 %attend.1 = (bf16[2,128,512]{2,1,0:T(8,128)(2,1)}, bf16[2,128,512]{2,1,0:T(8,128)(2,1)}, bf16[2,128,512]{2,1,0:T(8,128)(2,1)}, bf16[2,128,512]{2,1,0:T(8,128)(2,...) custom-call(s32[32,8]{1,0:T(8,128)} %copy.15.tiles_ref, ...), custom_call_target="tpu_custom_call" | custom-call | tf_op jit(solution)/shard_map/attend/pallas_call | solution.py:491
  48.8 0.1 collective-permute-start.4
  48.9 2.8 %collective-permute-done.4 = bf16[4096,128]{1,0:T(8,128)(2,1)S(1)} collective-permute-done((bf16[4096,128]{1,0:T(8,128)(2,1)}, bf16[4096,128]{1,0:T(8,128)(2,1)S(1)}, u32[]{:S(2)}, u32[]{:S(2)}) %collective-permute-start.4) | collective-permute-done | bytes 1048608 | tf_op jit(solution)/shard_map/ppermute | solution.py:388
  51.7 1.5 %add_convert_fusion = bf16[4096,128]{1,0:T(8,128)(2,1)S(1)} fusion(bf16[4096,128]{1,0:T(8,128)(2,1)S(1)} %collective-permute-done.4, bf16[4096,128]{1,0:T(8,128)(2,1)} %get-tuple-element.43), kind=kLoop, calls=%fused_computation | loop fusion | flops 2097152 | bytes 3145728 | tf_op jit(solution)/shard_map/convert_element_type | solution.py:529
  53.3 0.1 dynamic-slice_bitcast_fusion.2
  53.3 2.5 %collective-permute-start.7 = (bf16[1024,128]{1,0:T(8,128)(2,1)S(1)}, bf16[1024,128]{1,0:T(8,128)(2,1)S(1)}, u32[]{:S(2)}, u32[]{:S(2)}) collective-permute-start(bf16[1024,128]{1,0:T(8,128)(2,1)S(1)} %get-tuple-element.62), channel_id=1, source_target_pairs={{0,6},{1,7},{2,4},{3,5},{4,2},{5,3},{6,0},{7,1},{8,14},{9,15},{10,... | collective-permute-start | bytes 786440 | tf_op jit(solution)/shard_map/ppermute | solution.py:388
  55.8 0.5 collective-permute-start.6
  56.4 0.5 collective-permute-start.5
  56.9 6.6 %collective-permute-done.7 = bf16[1024,128]{1,0:T(8,128)(2,1)S(1)} collective-permute-done((bf16[1024,128]{1,0:T(8,128)(2,1)S(1)}, bf16[1024,128]{1,0:T(8,128)(2,1)S(1)}, u32[]{:S(2)}, u32[]{:S(2)}) %collective-permute-start.7) | collective-permute-done | bytes 262176 | tf_op jit(solution)/shard_map/ppermute | solution.py:388
  63.5 4.7 %collective-permute-done.6 = bf16[1024,128]{1,0:T(8,128)(2,1)S(1)} collective-permute-done((bf16[1024,128]{1,0:T(8,128)(2,1)S(1)}, bf16[1024,128]{1,0:T(8,128)(2,1)S(1)}, u32[]{:S(2)}, u32[]{:S(2)}) %collective-permute-start.6) | collective-permute-done | bytes 262176 | tf_op jit(solution)/shard_map/ppermute | solution.py:388
  68.3 0.1 collective-permute-done.5
  68.4 0.1 fusion.1
  68.5 2.9 %collective-permute-start.10 = (bf16[256,128]{1,0:T(8,128)(2,1)S(1)}, bf16[256,128]{1,0:T(8,128)(2,1)S(1)}, u32[]{:S(2)}, u32[]{:S(2)}) collective-permute-start(bf16[256,128]{1,0:T(8,128)(2,1)S(1)} %get-tuple-element.65), channel_id=1, source_target_pairs={{0,24},{1,25},{2,26},{3,27},{4,28},{5,29},{6,30},{7,31},{8,16},{9,... | collective-permute-start | bytes 196616 | tf_op jit(solution)/shard_map/ppermute | solution.py:388
  71.4 1.5 %collective-permute-start.8 = (bf16[256,128]{1,0:T(8,128)(2,1)S(1)}, bf16[256,128]{1,0:T(8,128)(2,1)S(1)}, u32[]{:S(2)}, u32[]{:S(2)}) collective-permute-start(bf16[256,128]{1,0:T(8,128)(2,1)S(1)} %get-tuple-element.64), channel_id=1, source_target_pairs={{0,8},{1,9},{2,10},{3,11},{4,12},{5,13},{6,14},{7,15},{8,0},{9,1},... | collective-permute-start | bytes 196616 | tf_op jit(solution)/shard_map/ppermute | solution.py:388
  73.0 2.8 %collective-permute-start.14 = (bf16[2,128,512]{2,1,0:T(8,128)(2,1)}, bf16[2,128,512]{2,1,0:T(8,128)(2,1)S(1)}, u32[]{:S(2)}, u32[]{:S(2)}) collective-permute-start(bf16[2,128,512]{2,1,0:T(8,128)(2,1)} %get-tuple-element.48), channel_id=1, source_target_pairs={{0,24},{4,28},{8,0},{12,4},{16,8},{20,12},{24,16},{28,20},{1,25},{... | collective-permute-start | bytes 786440 | tf_op jit(solution)/shard_map/ppermute | solution.py:384
  75.8 0.0 collective-permute-start.17
  75.9 3.9 %collective-permute-start.15 = (bf16[2,128,512]{2,1,0:T(8,128)(2,1)S(1)}, bf16[2,128,512]{2,1,0:T(8,128)(2,1)S(1)}, u32[]{:S(2)}, u32[]{:S(2)}) collective-permute-start(bf16[2,128,512]{2,1,0:T(8,128)(2,1)S(1)} %copy-done.10), channel_id=1, source_target_pairs={{0,28},{4,0},{8,4},{12,8},{16,12},{20,16},{24,20},{28,24},{1,29},{... | collective-permute-start | bytes 786440 | tf_op jit(solution)/shard_map/ppermute | solution.py:384
  79.8 0.1 copy.14
  79.9 0.1 collective-permute-start.11
  80.1 15.5 %collective-permute-done.11 = bf16[256,128]{1,0:T(8,128)(2,1)S(1)} collective-permute-done((bf16[256,128]{1,0:T(8,128)(2,1)S(1)}, bf16[256,128]{1,0:T(8,128)(2,1)S(1)}, u32[]{:S(2)}, u32[]{:S(2)}) %collective-permute-start.11) | collective-permute-done | bytes 65568 | tf_op jit(solution)/shard_map/ppermute | solution.py:388
  95.5 0.6 collective-permute-start.12
  96.2 5.2 %collective-permute-done.12 = bf16[256,128]{1,0:T(8,128)(2,1)S(1)} collective-permute-done((bf16[256,128]{1,0:T(8,128)(2,1)S(1)}, bf16[256,128]{1,0:T(8,128)(2,1)S(1)}, u32[]{:S(2)}, u32[]{:S(2)}) %collective-permute-start.12) | collective-permute-done | bytes 65568 | tf_op jit(solution)/shard_map/ppermute | solution.py:388
  101.4 2.2 %collective-permute-start.13 = (bf16[256,128]{1,0:T(8,128)(2,1)S(1)}, bf16[256,128]{1,0:T(8,128)(2,1)S(1)}, u32[]{:S(2)}, u32[]{:S(2)}) collective-permute-start(bf16[256,128]{1,0:T(8,128)(2,1)S(1)} %bitcast.66), channel_id=1, source_target_pairs={{0,24},{1,25},{2,26},{3,27},{4,28},{5,29},{6,30},{7,31},{8,16},{9,... | collective-permute-start | bytes 196616 | tf_op jit(solution)/shard_map/ppermute | solution.py:388
  103.6 3.9 %collective-permute-done.13 = bf16[256,128]{1,0:T(8,128)(2,1)S(1)} collective-permute-done((bf16[256,128]{1,0:T(8,128)(2,1)S(1)}, bf16[256,128]{1,0:T(8,128)(2,1)S(1)}, u32[]{:S(2)}, u32[]{:S(2)}) %collective-permute-start.13) | collective-permute-done | bytes 65568 | tf_op jit(solution)/shard_map/ppermute | solution.py:388
  107.5 0.0 copy-start.1
  107.6 0.8 collective-permute-start.18
  108.4 1.0 collective-permute-start.19
  109.4 1.7 %collective-permute-start.20 = (bf16[1024,128]{1,0:T(8,128)(2,1)S(1)}, bf16[1024,128]{1,0:T(8,128)(2,1)S(1)}, u32[]{:S(2)}, u32[]{:S(2)}) collective-permute-start(bf16[1024,128]{1,0:T(8,128)(2,1)S(1)} %bitcast.56), channel_id=1, source_target_pairs={{0,6},{1,7},{2,4},{3,5},{4,2},{5,3},{6,0},{7,1},{8,14},{9,15},{10,... | collective-permute-start | bytes 786440 | tf_op jit(solution)/shard_map/ppermute | solution.py:388
  111.1 0.1 broadcast_in_dim.48
  111.3 4.3 %collective-permute-done.18 = bf16[1024,128]{1,0:T(8,128)(2,1)S(1)} collective-permute-done((bf16[1024,128]{1,0:T(8,128)(2,1)S(1)}, bf16[1024,128]{1,0:T(8,128)(2,1)S(1)}, u32[]{:S(2)}, u32[]{:S(2)}) %collective-permute-start.18) | collective-permute-done | bytes 262176 | tf_op jit(solution)/shard_map/ppermute | solution.py:388
  115.7 3.5 %collective-permute-done.19 = bf16[1024,128]{1,0:T(8,128)(2,1)S(1)} collective-permute-done((bf16[1024,128]{1,0:T(8,128)(2,1)S(1)}, bf16[1024,128]{1,0:T(8,128)(2,1)S(1)}, u32[]{:S(2)}, u32[]{:S(2)}) %collective-permute-start.19) | collective-permute-done | bytes 262176 | tf_op jit(solution)/shard_map/ppermute | solution.py:388
  119.2 0.1 collective-permute-start.21
  119.4 4.8 %inputs.1 = bf16[512,512]{1,0:T(8,128)(2,1)} custom-call(s32[32,8]{1,0:T(8,128)} %copy.15.tiles_ref, s32[2]{0:T(128)} %pad_add_fusion.place_ref, bf16[512,512]{1,0:T(8,128)(2,1)} %bitcast.51, bf16[512,512]{1,0:T(8,128)(2,1)} %bitcast.59, bf16[512,512]{1,0:T(8,128)(2,1)} %get-tuple-element.41.dquery_ref, bf16[1024,512]{1,0:T(8,128)(2,1)} %get-tuple-element.42.dpair_ref, ...), custom_call_target="tpu_custom_call" | custom-call | flops 805306368 | bytes 6291456 | tf_op jit(solution)/shard_map/inputs/pallas_call | solution.py:547
  124.1 1.9 %outputs.2 = (f32[512,1536]{1,0:T(8,128)}, f32[512,512]{1,0:T(8,128)}) custom-call(s32[2]{0:T(128)S(1)} %copy-done, bf16[4096,128]{1,0:T(8,128)(2,1)S(1)} %bitcast.46), custom_call_target="tpu_custom_call" | custom-call | bytes 4194304 | tf_op jit(solution)/shard_map/outputs/pallas_call | solution.py:566
  126.1 1.9 %outputs.3 = (f32[512,1536]{1,0:T(8,128)}, f32[512,512]{1,0:T(8,128)}) custom-call(s32[2]{0:T(128)S(1)} %copy-done, bf16[4096,128]{1,0:T(8,128)(2,1)S(1)} %collective-permute-done.21.gathered_ref, f32[512,1536]{1,0:T(8,128)} %get-tuple-element.57.refs_0_, f32[512,512]{1,0:T(8,128)} %get-tuple-element.58.refs_1_), custom_call_target="tpu_custom_call", output_to_operand_aliasing={{0}: (2, {}), {1}: (3, {})} | custom-call | bytes 4194304 | tf_op jit(solution)/shard_map/outputs/pallas_call | solution.py:566
  (47 shorter events, 0.4 us)
Async XLA Ops:
  4.6 14.0 %collective-permute-start = (bf16[2,128,512]{2,1,0:T(8,128)(2,1)}, bf16[2,128,512]{2,1,0:T(8,128)(2,1)S(1)}, u32[]{:S(2)}, u32[]{:S(2)}) collective-permute-start(bf16[2,128,512]{2,1,0:T(8,128)(2,1)} %get-tuple-element.37), channel_id=1, source_target_pairs={{0,8},{4,12},{8,16},{12,20},{16,24},{20,28},{24,0},{28,4},{1,9},{5... | collective-permute-start | bytes 786440 | tf_op jit(solution)/shard_map/ppermute | solution.py:384
  7.7 16.2 %collective-permute-start.1 = (bf16[2,128,512]{2,1,0:T(8,128)(2,1)}, bf16[2,128,512]{2,1,0:T(8,128)(2,1)S(1)}, u32[]{:S(2)}, u32[]{:S(2)}) collective-permute-start(bf16[2,128,512]{2,1,0:T(8,128)(2,1)} %get-tuple-element.38), channel_id=1, source_target_pairs={{0,4},{4,8},{8,12},{12,16},{16,20},{20,24},{24,28},{28,0},{1,5},{5... | collective-permute-start | bytes 786440 | tf_op jit(solution)/shard_map/ppermute | solution.py:384
  9.2 14.7 %collective-permute-start.2 = (bf16[2,128,512]{2,1,0:T(8,128)(2,1)}, bf16[2,128,512]{2,1,0:T(8,128)(2,1)S(1)}, u32[]{:S(2)}, u32[]{:S(2)}) collective-permute-start(bf16[2,128,512]{2,1,0:T(8,128)(2,1)} %get-tuple-element.39), channel_id=1, source_target_pairs={{0,28},{4,0},{8,4},{12,8},{16,12},{20,16},{24,20},{28,24},{1,29},{... | collective-permute-start | bytes 786440 | tf_op jit(solution)/shard_map/ppermute | solution.py:384
  12.4 15.0 %collective-permute-start.3 = (bf16[2,128,512]{2,1,0:T(8,128)(2,1)}, bf16[2,128,512]{2,1,0:T(8,128)(2,1)S(1)}, u32[]{:S(2)}, u32[]{:S(2)}) collective-permute-start(bf16[2,128,512]{2,1,0:T(8,128)(2,1)} %get-tuple-element.40), channel_id=1, source_target_pairs={{0,24},{4,28},{8,0},{12,4},{16,8},{20,12},{24,16},{28,20},{1,25},{... | collective-permute-start | bytes 786440 | tf_op jit(solution)/shard_map/ppermute | solution.py:384
  18.7 8.8 %copy-start.5 = (bf16[2,128,512]{2,1,0:T(8,128)(2,1)}, bf16[2,128,512]{2,1,0:T(8,128)(2,1)S(1)}, u32[]{:S(2)}) copy-start(bf16[2,128,512]{2,1,0:T(8,128)(2,1)S(1)} %collective-permute-done.halo_a) | copy-start | bytes 786436
  23.9 3.6 %copy-start.6 = (bf16[2,128,512]{2,1,0:T(8,128)(2,1)}, bf16[2,128,512]{2,1,0:T(8,128)(2,1)S(1)}, u32[]{:S(2)}) copy-start(bf16[2,128,512]{2,1,0:T(8,128)(2,1)S(1)} %collective-permute-done.1.halo_b) | copy-start | bytes 786436
  23.9 3.6 %copy-start.7 = (bf16[2,128,512]{2,1,0:T(8,128)(2,1)}, bf16[2,128,512]{2,1,0:T(8,128)(2,1)S(1)}, u32[]{:S(2)}) copy-start(bf16[2,128,512]{2,1,0:T(8,128)(2,1)S(1)} %collective-permute-done.2.halo_c) | copy-start | bytes 786436
  27.5 0.7 copy-start.8
  48.8 2.9 %collective-permute-start.4 = (bf16[4096,128]{1,0:T(8,128)(2,1)}, bf16[4096,128]{1,0:T(8,128)(2,1)S(1)}, u32[]{:S(2)}, u32[]{:S(2)}) collective-permute-start(bf16[4096,128]{1,0:T(8,128)(2,1)} %get-tuple-element.44), channel_id=1, source_target_pairs={{0,1},{1,0},{2,3},{3,2},{4,5},{5,4},{6,7},{7,6},{8,9},{9,8},{10,11... | collective-permute-start | bytes 3145736 | tf_op jit(solution)/shard_map/ppermute | solution.py:388
  53.2 22.6 %copy-start.11 = (bf16[2,128,512]{2,1,0:T(8,128)(2,1)S(1)}, bf16[2,128,512]{2,1,0:T(8,128)(2,1)}, u32[]{:S(2)}) copy-start(bf16[2,128,512]{2,1,0:T(8,128)(2,1)} %get-tuple-element.51) | copy-start | bytes 786436
  53.2 22.6 %copy-start.10 = (bf16[2,128,512]{2,1,0:T(8,128)(2,1)S(1)}, bf16[2,128,512]{2,1,0:T(8,128)(2,1)}, u32[]{:S(2)}) copy-start(bf16[2,128,512]{2,1,0:T(8,128)(2,1)} %get-tuple-element.49) | copy-start | bytes 786436
  53.3 26.5 %copy-start.9 = (bf16[2,128,512]{2,1,0:T(8,128)(2,1)S(1)}, bf16[2,128,512]{2,1,0:T(8,128)(2,1)}, u32[]{:S(2)}) copy-start(bf16[2,128,512]{2,1,0:T(8,128)(2,1)} %get-tuple-element.50) | copy-start | bytes 786436
  53.3 10.2 %collective-permute-start.7 = (bf16[1024,128]{1,0:T(8,128)(2,1)S(1)}, bf16[1024,128]{1,0:T(8,128)(2,1)S(1)}, u32[]{:S(2)}, u32[]{:S(2)}) collective-permute-start(bf16[1024,128]{1,0:T(8,128)(2,1)S(1)} %get-tuple-element.62), channel_id=1, source_target_pairs={{0,6},{1,7},{2,4},{3,5},{4,2},{5,3},{6,0},{7,1},{8,14},{9,15},{10,... | collective-permute-start | bytes 786440 | tf_op jit(solution)/shard_map/ppermute | solution.py:388
  55.8 12.4 %collective-permute-start.6 = (bf16[1024,128]{1,0:T(8,128)(2,1)S(1)}, bf16[1024,128]{1,0:T(8,128)(2,1)S(1)}, u32[]{:S(2)}, u32[]{:S(2)}) collective-permute-start(bf16[1024,128]{1,0:T(8,128)(2,1)S(1)} %get-tuple-element.63), channel_id=1, source_target_pairs={{0,4},{1,5},{2,6},{3,7},{4,0},{5,1},{6,2},{7,3},{8,12},{9,13},{10,... | collective-permute-start | bytes 786440 | tf_op jit(solution)/shard_map/ppermute | solution.py:388
  56.4 12.0 %collective-permute-start.5 = (bf16[1024,128]{1,0:T(8,128)(2,1)S(1)}, bf16[1024,128]{1,0:T(8,128)(2,1)S(1)}, u32[]{:S(2)}, u32[]{:S(2)}) collective-permute-start(bf16[1024,128]{1,0:T(8,128)(2,1)S(1)} %get-tuple-element.61), channel_id=1, source_target_pairs={{0,2},{1,3},{2,0},{3,1},{4,6},{5,7},{6,4},{7,5},{8,10},{9,11},{10,... | collective-permute-start | bytes 786440 | tf_op jit(solution)/shard_map/ppermute | solution.py:388
  68.5 7.3 %collective-permute-start.10 = (bf16[256,128]{1,0:T(8,128)(2,1)S(1)}, bf16[256,128]{1,0:T(8,128)(2,1)S(1)}, u32[]{:S(2)}, u32[]{:S(2)}) collective-permute-start(bf16[256,128]{1,0:T(8,128)(2,1)S(1)} %get-tuple-element.65), channel_id=1, source_target_pairs={{0,24},{1,25},{2,26},{3,27},{4,28},{5,29},{6,30},{7,31},{8,16},{9,... | collective-permute-start | bytes 196616 | tf_op jit(solution)/shard_map/ppermute | solution.py:388
  71.4 8.3 %collective-permute-start.9 = (bf16[256,128]{1,0:T(8,128)(2,1)S(1)}, bf16[256,128]{1,0:T(8,128)(2,1)S(1)}, u32[]{:S(2)}, u32[]{:S(2)}) collective-permute-start(bf16[256,128]{1,0:T(8,128)(2,1)S(1)} %get-tuple-element.66), channel_id=1, source_target_pairs={{0,16},{1,17},{2,18},{3,19},{4,20},{5,21},{6,22},{7,23},{8,24},{9,... | collective-permute-start | bytes 196616 | tf_op jit(solution)/shard_map/ppermute | solution.py:388
  71.4 8.3 %collective-permute-start.8 = (bf16[256,128]{1,0:T(8,128)(2,1)S(1)}, bf16[256,128]{1,0:T(8,128)(2,1)S(1)}, u32[]{:S(2)}, u32[]{:S(2)}) collective-permute-start(bf16[256,128]{1,0:T(8,128)(2,1)S(1)} %get-tuple-element.64), channel_id=1, source_target_pairs={{0,8},{1,9},{2,10},{3,11},{4,12},{5,13},{6,14},{7,15},{8,0},{9,1},... | collective-permute-start | bytes 196616 | tf_op jit(solution)/shard_map/ppermute | solution.py:388
  73.0 34.5 %collective-permute-start.14 = (bf16[2,128,512]{2,1,0:T(8,128)(2,1)}, bf16[2,128,512]{2,1,0:T(8,128)(2,1)S(1)}, u32[]{:S(2)}, u32[]{:S(2)}) collective-permute-start(bf16[2,128,512]{2,1,0:T(8,128)(2,1)} %get-tuple-element.48), channel_id=1, source_target_pairs={{0,24},{4,28},{8,0},{12,4},{16,8},{20,12},{24,16},{28,20},{1,25},{... | collective-permute-start | bytes 786440 | tf_op jit(solution)/shard_map/ppermute | solution.py:384
  75.8 31.7 %collective-permute-start.17 = (bf16[2,128,512]{2,1,0:T(8,128)(2,1)S(1)}, bf16[2,128,512]{2,1,0:T(8,128)(2,1)S(1)}, u32[]{:S(2)}, u32[]{:S(2)}) collective-permute-start(bf16[2,128,512]{2,1,0:T(8,128)(2,1)S(1)} %copy-done.11), channel_id=1, source_target_pairs={{0,8},{4,12},{8,16},{12,20},{16,24},{20,28},{24,0},{28,4},{1,9},{5... | collective-permute-start | bytes 786440 | tf_op jit(solution)/shard_map/ppermute | solution.py:384
  75.9 31.7 %collective-permute-start.15 = (bf16[2,128,512]{2,1,0:T(8,128)(2,1)S(1)}, bf16[2,128,512]{2,1,0:T(8,128)(2,1)S(1)}, u32[]{:S(2)}, u32[]{:S(2)}) collective-permute-start(bf16[2,128,512]{2,1,0:T(8,128)(2,1)S(1)} %copy-done.10), channel_id=1, source_target_pairs={{0,28},{4,0},{8,4},{12,8},{16,12},{20,16},{24,20},{28,24},{1,29},{... | collective-permute-start | bytes 786440 | tf_op jit(solution)/shard_map/ppermute | solution.py:384
  79.7 27.8 %collective-permute-start.16 = (bf16[2,128,512]{2,1,0:T(8,128)(2,1)S(1)}, bf16[2,128,512]{2,1,0:T(8,128)(2,1)S(1)}, u32[]{:S(2)}, u32[]{:S(2)}) collective-permute-start(bf16[2,128,512]{2,1,0:T(8,128)(2,1)S(1)} %copy-done.9), channel_id=1, source_target_pairs={{0,4},{4,8},{8,12},{12,16},{16,20},{20,24},{24,28},{28,0},{1,5},{5... | collective-permute-start | bytes 786440 | tf_op jit(solution)/shard_map/ppermute | solution.py:384
  79.9 15.6 %collective-permute-start.11 = (bf16[256,128]{1,0:T(8,128)(2,1)S(1)}, bf16[256,128]{1,0:T(8,128)(2,1)S(1)}, u32[]{:S(2)}, u32[]{:S(2)}) collective-permute-start(bf16[256,128]{1,0:T(8,128)(2,1)S(1)} %bitcast.63), channel_id=1, source_target_pairs={{0,8},{1,9},{2,10},{3,11},{4,12},{5,13},{6,14},{7,15},{8,0},{9,1},... | collective-permute-start | bytes 196616 | tf_op jit(solution)/shard_map/ppermute | solution.py:388
  95.5 5.9 %collective-permute-start.12 = (bf16[256,128]{1,0:T(8,128)(2,1)S(1)}, bf16[256,128]{1,0:T(8,128)(2,1)S(1)}, u32[]{:S(2)}, u32[]{:S(2)}) collective-permute-start(bf16[256,128]{1,0:T(8,128)(2,1)S(1)} %bitcast.65), channel_id=1, source_target_pairs={{0,16},{1,17},{2,18},{3,19},{4,20},{5,21},{6,22},{7,23},{8,24},{9,... | collective-permute-start | bytes 196616 | tf_op jit(solution)/shard_map/ppermute | solution.py:388
  101.4 6.1 %collective-permute-start.13 = (bf16[256,128]{1,0:T(8,128)(2,1)S(1)}, bf16[256,128]{1,0:T(8,128)(2,1)S(1)}, u32[]{:S(2)}, u32[]{:S(2)}) collective-permute-start(bf16[256,128]{1,0:T(8,128)(2,1)S(1)} %bitcast.66), channel_id=1, source_target_pairs={{0,24},{1,25},{2,26},{3,27},{4,28},{5,29},{6,30},{7,31},{8,16},{9,... | collective-permute-start | bytes 196616 | tf_op jit(solution)/shard_map/ppermute | solution.py:388
  107.5 11.8 %copy-start.1 = (bf16[2,128,512]{2,1,0:T(8,128)(2,1)}, bf16[2,128,512]{2,1,0:T(8,128)(2,1)S(1)}, u32[]{:S(2)}) copy-start(bf16[2,128,512]{2,1,0:T(8,128)(2,1)S(1)} %collective-permute-done.14.back_a) | copy-start | bytes 786436
  107.5 11.8 %copy-start.2 = (bf16[2,128,512]{2,1,0:T(8,128)(2,1)}, bf16[2,128,512]{2,1,0:T(8,128)(2,1)S(1)}, u32[]{:S(2)}) copy-start(bf16[2,128,512]{2,1,0:T(8,128)(2,1)S(1)} %collective-permute-done.17.back_d) | copy-start | bytes 786436
  107.5 11.8 %copy-start.3 = (bf16[2,128,512]{2,1,0:T(8,128)(2,1)}, bf16[2,128,512]{2,1,0:T(8,128)(2,1)S(1)}, u32[]{:S(2)}) copy-start(bf16[2,128,512]{2,1,0:T(8,128)(2,1)S(1)} %collective-permute-done.15.back_b) | copy-start | bytes 786436
  107.6 11.8 %copy-start.4 = (bf16[2,128,512]{2,1,0:T(8,128)(2,1)}, bf16[2,128,512]{2,1,0:T(8,128)(2,1)S(1)}, u32[]{:S(2)}) copy-start(bf16[2,128,512]{2,1,0:T(8,128)(2,1)S(1)} %collective-permute-done.16.back_c) | copy-start | bytes 786436
  107.6 8.1 %collective-permute-start.18 = (bf16[1024,128]{1,0:T(8,128)(2,1)S(1)}, bf16[1024,128]{1,0:T(8,128)(2,1)S(1)}, u32[]{:S(2)}, u32[]{:S(2)}) collective-permute-start(bf16[1024,128]{1,0:T(8,128)(2,1)S(1)} %bitcast.54), channel_id=1, source_target_pairs={{0,2},{1,3},{2,0},{3,1},{4,6},{5,7},{6,4},{7,5},{8,10},{9,11},{10,... | collective-permute-start | bytes 786440 | tf_op jit(solution)/shard_map/ppermute | solution.py:388
  108.4 10.8 %collective-permute-start.19 = (bf16[1024,128]{1,0:T(8,128)(2,1)S(1)}, bf16[1024,128]{1,0:T(8,128)(2,1)S(1)}, u32[]{:S(2)}, u32[]{:S(2)}) collective-permute-start(bf16[1024,128]{1,0:T(8,128)(2,1)S(1)} %bitcast.55), channel_id=1, source_target_pairs={{0,4},{1,5},{2,6},{3,7},{4,0},{5,1},{6,2},{7,3},{8,12},{9,13},{10,... | collective-permute-start | bytes 786440 | tf_op jit(solution)/shard_map/ppermute | solution.py:388
  109.4 9.8 %collective-permute-start.20 = (bf16[1024,128]{1,0:T(8,128)(2,1)S(1)}, bf16[1024,128]{1,0:T(8,128)(2,1)S(1)}, u32[]{:S(2)}, u32[]{:S(2)}) collective-permute-start(bf16[1024,128]{1,0:T(8,128)(2,1)S(1)} %bitcast.56), channel_id=1, source_target_pairs={{0,6},{1,7},{2,4},{3,5},{4,2},{5,3},{6,0},{7,1},{8,14},{9,15},{10,... | collective-permute-start | bytes 786440 | tf_op jit(solution)/shard_map/ppermute | solution.py:388
  119.2 6.8 %collective-permute-start.21 = (bf16[4096,128]{1,0:T(8,128)(2,1)S(1)}, bf16[4096,128]{1,0:T(8,128)(2,1)S(1)}, u32[]{:S(2)}, u32[]{:S(2)}) collective-permute-start(bf16[4096,128]{1,0:T(8,128)(2,1)S(1)} %bitcast.45), channel_id=1, source_target_pairs={{0,1},{1,0},{2,3},{3,2},{4,5},{5,4},{6,7},{7,6},{8,9},{9,8},{10,11... | collective-permute-start | bytes 3145736 | tf_op jit(solution)/shard_map/ppermute | solution.py:388
  119.4 4.8 %copy-start = (s32[2]{0:T(128)S(1)}, s32[2]{0:T(128)}, u32[]{:S(2)}) copy-start(s32[2]{0:T(128)} %pad_add_fusion.place_ref) | copy-start | bytes 28

commit v4 on v3

--- a/solution.py
+++ b/solution.py
@@ -44,7 +44,7 @@
 
 
 def named_pair(tiles_ref, first_row, column, count):
-    named = [tiles_ref[first_row + row, column] for row in range(count)]
+    named = [tiles_ref[column, first_row + row] for row in range(count)]
     low = high = named[0]
     for entry in named[1:]:
         low = jnp.minimum(low, entry)
@@ -58,8 +58,8 @@
     return [pl.multiple_of((entry - position * tile_count) * TILE, TILE) for entry in pair]
 
 
-def pack_kernel(patches, tiles_ref, place_ref, features_ref, *packed_refs):
-    position = place_ref[0]
+def pack_kernel(patches, tiles_ref, features_ref, *packed_refs):
+    position = lax.axis_index("patch").astype(jnp.int32)
     tile_count = features_ref.shape[0] // TILE
     for column, shift_by in enumerate(OFFSETS):
         rows = sent_rows(tiles_ref, position, patches, column, shift_by, tile_count)
@@ -146,15 +146,15 @@
             flag = jnp.int32(0)
             for column in range(LOCAL):
                 flag = flag + jnp.where(
-                    tiles_ref[row, column] == first_row + other, valid_ref[row, column], 0
+                    tiles_ref[column, row] == first_row + other, valid_ref[column, row], 0
                 )
             pieces.append(jnp.where(lane_tile + flag > 0, 0.0, MASKED))
         places = []
         for column in range(len(OFFSETS)):
             high = named_pair(tiles_ref, first_row, LOCAL + column, tile_count)[1]
-            place = jnp.where(tiles_ref[row, LOCAL + column] == high, 1, 0)
+            place = jnp.where(tiles_ref[LOCAL + column, row] == high, 1, 0)
             places.append(column * CAP + place)
-            flag = valid_ref[row, LOCAL + column]
+            flag = valid_ref[LOCAL + column, row]
             pieces.append(jnp.where(lane_tile + flag > 0, 0.0, MASKED))
         biases.append(jnp.concatenate(pieces, 1))
         slots.append(places)
@@ -246,7 +246,7 @@
     open_head(0)
     products(*steps[0])
     for place, (head, tile) in enumerate(steps):
-        if tile == 1 and head + 1 < HEADS:
+        if tile == 2 and head + 1 < HEADS:
             project(head + 1)
         if tile == OPEN_AT and head + 1 < HEADS:
             open_head(head + 1)
@@ -459,15 +459,18 @@
         return pltpu.CompilerParams(vmem_limit_bytes=mebibytes << 20)
 
     place = jnp.stack([position, index & 1])
+    tiles, valid = key_tiles.T, tile_valid.T
     packed = pl.pallas_call(
         partial(pack_kernel, patches),
         out_shape=[shape(CAP, TILE, width)] * len(OFFSETS),
-        in_specs=[SMEM, SMEM, VMEM],
+        in_specs=[SMEM, VMEM],
         out_specs=[VMEM] * len(OFFSETS),
         compiler_params=params(60),
         name="pack",
-    )(key_tiles, place, rows)
-    halos = [from_behind(piece, -shift_by) for piece, shift_by in zip(packed, OFFSETS)]
+    )(tiles, rows)
+    halos = []
+    for piece, shift_by in zip(packed, OFFSETS):
+        halos.append(from_behind(piece, -shift_by))
     square = shape(rows_local, width)
     normed_low, normed_t, cotangent_t, projected, grad_attended = pl.pallas_call(
         front_kernel,
@@ -503,8 +506,8 @@
         compiler_params=params(60),
         name="attend",
     )(
-        key_tiles,
-        tile_valid,
+        tiles,
+        valid,
         place,
         projected,
         grad_attended,
@@ -555,7 +558,7 @@
                     flops=6 * rows_local * width * width, bytes_accessed=6 << 20, transcendentals=0
                 ),
                 name="inputs",
-            )(key_tiles, place, rows, grad_rows, dquery, dpair, weight_qkv, *held)
+            )(tiles, place, rows, grad_rows, dquery, dpair, weight_qkv, *held)
         gathered = gather_phase(gathered, index, bits, count)
     other = exchange(gathered, 1, count)
     if not whole_chunks:

time: 128 us -> 127 us (level)
  local copies, waits for them, and re-layouts: 4.05 us -> 1.32 us
    unnamed x26 -> x24, local copies, waits for them, and re-layouts: 3.46 us -> 0.74 us
where the time goes in v4:
time: 127 us
  waiting for transfers between devices  56.3 us (44%)
  Pallas kernels  36.2 us (29%)
  starting transfers between devices  29.4 us (23%)
  other arithmetic  2.32 us (2%)
  local copies, waits for them, and re-layouts  1.32 us (1%)
    ppermute x14, waiting for transfers between devices, exchange(): lax.ppermute(value, AXES, [(source, source ^ flip) for source in range(co...  46.6 us
    pallas_call x1, Pallas kernels, on_device(): pl.pallas_call(main_kernel, out_shape=[shape(CAP, TILE, width)] * len(OFF...  20.9 us
    ppermute x8, starting transfers between devices, from_behind(): return lax.ppermute(value, 'patch', pairs)  14.8 us
    ppermute x14, starting transfers between devices, exchange(): lax.ppermute(value, AXES, [(source, source ^ flip) for source in range(co...  14.6 us
    ppermute x8, waiting for transfers between devices, from_behind(): return lax.ppermute(value, 'patch', pairs)  9.61 us
    pallas_call x1, Pallas kernels, on_device(): pl.pallas_call(partial(input_kernel, patches), out_shape=square, in_specs...  4.76 us
    pallas_call x1, Pallas kernels, on_device(): pl.pallas_call(front_kernel, out_shape=[square, shape(width, rows_local),...  4.55 us
    pallas_call x2, Pallas kernels, outputs(): pl.pallas_call(partial(output_kernel, flip), out_shape=[shape(width, 3 *...  3.87 us
  transfers between devices with their start and end apart: 22, of which 11 were waited for; matrix products, arithmetic and copies ran while one was open for 1% of the time, Pallas kernels for 9%

profile of v4, /device:TPU:0, one launch (start us, length us, event | category | flops | bytes accessed | tf_op | source)
XLA Modules:
  0.0 126.6 jit_solution(18197210108824824532)
XLA Ops:
  0.6 2.1 %pack.1 = (bf16[2,128,512]{2,1,0:T(8,128)(2,1)}, bf16[2,128,512]{2,1,0:T(8,128)(2,1)}, bf16[2,128,512]{2,1,0:T(8,128)(2,1)}, bf16[2,128,512]{2,1,0:T(8,128)(2,1)}) custom-call(s32[8,32]{1,0:T(8,128)} %bitcast.70, bf16[512,512]{1,0:T(8,128)(2,1)} %bitcast.51), custom_call_target="tpu_custom_call" | custom-call | tf_op jit(solution)/shard_map/pack/pallas_call | solution.py:463
  2.7 3.1 %collective-permute-start = (bf16[2,128,512]{2,1,0:T(8,128)(2,1)}, bf16[2,128,512]{2,1,0:T(8,128)(2,1)S(1)}, u32[]{:S(2)}, u32[]{:S(2)}) collective-permute-start(bf16[2,128,512]{2,1,0:T(8,128)(2,1)} %get-tuple-element.37), channel_id=1, source_target_pairs={{0,8},{4,12},{8,16},{12,20},{16,24},{20,28},{24,0},{28,4},{1,9},{5... | collective-permute-start | bytes 786440 | tf_op jit(solution)/shard_map/ppermute | solution.py:384
  5.8 1.5 %collective-permute-start.1 = (bf16[2,128,512]{2,1,0:T(8,128)(2,1)}, bf16[2,128,512]{2,1,0:T(8,128)(2,1)S(1)}, u32[]{:S(2)}, u32[]{:S(2)}) collective-permute-start(bf16[2,128,512]{2,1,0:T(8,128)(2,1)} %get-tuple-element.38), channel_id=1, source_target_pairs={{0,4},{4,8},{8,12},{12,16},{16,20},{20,24},{24,28},{28,0},{1,5},{5... | collective-permute-start | bytes 786440 | tf_op jit(solution)/shard_map/ppermute | solution.py:384
  7.3 3.2 %collective-permute-start.2 = (bf16[2,128,512]{2,1,0:T(8,128)(2,1)}, bf16[2,128,512]{2,1,0:T(8,128)(2,1)S(1)}, u32[]{:S(2)}, u32[]{:S(2)}) collective-permute-start(bf16[2,128,512]{2,1,0:T(8,128)(2,1)} %get-tuple-element.39), channel_id=1, source_target_pairs={{0,28},{4,0},{8,4},{12,8},{16,12},{20,16},{24,20},{28,24},{1,29},{... | collective-permute-start | bytes 786440 | tf_op jit(solution)/shard_map/ppermute | solution.py:384
  10.5 0.3 collective-permute-start.3
  10.8 4.5 %front.1 = (bf16[512,512]{1,0:T(8,128)(2,1)}, bf16[512,512]{1,0:T(8,128)(2,1)}, bf16[512,512]{1,0:T(8,128)(2,1)}, bf16[512,1536]{1,0:T(8,128)(2,1)}, bf16[512,512]{1,0:T(8,128)(2,1)}) custom-call(bf16[512,512]{1,0:T(8,128)(2,1)} %bitcast.52, bf16[512,512]{1,0:T(8,128)(2,1)} %bitcast.60, bf16[512,1536]{1,0:T(8,128)(2,1)} %weight_ref.3, ...), custom_call_target="tpu_custom_call" | custom-call | flops 1073741824 | bytes 6291456 | tf_op jit(solution)/shard_map/front/pallas_call | solution.py:475
  15.3 0.6 pad_add_fusion.place_ref
  16.0 6.1 %collective-permute-done.1.halo_b = bf16[2,128,512]{2,1,0:T(8,128)(2,1)S(1)} collective-permute-done((bf16[2,128,512]{2,1,0:T(8,128)(2,1)}, bf16[2,128,512]{2,1,0:T(8,128)(2,1)S(1)}, u32[]{:S(2)}, u32[]{:S(2)}) %collective-permute-start.1) | collective-permute-done | bytes 262176 | tf_op jit(solution)/shard_map/ppermute | solution.py:384
  22.0 0.0 collective-permute-done.2.halo_c
  22.0 3.5 %collective-permute-done.3.halo_d = bf16[2,128,512]{2,1,0:T(8,128)(2,1)S(1)} collective-permute-done((bf16[2,128,512]{2,1,0:T(8,128)(2,1)}, bf16[2,128,512]{2,1,0:T(8,128)(2,1)S(1)}, u32[]{:S(2)}, u32[]{:S(2)}) %collective-permute-start.3) | collective-permute-done | bytes 262176 | tf_op jit(solution)/shard_map/ppermute | solution.py:384
  25.6 0.7 copy-done.4
  26.3 20.9 %attend.1 = (bf16[2,128,512]{2,1,0:T(8,128)(2,1)}, bf16[2,128,512]{2,1,0:T(8,128)(2,1)}, bf16[2,128,512]{2,1,0:T(8,128)(2,1)}, bf16[2,128,512]{2,1,0:T(8,128)(2,...) custom-call(s32[8,32]{1,0:T(8,128)} %bitcast.71, ...), custom_call_target="tpu_custom_call" | custom-call | tf_op jit(solution)/shard_map/attend/pallas_call | solution.py:494
  47.2 0.1 collective-permute-start.4
  47.3 2.8 %collective-permute-done.4 = bf16[4096,128]{1,0:T(8,128)(2,1)S(1)} collective-permute-done((bf16[4096,128]{1,0:T(8,128)(2,1)}, bf16[4096,128]{1,0:T(8,128)(2,1)S(1)}, u32[]{:S(2)}, u32[]{:S(2)}) %collective-permute-start.4) | collective-permute-done | bytes 1048608 | tf_op jit(solution)/shard_map/ppermute | solution.py:388
  50.1 1.5 %add_convert_fusion = bf16[4096,128]{1,0:T(8,128)(2,1)S(1)} fusion(bf16[4096,128]{1,0:T(8,128)(2,1)S(1)} %collective-permute-done.4, bf16[4096,128]{1,0:T(8,128)(2,1)} %get-tuple-element.43), kind=kLoop, calls=%fused_computation | loop fusion | flops 2097152 | bytes 3145728 | tf_op jit(solution)/shard_map/convert_element_type | solution.py:532
  51.6 0.1 dynamic-slice_bitcast_fusion.2
  51.7 2.5 %collective-permute-start.7 = (bf16[1024,128]{1,0:T(8,128)(2,1)S(1)}, bf16[1024,128]{1,0:T(8,128)(2,1)S(1)}, u32[]{:S(2)}, u32[]{:S(2)}) collective-permute-start(bf16[1024,128]{1,0:T(8,128)(2,1)S(1)} %get-tuple-element.62), channel_id=1, source_target_pairs={{0,6},{1,7},{2,4},{3,5},{4,2},{5,3},{6,0},{7,1},{8,14},{9,15},{10,... | collective-permute-start | bytes 786440 | tf_op jit(solution)/shard_map/ppermute | solution.py:388
  54.2 0.5 collective-permute-start.6
  54.7 0.5 collective-permute-start.5
  55.3 6.6 %collective-permute-done.7 = bf16[1024,128]{1,0:T(8,128)(2,1)S(1)} collective-permute-done((bf16[1024,128]{1,0:T(8,128)(2,1)S(1)}, bf16[1024,128]{1,0:T(8,128)(2,1)S(1)}, u32[]{:S(2)}, u32[]{:S(2)}) %collective-permute-start.7) | collective-permute-done | bytes 262176 | tf_op jit(solution)/shard_map/ppermute | solution.py:388
  61.9 4.7 %collective-permute-done.6 = bf16[1024,128]{1,0:T(8,128)(2,1)S(1)} collective-permute-done((bf16[1024,128]{1,0:T(8,128)(2,1)S(1)}, bf16[1024,128]{1,0:T(8,128)(2,1)S(1)}, u32[]{:S(2)}, u32[]{:S(2)}) %collective-permute-start.6) | collective-permute-done | bytes 262176 | tf_op jit(solution)/shard_map/ppermute | solution.py:388
  66.6 0.1 collective-permute-done.5
  66.7 0.1 fusion.1
  66.9 2.9 %collective-permute-start.10 = (bf16[256,128]{1,0:T(8,128)(2,1)S(1)}, bf16[256,128]{1,0:T(8,128)(2,1)S(1)}, u32[]{:S(2)}, u32[]{:S(2)}) collective-permute-start(bf16[256,128]{1,0:T(8,128)(2,1)S(1)} %get-tuple-element.65), channel_id=1, source_target_pairs={{0,24},{1,25},{2,26},{3,27},{4,28},{5,29},{6,30},{7,31},{8,16},{9,... | collective-permute-start | bytes 196616 | tf_op jit(solution)/shard_map/ppermute | solution.py:388
  69.8 1.5 %collective-permute-start.8 = (bf16[256,128]{1,0:T(8,128)(2,1)S(1)}, bf16[256,128]{1,0:T(8,128)(2,1)S(1)}, u32[]{:S(2)}, u32[]{:S(2)}) collective-permute-start(bf16[256,128]{1,0:T(8,128)(2,1)S(1)} %get-tuple-element.64), channel_id=1, source_target_pairs={{0,8},{1,9},{2,10},{3,11},{4,12},{5,13},{6,14},{7,15},{8,0},{9,1},... | collective-permute-start | bytes 196616 | tf_op jit(solution)/shard_map/ppermute | solution.py:388
  71.4 2.8 %collective-permute-start.14 = (bf16[2,128,512]{2,1,0:T(8,128)(2,1)}, bf16[2,128,512]{2,1,0:T(8,128)(2,1)S(1)}, u32[]{:S(2)}, u32[]{:S(2)}) collective-permute-start(bf16[2,128,512]{2,1,0:T(8,128)(2,1)} %get-tuple-element.48), channel_id=1, source_target_pairs={{0,24},{4,28},{8,0},{12,4},{16,8},{20,12},{24,16},{28,20},{1,25},{... | collective-permute-start | bytes 786440 | tf_op jit(solution)/shard_map/ppermute | solution.py:384
  74.2 0.0 collective-permute-start.17
  74.2 0.0 collective-permute-done.10
  74.2 3.9 %collective-permute-start.15 = (bf16[2,128,512]{2,1,0:T(8,128)(2,1)S(1)}, bf16[2,128,512]{2,1,0:T(8,128)(2,1)S(1)}, u32[]{:S(2)}, u32[]{:S(2)}) collective-permute-start(bf16[2,128,512]{2,1,0:T(8,128)(2,1)S(1)} %copy-done.10), channel_id=1, source_target_pairs={{0,28},{4,0},{8,4},{12,8},{16,12},{20,16},{24,20},{28,24},{1,29},{... | collective-permute-start | bytes 786440 | tf_op jit(solution)/shard_map/ppermute | solution.py:384
  78.1 0.0 collective-permute-start.16
  78.2 0.1 copy.11
  78.3 0.1 collective-permute-start.11
  78.5 15.5 %collective-permute-done.11 = bf16[256,128]{1,0:T(8,128)(2,1)S(1)} collective-permute-done((bf16[256,128]{1,0:T(8,128)(2,1)S(1)}, bf16[256,128]{1,0:T(8,128)(2,1)S(1)}, u32[]{:S(2)}, u32[]{:S(2)}) %collective-permute-start.11) | collective-permute-done | bytes 65568 | tf_op jit(solution)/shard_map/ppermute | solution.py:388
  93.9 0.6 collective-permute-start.12
  94.6 5.2 %collective-permute-done.12 = bf16[256,128]{1,0:T(8,128)(2,1)S(1)} collective-permute-done((bf16[256,128]{1,0:T(8,128)(2,1)S(1)}, bf16[256,128]{1,0:T(8,128)(2,1)S(1)}, u32[]{:S(2)}, u32[]{:S(2)}) %collective-permute-start.12) | collective-permute-done | bytes 65568 | tf_op jit(solution)/shard_map/ppermute | solution.py:388
  99.8 2.2 %collective-permute-start.13 = (bf16[256,128]{1,0:T(8,128)(2,1)S(1)}, bf16[256,128]{1,0:T(8,128)(2,1)S(1)}, u32[]{:S(2)}, u32[]{:S(2)}) collective-permute-start(bf16[256,128]{1,0:T(8,128)(2,1)S(1)} %bitcast.68), channel_id=1, source_target_pairs={{0,24},{1,25},{2,26},{3,27},{4,28},{5,29},{6,30},{7,31},{8,16},{9,... | collective-permute-start | bytes 196616 | tf_op jit(solution)/shard_map/ppermute | solution.py:388
  102.0 3.9 %collective-permute-done.13 = bf16[256,128]{1,0:T(8,128)(2,1)S(1)} collective-permute-done((bf16[256,128]{1,0:T(8,128)(2,1)S(1)}, bf16[256,128]{1,0:T(8,128)(2,1)S(1)}, u32[]{:S(2)}, u32[]{:S(2)}) %collective-permute-start.13) | collective-permute-done | bytes 65568 | tf_op jit(solution)/shard_map/ppermute | solution.py:388
  105.9 0.0 copy-start.5
  106.0 0.8 collective-permute-start.18
  106.8 1.0 collective-permute-start.19
  107.8 1.7 %collective-permute-start.20 = (bf16[1024,128]{1,0:T(8,128)(2,1)S(1)}, bf16[1024,128]{1,0:T(8,128)(2,1)S(1)}, u32[]{:S(2)}, u32[]{:S(2)}) collective-permute-start(bf16[1024,128]{1,0:T(8,128)(2,1)S(1)} %bitcast.58), channel_id=1, source_target_pairs={{0,6},{1,7},{2,4},{3,5},{4,2},{5,3},{6,0},{7,1},{8,14},{9,15},{10,... | collective-permute-start | bytes 786440 | tf_op jit(solution)/shard_map/ppermute | solution.py:388
  109.5 0.1 broadcast_in_dim.48
  109.7 4.3 %collective-permute-done.18 = bf16[1024,128]{1,0:T(8,128)(2,1)S(1)} collective-permute-done((bf16[1024,128]{1,0:T(8,128)(2,1)S(1)}, bf16[1024,128]{1,0:T(8,128)(2,1)S(1)}, u32[]{:S(2)}, u32[]{:S(2)}) %collective-permute-start.18) | collective-permute-done | bytes 262176 | tf_op jit(solution)/shard_map/ppermute | solution.py:388
  114.1 3.5 %collective-permute-done.19 = bf16[1024,128]{1,0:T(8,128)(2,1)S(1)} collective-permute-done((bf16[1024,128]{1,0:T(8,128)(2,1)S(1)}, bf16[1024,128]{1,0:T(8,128)(2,1)S(1)}, u32[]{:S(2)}, u32[]{:S(2)}) %collective-permute-start.19) | collective-permute-done | bytes 262176 | tf_op jit(solution)/shard_map/ppermute | solution.py:388
  117.6 0.1 collective-permute-start.21
  117.8 4.8 %inputs.1 = bf16[512,512]{1,0:T(8,128)(2,1)} custom-call(s32[8,32]{1,0:T(8,128)} %bitcast.72, s32[2]{0:T(128)} %pad_add_fusion.place_ref, bf16[512,512]{1,0:T(8,128)(2,1)} %bitcast.53, bf16[512,512]{1,0:T(8,128)(2,1)} %bitcast.61, bf16[512,512]{1,0:T(8,128)(2,1)} %get-tuple-element.41.dquery_ref, bf16[1024,512]{1,0:T(8,128)(2,1)} %get-tuple-element.42.dpair_ref, ...), custom_call_target="tpu_custom_call" | custom-call | flops 805306368 | bytes 6291456 | tf_op jit(solution)/shard_map/inputs/pallas_call | solution.py:550
  122.5 1.9 %outputs.2 = (f32[512,1536]{1,0:T(8,128)}, f32[512,512]{1,0:T(8,128)}) custom-call(s32[2]{0:T(128)S(1)} %copy-done, bf16[4096,128]{1,0:T(8,128)(2,1)S(1)} %bitcast.48), custom_call_target="tpu_custom_call" | custom-call | bytes 4194304 | tf_op jit(solution)/shard_map/outputs/pallas_call | solution.py:569
  124.5 1.9 %outputs.3 = (f32[512,1536]{1,0:T(8,128)}, f32[512,512]{1,0:T(8,128)}) custom-call(s32[2]{0:T(128)S(1)} %copy-done, bf16[4096,128]{1,0:T(8,128)(2,1)S(1)} %collective-permute-done.21.gathered_ref, f32[512,1536]{1,0:T(8,128)} %get-tuple-element.57.refs_0_, f32[512,512]{1,0:T(8,128)} %get-tuple-element.58.refs_1_), custom_call_target="tpu_custom_call", output_to_operand_aliasing={{0}: (2, {}), {1}: (3, {})} | custom-call | bytes 4194304 | tf_op jit(solution)/shard_map/outputs/pallas_call | solution.py:569
  (45 shorter events, 0.4 us)
Async XLA Ops:
  2.7 13.2 %collective-permute-start = (bf16[2,128,512]{2,1,0:T(8,128)(2,1)}, bf16[2,128,512]{2,1,0:T(8,128)(2,1)S(1)}, u32[]{:S(2)}, u32[]{:S(2)}) collective-permute-start(bf16[2,128,512]{2,1,0:T(8,128)(2,1)} %get-tuple-element.37), channel_id=1, source_target_pairs={{0,8},{4,12},{8,16},{12,20},{16,24},{20,28},{24,0},{28,4},{1,9},{5... | collective-permute-start | bytes 786440 | tf_op jit(solution)/shard_map/ppermute | solution.py:384
  5.8 16.2 %collective-permute-start.1 = (bf16[2,128,512]{2,1,0:T(8,128)(2,1)}, bf16[2,128,512]{2,1,0:T(8,128)(2,1)S(1)}, u32[]{:S(2)}, u32[]{:S(2)}) collective-permute-start(bf16[2,128,512]{2,1,0:T(8,128)(2,1)} %get-tuple-element.38), channel_id=1, source_target_pairs={{0,4},{4,8},{8,12},{12,16},{16,20},{20,24},{24,28},{28,0},{1,5},{5... | collective-permute-start | bytes 786440 | tf_op jit(solution)/shard_map/ppermute | solution.py:384
  7.3 14.7 %collective-permute-start.2 = (bf16[2,128,512]{2,1,0:T(8,128)(2,1)}, bf16[2,128,512]{2,1,0:T(8,128)(2,1)S(1)}, u32[]{:S(2)}, u32[]{:S(2)}) collective-permute-start(bf16[2,128,512]{2,1,0:T(8,128)(2,1)} %get-tuple-element.39), channel_id=1, source_target_pairs={{0,28},{4,0},{8,4},{12,8},{16,12},{20,16},{24,20},{28,24},{1,29},{... | collective-permute-start | bytes 786440 | tf_op jit(solution)/shard_map/ppermute | solution.py:384
  10.5 15.0 %collective-permute-start.3 = (bf16[2,128,512]{2,1,0:T(8,128)(2,1)}, bf16[2,128,512]{2,1,0:T(8,128)(2,1)S(1)}, u32[]{:S(2)}, u32[]{:S(2)}) collective-permute-start(bf16[2,128,512]{2,1,0:T(8,128)(2,1)} %get-tuple-element.40), channel_id=1, source_target_pairs={{0,24},{4,28},{8,0},{12,4},{16,8},{20,12},{24,16},{28,20},{1,25},{... | collective-permute-start | bytes 786440 | tf_op jit(solution)/shard_map/ppermute | solution.py:384
  16.0 9.6 %copy-start.1 = (bf16[2,128,512]{2,1,0:T(8,128)(2,1)}, bf16[2,128,512]{2,1,0:T(8,128)(2,1)S(1)}, u32[]{:S(2)}) copy-start(bf16[2,128,512]{2,1,0:T(8,128)(2,1)S(1)} %collective-permute-done.halo_a) | copy-start | bytes 786436
  22.0 3.6 %copy-start.2 = (bf16[2,128,512]{2,1,0:T(8,128)(2,1)}, bf16[2,128,512]{2,1,0:T(8,128)(2,1)S(1)}, u32[]{:S(2)}) copy-start(bf16[2,128,512]{2,1,0:T(8,128)(2,1)S(1)} %collective-permute-done.1.halo_b) | copy-start | bytes 786436
  22.0 3.6 %copy-start.3 = (bf16[2,128,512]{2,1,0:T(8,128)(2,1)}, bf16[2,128,512]{2,1,0:T(8,128)(2,1)S(1)}, u32[]{:S(2)}) copy-start(bf16[2,128,512]{2,1,0:T(8,128)(2,1)S(1)} %collective-permute-done.2.halo_c) | copy-start | bytes 786436
  25.6 0.7 copy-start.4
  47.2 2.9 %collective-permute-start.4 = (bf16[4096,128]{1,0:T(8,128)(2,1)}, bf16[4096,128]{1,0:T(8,128)(2,1)S(1)}, u32[]{:S(2)}, u32[]{:S(2)}) collective-permute-start(bf16[4096,128]{1,0:T(8,128)(2,1)} %get-tuple-element.44), channel_id=1, source_target_pairs={{0,1},{1,0},{2,3},{3,2},{4,5},{5,4},{6,7},{7,6},{8,9},{9,8},{10,11... | collective-permute-start | bytes 3145736 | tf_op jit(solution)/shard_map/ppermute | solution.py:388
  51.6 22.6 %copy-start.11 = (bf16[2,128,512]{2,1,0:T(8,128)(2,1)S(1)}, bf16[2,128,512]{2,1,0:T(8,128)(2,1)}, u32[]{:S(2)}) copy-start(bf16[2,128,512]{2,1,0:T(8,128)(2,1)} %get-tuple-element.51) | copy-start | bytes 786436
  51.6 22.6 %copy-start.10 = (bf16[2,128,512]{2,1,0:T(8,128)(2,1)S(1)}, bf16[2,128,512]{2,1,0:T(8,128)(2,1)}, u32[]{:S(2)}) copy-start(bf16[2,128,512]{2,1,0:T(8,128)(2,1)} %get-tuple-element.49) | copy-start | bytes 786436
  51.6 26.5 %copy-start.9 = (bf16[2,128,512]{2,1,0:T(8,128)(2,1)S(1)}, bf16[2,128,512]{2,1,0:T(8,128)(2,1)}, u32[]{:S(2)}) copy-start(bf16[2,128,512]{2,1,0:T(8,128)(2,1)} %get-tuple-element.50) | copy-start | bytes 786436
  51.7 10.2 %collective-permute-start.7 = (bf16[1024,128]{1,0:T(8,128)(2,1)S(1)}, bf16[1024,128]{1,0:T(8,128)(2,1)S(1)}, u32[]{:S(2)}, u32[]{:S(2)}) collective-permute-start(bf16[1024,128]{1,0:T(8,128)(2,1)S(1)} %get-tuple-element.62), channel_id=1, source_target_pairs={{0,6},{1,7},{2,4},{3,5},{4,2},{5,3},{6,0},{7,1},{8,14},{9,15},{10,... | collective-permute-start | bytes 786440 | tf_op jit(solution)/shard_map/ppermute | solution.py:388
  54.2 12.4 %collective-permute-start.6 = (bf16[1024,128]{1,0:T(8,128)(2,1)S(1)}, bf16[1024,128]{1,0:T(8,128)(2,1)S(1)}, u32[]{:S(2)}, u32[]{:S(2)}) collective-permute-start(bf16[1024,128]{1,0:T(8,128)(2,1)S(1)} %get-tuple-element.63), channel_id=1, source_target_pairs={{0,4},{1,5},{2,6},{3,7},{4,0},{5,1},{6,2},{7,3},{8,12},{9,13},{10,... | collective-permute-start | bytes 786440 | tf_op jit(solution)/shard_map/ppermute | solution.py:388
  54.7 12.0 %collective-permute-start.5 = (bf16[1024,128]{1,0:T(8,128)(2,1)S(1)}, bf16[1024,128]{1,0:T(8,128)(2,1)S(1)}, u32[]{:S(2)}, u32[]{:S(2)}) collective-permute-start(bf16[1024,128]{1,0:T(8,128)(2,1)S(1)} %get-tuple-element.61), channel_id=1, source_target_pairs={{0,2},{1,3},{2,0},{3,1},{4,6},{5,7},{6,4},{7,5},{8,10},{9,11},{10,... | collective-permute-start | bytes 786440 | tf_op jit(solution)/shard_map/ppermute | solution.py:388
  66.9 7.3 %collective-permute-start.10 = (bf16[256,128]{1,0:T(8,128)(2,1)S(1)}, bf16[256,128]{1,0:T(8,128)(2,1)S(1)}, u32[]{:S(2)}, u32[]{:S(2)}) collective-permute-start(bf16[256,128]{1,0:T(8,128)(2,1)S(1)} %get-tuple-element.65), channel_id=1, source_target_pairs={{0,24},{1,25},{2,26},{3,27},{4,28},{5,29},{6,30},{7,31},{8,16},{9,... | collective-permute-start | bytes 196616 | tf_op jit(solution)/shard_map/ppermute | solution.py:388
  69.8 8.3 %collective-permute-start.9 = (bf16[256,128]{1,0:T(8,128)(2,1)S(1)}, bf16[256,128]{1,0:T(8,128)(2,1)S(1)}, u32[]{:S(2)}, u32[]{:S(2)}) collective-permute-start(bf16[256,128]{1,0:T(8,128)(2,1)S(1)} %get-tuple-element.66), channel_id=1, source_target_pairs={{0,16},{1,17},{2,18},{3,19},{4,20},{5,21},{6,22},{7,23},{8,24},{9,... | collective-permute-start | bytes 196616 | tf_op jit(solution)/shard_map/ppermute | solution.py:388
  69.8 8.3 %collective-permute-start.8 = (bf16[256,128]{1,0:T(8,128)(2,1)S(1)}, bf16[256,128]{1,0:T(8,128)(2,1)S(1)}, u32[]{:S(2)}, u32[]{:S(2)}) collective-permute-start(bf16[256,128]{1,0:T(8,128)(2,1)S(1)} %get-tuple-element.64), channel_id=1, source_target_pairs={{0,8},{1,9},{2,10},{3,11},{4,12},{5,13},{6,14},{7,15},{8,0},{9,1},... | collective-permute-start | bytes 196616 | tf_op jit(solution)/shard_map/ppermute | solution.py:388
  71.4 34.5 %collective-permute-start.14 = (bf16[2,128,512]{2,1,0:T(8,128)(2,1)}, bf16[2,128,512]{2,1,0:T(8,128)(2,1)S(1)}, u32[]{:S(2)}, u32[]{:S(2)}) collective-permute-start(bf16[2,128,512]{2,1,0:T(8,128)(2,1)} %get-tuple-element.48), channel_id=1, source_target_pairs={{0,24},{4,28},{8,0},{12,4},{16,8},{20,12},{24,16},{28,20},{1,25},{... | collective-permute-start | bytes 786440 | tf_op jit(solution)/shard_map/ppermute | solution.py:384
  74.2 31.7 %collective-permute-start.17 = (bf16[2,128,512]{2,1,0:T(8,128)(2,1)S(1)}, bf16[2,128,512]{2,1,0:T(8,128)(2,1)S(1)}, u32[]{:S(2)}, u32[]{:S(2)}) collective-permute-start(bf16[2,128,512]{2,1,0:T(8,128)(2,1)S(1)} %copy-done.11), channel_id=1, source_target_pairs={{0,8},{4,12},{8,16},{12,20},{16,24},{20,28},{24,0},{28,4},{1,9},{5... | collective-permute-start | bytes 786440 | tf_op jit(solution)/shard_map/ppermute | solution.py:384
  74.2 31.7 %collective-permute-start.15 = (bf16[2,128,512]{2,1,0:T(8,128)(2,1)S(1)}, bf16[2,128,512]{2,1,0:T(8,128)(2,1)S(1)}, u32[]{:S(2)}, u32[]{:S(2)}) collective-permute-start(bf16[2,128,512]{2,1,0:T(8,128)(2,1)S(1)} %copy-done.10), channel_id=1, source_target_pairs={{0,28},{4,0},{8,4},{12,8},{16,12},{20,16},{24,20},{28,24},{1,29},{... | collective-permute-start | bytes 786440 | tf_op jit(solution)/shard_map/ppermute | solution.py:384
  78.1 27.8 %collective-permute-start.16 = (bf16[2,128,512]{2,1,0:T(8,128)(2,1)S(1)}, bf16[2,128,512]{2,1,0:T(8,128)(2,1)S(1)}, u32[]{:S(2)}, u32[]{:S(2)}) collective-permute-start(bf16[2,128,512]{2,1,0:T(8,128)(2,1)S(1)} %copy-done.9), channel_id=1, source_target_pairs={{0,4},{4,8},{8,12},{12,16},{16,20},{20,24},{24,28},{28,0},{1,5},{5... | collective-permute-start | bytes 786440 | tf_op jit(solution)/shard_map/ppermute | solution.py:384
  78.3 15.6 %collective-permute-start.11 = (bf16[256,128]{1,0:T(8,128)(2,1)S(1)}, bf16[256,128]{1,0:T(8,128)(2,1)S(1)}, u32[]{:S(2)}, u32[]{:S(2)}) collective-permute-start(bf16[256,128]{1,0:T(8,128)(2,1)S(1)} %bitcast.65), channel_id=1, source_target_pairs={{0,8},{1,9},{2,10},{3,11},{4,12},{5,13},{6,14},{7,15},{8,0},{9,1},... | collective-permute-start | bytes 196616 | tf_op jit(solution)/shard_map/ppermute | solution.py:388
  93.9 5.9 %collective-permute-start.12 = (bf16[256,128]{1,0:T(8,128)(2,1)S(1)}, bf16[256,128]{1,0:T(8,128)(2,1)S(1)}, u32[]{:S(2)}, u32[]{:S(2)}) collective-permute-start(bf16[256,128]{1,0:T(8,128)(2,1)S(1)} %bitcast.67), channel_id=1, source_target_pairs={{0,16},{1,17},{2,18},{3,19},{4,20},{5,21},{6,22},{7,23},{8,24},{9,... | collective-permute-start | bytes 196616 | tf_op jit(solution)/shard_map/ppermute | solution.py:388
  99.8 6.1 %collective-permute-start.13 = (bf16[256,128]{1,0:T(8,128)(2,1)S(1)}, bf16[256,128]{1,0:T(8,128)(2,1)S(1)}, u32[]{:S(2)}, u32[]{:S(2)}) collective-permute-start(bf16[256,128]{1,0:T(8,128)(2,1)S(1)} %bitcast.68), channel_id=1, source_target_pairs={{0,24},{1,25},{2,26},{3,27},{4,28},{5,29},{6,30},{7,31},{8,16},{9,... | collective-permute-start | bytes 196616 | tf_op jit(solution)/shard_map/ppermute | solution.py:388
  105.9 11.8 %copy-start.5 = (bf16[2,128,512]{2,1,0:T(8,128)(2,1)}, bf16[2,128,512]{2,1,0:T(8,128)(2,1)S(1)}, u32[]{:S(2)}) copy-start(bf16[2,128,512]{2,1,0:T(8,128)(2,1)S(1)} %collective-permute-done.14.back_a) | copy-start | bytes 786436
  105.9 11.8 %copy-start.6 = (bf16[2,128,512]{2,1,0:T(8,128)(2,1)}, bf16[2,128,512]{2,1,0:T(8,128)(2,1)S(1)}, u32[]{:S(2)}) copy-start(bf16[2,128,512]{2,1,0:T(8,128)(2,1)S(1)} %collective-permute-done.17.back_d) | copy-start | bytes 786436
  105.9 11.8 %copy-start.7 = (bf16[2,128,512]{2,1,0:T(8,128)(2,1)}, bf16[2,128,512]{2,1,0:T(8,128)(2,1)S(1)}, u32[]{:S(2)}) copy-start(bf16[2,128,512]{2,1,0:T(8,128)(2,1)S(1)} %collective-permute-done.15.back_b) | copy-start | bytes 786436
  105.9 11.8 %copy-start.8 = (bf16[2,128,512]{2,1,0:T(8,128)(2,1)}, bf16[2,128,512]{2,1,0:T(8,128)(2,1)S(1)}, u32[]{:S(2)}) copy-start(bf16[2,128,512]{2,1,0:T(8,128)(2,1)S(1)} %collective-permute-done.16.back_c) | copy-start | bytes 786436
  106.0 8.1 %collective-permute-start.18 = (bf16[1024,128]{1,0:T(8,128)(2,1)S(1)}, bf16[1024,128]{1,0:T(8,128)(2,1)S(1)}, u32[]{:S(2)}, u32[]{:S(2)}) collective-permute-start(bf16[1024,128]{1,0:T(8,128)(2,1)S(1)} %bitcast.56), channel_id=1, source_target_pairs={{0,2},{1,3},{2,0},{3,1},{4,6},{5,7},{6,4},{7,5},{8,10},{9,11},{10,... | collective-permute-start | bytes 786440 | tf_op jit(solution)/shard_map/ppermute | solution.py:388
  106.8 10.8 %collective-permute-start.19 = (bf16[1024,128]{1,0:T(8,128)(2,1)S(1)}, bf16[1024,128]{1,0:T(8,128)(2,1)S(1)}, u32[]{:S(2)}, u32[]{:S(2)}) collective-permute-start(bf16[1024,128]{1,0:T(8,128)(2,1)S(1)} %bitcast.57), channel_id=1, source_target_pairs={{0,4},{1,5},{2,6},{3,7},{4,0},{5,1},{6,2},{7,3},{8,12},{9,13},{10,... | collective-permute-start | bytes 786440 | tf_op jit(solution)/shard_map/ppermute | solution.py:388
  107.8 9.8 %collective-permute-start.20 = (bf16[1024,128]{1,0:T(8,128)(2,1)S(1)}, bf16[1024,128]{1,0:T(8,128)(2,1)S(1)}, u32[]{:S(2)}, u32[]{:S(2)}) collective-permute-start(bf16[1024,128]{1,0:T(8,128)(2,1)S(1)} %bitcast.58), channel_id=1, source_target_pairs={{0,6},{1,7},{2,4},{3,5},{4,2},{5,3},{6,0},{7,1},{8,14},{9,15},{10,... | collective-permute-start | bytes 786440 | tf_op jit(solution)/shard_map/ppermute | solution.py:388
  117.6 6.8 %collective-permute-start.21 = (bf16[4096,128]{1,0:T(8,128)(2,1)S(1)}, bf16[4096,128]{1,0:T(8,128)(2,1)S(1)}, u32[]{:S(2)}, u32[]{:S(2)}) collective-permute-start(bf16[4096,128]{1,0:T(8,128)(2,1)S(1)} %bitcast.47), channel_id=1, source_target_pairs={{0,1},{1,0},{2,3},{3,2},{4,5},{5,4},{6,7},{7,6},{8,9},{9,8},{10,11... | collective-permute-start | bytes 3145736 | tf_op jit(solution)/shard_map/ppermute | solution.py:388
  117.7 4.8 %copy-start = (s32[2]{0:T(128)S(1)}, s32[2]{0:T(128)}, u32[]{:S(2)}) copy-start(s32[2]{0:T(128)} %pad_add_fusion.place_ref) | copy-start | bytes 28
